TPU v7x, 256 devices: a whole 4x4x8 slice. The times are simulated.
256 devices in a mesh: ctx: 16 (over y_hi, x, core), head: 16 (over y_lo, z).
Axes of the slice: x: 4, y: 4 (y_hi: 2, y_lo: 2; y = y_hi * 2 + y_lo), z: 8, core: 2. Of those that a mesh axis runs over, the one named last changes fastest.
Arguments:
- queries: bfloat16 [16384, 4096], P('ctx', 'head'), may hold values from -8 to 8
- keys: bfloat16 [16384, 1024], P('ctx'), may hold values from -8 to 8
- values: bfloat16 [16384, 1024], P('ctx'), may hold values from -8 to 8
- grad_out: bfloat16 [16384, 4096], P('ctx', 'head'), may hold values from -8 to 8
- block_index: int32 [16, 4], replicated, may hold values from 0 to 3
Outputs:
- grad_queries: bfloat16 [16384, 4096], P(('ctx', 'head'))
- grad_keys: bfloat16 [16384, 1024], P(('ctx', 'head'))
- grad_values: bfloat16 [16384, 1024], P(('ctx', 'head'))
Inputs may be any that keep to these rules, and one draw needn't show every extreme that they name: block_index[c, l] is read only where c >= 2**l.
All inputs are finite; a program needn't handle non-finite values.
Results may differ from a plain program's by a relative error of at most 0.023.
Values may be sent and summed in bfloat16 or wider, within the bound.
No kernel may reach another device: no remote copies, remote signals or barrier semaphores. Data moves between devices by JAX's collectives and lax.ppermute only.
A program may use at most 64 MiB of HBM per device.

v0:
```python
import jax
import jax.numpy as jnp
from jax import lax
from jax.sharding import PartitionSpec as P

HD = 128
BLK = 256


def from_behind(value, axis, steps):
    count = lax.axis_size(axis)
    leading, last = (max(0, -steps), min(count, count - steps))
    return lax.ppermute(value, axis, [(source, source + steps) for source in range(leading, last)])


def attend(queries, grad_out, key_all, value_all, ctx_index, levels, local_heads):
    softmax_scale = HD ** (-0.5)
    shard_rows = queries.shape[0]
    key_count = key_all.shape[0]
    block_rows = min(512, shard_rows)
    partner_live = jnp.concatenate(
        [jnp.broadcast_to(ctx_index >= 2**level_num, (BLK,)) for level_num in range(levels)]
    )
    key_position = jnp.arange(shard_rows)
    key_acc = jnp.zeros((key_count, HD), jnp.float32)
    value_acc = jnp.zeros((key_count, HD), jnp.float32)
    dq_columns = []
    for head_slot in range(local_heads):
        query_head = queries[:, head_slot * HD : (head_slot + 1) * HD]
        grad_head = grad_out[:, head_slot * HD : (head_slot + 1) * HD]
        pieces = []
        for row_start in range(0, shard_rows, block_rows):
            query_rows = query_head[row_start : row_start + block_rows]
            grad_rows = grad_head[row_start : row_start + block_rows]
            causal_part = key_position[None, :] <= (row_start + jnp.arange(block_rows))[:, None]
            visible = jnp.concatenate(
                [causal_part, jnp.broadcast_to(partner_live[None, :], (block_rows, levels * BLK))],
                axis=1,
            )
            scores = (
                jnp.einsum("qd,kd->qk", query_rows, key_all, preferred_element_type=jnp.float32)
                * softmax_scale
            )
            scores = jnp.where(visible, scores, -jnp.inf)
            row_max = jnp.max(scores, axis=-1, keepdims=True)
            weights = jnp.exp(scores - row_max)
            probs = weights / jnp.sum(weights, axis=-1, keepdims=True)
            probs_low = probs.astype(jnp.bfloat16)
            grad_probs = jnp.einsum(
                "qd,kd->qk", grad_rows, value_all, preferred_element_type=jnp.float32
            )
            delta = jnp.sum(probs * grad_probs, axis=-1, keepdims=True)
            scores_low = (probs * (grad_probs - delta)).astype(jnp.bfloat16)
            pieces.append(
                (
                    softmax_scale * jnp.dot(scores_low, key_all, preferred_element_type=jnp.float32)
                ).astype(jnp.bfloat16)
            )
            key_acc = key_acc + softmax_scale * jnp.einsum(
                "qk,qd->kd", scores_low, query_rows, preferred_element_type=jnp.float32
            )
            value_acc = value_acc + jnp.einsum(
                "qk,qd->kd", probs_low, grad_rows, preferred_element_type=jnp.float32
            )
        dq_columns.append(jnp.concatenate(pieces, axis=0))
    return (jnp.concatenate(dq_columns, axis=1), key_acc, value_acc)


def on_device(queries, keys, values, grad_out, block_index):
    shard_rows = queries.shape[0]
    local_heads = queries.shape[1] // HD
    ctx_count = lax.axis_size("ctx")
    head_count = lax.axis_size("head")
    levels = ctx_count.bit_length() - 1
    ctx_index = lax.axis_index("ctx")
    head_index = lax.axis_index("head")
    group_begin = head_index // 2 * HD
    key_own = lax.dynamic_slice_in_dim(keys, group_begin, HD, 1)
    value_own = lax.dynamic_slice_in_dim(values, group_begin, HD, 1)
    kv_whole = jnp.concatenate([key_own, value_own], axis=1)

    def block_start(level_num):
        target = jnp.minimum(ctx_index + 2**level_num, ctx_count - 1)
        return block_index[target, level_num] * BLK

    received = []
    for level_num in range(levels):
        sliced = lax.dynamic_slice_in_dim(kv_whole, block_start(level_num), BLK, 0)
        received.append(from_behind(sliced, "ctx", 2**level_num))
    blocks = jnp.concatenate(received, axis=0)
    joined = jnp.concatenate([kv_whole, blocks], axis=0)
    key_all = joined[:, :HD]
    value_all = joined[:, HD:]
    dq_local, key_acc, value_acc = attend(
        queries, grad_out, key_all, value_all, ctx_index, levels, local_heads
    )
    gradients = jnp.concatenate([key_acc, value_acc], axis=1)
    owned = gradients[:shard_rows]
    for level_num in range(levels):
        lower = shard_rows + level_num * BLK
        returned = from_behind(
            gradients[lower : lower + BLK].astype(jnp.bfloat16), "ctx", -(2**level_num)
        ).astype(jnp.float32)
        begin = block_start(level_num)
        current = lax.dynamic_slice_in_dim(owned, begin, returned.shape[0], 0)
        owned = lax.dynamic_update_slice_in_dim(owned, current + returned, begin, 0)
    regrouped = lax.all_to_all(
        owned.astype(jnp.bfloat16), "head", split_axis=0, concat_axis=1, tiled=True
    ).astype(owned.dtype)
    token_rows = regrouped.shape[0]
    paired = regrouped.reshape(token_rows, head_count // 2, 2, 2 * HD)
    paired = paired[:, :, 0] + paired[:, :, 1]
    grad_keys = paired[:, :, :HD].reshape(token_rows, head_count // 2 * HD).astype(jnp.bfloat16)
    grad_values = paired[:, :, HD:].reshape(token_rows, head_count // 2 * HD).astype(jnp.bfloat16)
    grad_queries = lax.all_to_all(dq_local, "head", split_axis=0, concat_axis=1, tiled=True)
    return (grad_queries, grad_keys, grad_values)


def solution(mesh):
    placed = (P("ctx", "head"), P("ctx", None), P("ctx", None), P("ctx", "head"), P())
    return jax.shard_map(
        on_device,
        mesh=mesh,
        in_specs=placed,
        out_specs=(P(("ctx", "head"), None), P(("ctx", "head"), None), P(("ctx", "head"), None)),
        check_vma=False,
    )
```

profile of v0, /device:TPU:6, one launch (start us, length us, event | category | flops | bytes accessed | tf_op | source)
XLA Modules:
  0.0 104.9 jit_solution(7154535488718692799)
XLA Ops:
  0.7 1.5 %constant_dynamic-slice_fusion.3 = (s32[1,1]{0,1:T(1,128)}, s32[1,1]{0,1:T(1,128)}, s32[1,1]{0,1:T(1,128)}, s32[1,1]{0,1:T(1,128)}) fusion(s32[16,4]{0,1:T(4,128)} %param.9, s32[]{:T(128)S(6)} %select_n.66, s32[]{:T(128)S(6)} %select_n.62, s32[]{:T(128)S(6)} %select_n.60, s32[]{:T(128)S(6)} %select_n.64), kind=kLoop, calls=%fused_computation.133 | loop fusion | bytes 48 | tf_op jit(solution)/shard_map/dynamic_slice | solution.py:84
  4.8 1.1 %constant_dynamic-slice_fusion.1 = (bf16[1024,128]{1,0:T(8,128)(2,1)S(1)}, bf16[1024,128]{1,0:T(8,128)(2,1)S(1)}) fusion(bf16[1024,1024]{1,0:T(8,128)(2,1)} %param.7, s32[]{:T(128)S(6)} %select_n.59, bf16[1024,1024]{1,0:T(8,128)(2,1)} %param.6), kind=kLoop, calls=%fused_computation.129 | loop fusion | bytes 1048580 | tf_op jit(solution)/shard_map/dynamic_slice | solution.py:79
  5.9 0.7 fusion.46
  6.6 5.1 %collective-permute-start.3 = (bf16[256,256]{1,0:T(8,128)(2,1)S(1)}, bf16[256,256]{1,0:T(8,128)(2,1)S(1)}, u32[]{:S(2)}, u32[]{:S(2)}) collective-permute-start(bf16[256,256]{1,0:T(8,128)(2,1)S(1)} %get-tuple-element.7), channel_id=1, source_target_pairs={{0,128},{16,144},{32,160},{48,176},{64,192},{80,208},{96,224},{112... | collective-permute-start | bytes 393224 | tf_op jit(solution)/shard_map/ppermute | solution.py:13
  11.8 1.9 %collective-permute-start = (bf16[256,256]{1,0:T(8,128)(2,1)}, bf16[256,256]{1,0:T(8,128)(2,1)S(1)}, u32[]{:S(2)}, u32[]{:S(2)}) collective-permute-start(bf16[256,256]{1,0:T(8,128)(2,1)} %get-tuple-element.8), channel_id=1, source_target_pairs={{0,16},{16,32},{32,48},{48,64},{64,80},{80,96},{96,112},{112,128},... | collective-permute-start | bytes 393224 | tf_op jit(solution)/shard_map/ppermute | solution.py:13
  13.7 1.9 %collective-permute-start.1 = (bf16[256,256]{1,0:T(8,128)(2,1)S(1)}, bf16[256,256]{1,0:T(8,128)(2,1)S(1)}, u32[]{:S(2)}, u32[]{:S(2)}) collective-permute-start(bf16[256,256]{1,0:T(8,128)(2,1)S(1)} %get-tuple-element.9), channel_id=1, source_target_pairs={{0,32},{16,48},{32,64},{48,80},{64,96},{80,112},{96,128},{112,144}... | collective-permute-start | bytes 393224 | tf_op jit(solution)/shard_map/ppermute | solution.py:13
  15.6 3.6 %collective-permute-start.2 = (bf16[256,256]{1,0:T(8,128)(2,1)S(1)}, bf16[256,256]{1,0:T(8,128)(2,1)S(1)}, u32[]{:S(2)}, u32[]{:S(2)}) collective-permute-start(bf16[256,256]{1,0:T(8,128)(2,1)S(1)} %get-tuple-element.10), channel_id=1, source_target_pairs={{0,64},{16,80},{32,96},{48,112},{64,128},{80,144},{96,160},{112,17... | collective-permute-start | bytes 393224 | tf_op jit(solution)/shard_map/ppermute | solution.py:13
  20.0 1.8 %collective-permute-done.1 = bf16[256,256]{1,0:T(8,128)(2,1)S(1)} collective-permute-done((bf16[256,256]{1,0:T(8,128)(2,1)S(1)}, bf16[256,256]{1,0:T(8,128)(2,1)S(1)}, u32[]{:S(2)}, u32[]{:S(2)}) %collective-permute-start.1) | collective-permute-done | bytes 131104 | tf_op jit(solution)/shard_map/ppermute | solution.py:13
  21.7 3.3 %collective-permute-done.2 = bf16[256,256]{1,0:T(8,128)(2,1)S(1)} collective-permute-done((bf16[256,256]{1,0:T(8,128)(2,1)S(1)}, bf16[256,256]{1,0:T(8,128)(2,1)S(1)}, u32[]{:S(2)}, u32[]{:S(2)}) %collective-permute-start.2) | collective-permute-done | bytes 131104 | tf_op jit(solution)/shard_map/ppermute | solution.py:13
  25.1 0.9 fusion.79
  25.9 0.8 fusion.77
  26.8 0.9 fusion.78
  27.6 0.9 fusion.80
  29.1 0.9 fusion.25
  30.1 1.0 fusion.9
  31.1 1.2 %fusion.11 = bf16[512,2048]{0,1:T(8,128)(2,1)S(1)} fusion(f32[2048,512]{1,0:T(8,128)S(1)} %get-tuple-element.32, f32[512]{0:T(512)S(1)} %get-tuple-element.31, f32[512]{0:T(512)S(1)} %fusion.13, f32[512,2048]{0,1:T(8,128)S(1)} %get-tuple-element.30, f32[512]{0:T(512)S(1)} %get-tuple-element.29), kind=kLoop, calls=%fused_computation.22 | loop fusion | flops 5242880 | bytes 10491904 | tf_op jit(solution)/shard_map/convert_element_type | solution.py:53
  32.3 0.8 fusion.27
  33.0 0.8 fusion.61
  34.5 1.0 fusion
  35.5 1.2 %fusion.2 = bf16[512,2048]{0,1:T(8,128)(2,1)S(1)} fusion(f32[2048,512]{1,0:T(8,128)S(1)} %get-tuple-element.20, f32[512]{0:T(512)S(1)} %get-tuple-element.19, f32[512]{0:T(512)S(1)} %fusion.19, f32[512,2048]{0,1:T(8,128)S(1)} %get-tuple-element.18, f32[512]{0:T(512)S(1)} %get-tuple-element.17), kind=kLoop, calls=%fused_computation.4 | loop fusion | flops 5242880 | bytes 10491904 | tf_op jit(solution)/shard_map/convert_element_type | solution.py:53
  36.6 1.0 fusion.30
  38.2 1.0 fusion.6
  39.2 1.2 %fusion.8 = bf16[512,2048]{0,1:T(8,128)(2,1)S(1)} fusion(f32[2048,512]{1,0:T(8,128)S(1)} %get-tuple-element.28, f32[512]{0:T(512)S(1)} %get-tuple-element.27, f32[512]{0:T(512)S(1)} %fusion.15, f32[512,2048]{0,1:T(8,128)S(1)} %get-tuple-element.26, f32[512]{0:T(512)S(1)} %get-tuple-element.25), kind=kLoop, calls=%fused_computation.16 | loop fusion | flops 5242880 | bytes 10491904 | tf_op jit(solution)/shard_map/convert_element_type | solution.py:53
  40.4 0.8 fusion.28
  41.2 0.9 convolution_add_fusion.2
  42.1 0.6 fusion.17
  42.8 1.0 fusion.3
  43.8 0.9 convolution_add_fusion.1
  44.7 0.9 convolution_add_fusion
  45.7 0.8 convolution_add_fusion.5
  46.5 1.2 %fusion.5 = bf16[512,2048]{0,1:T(8,128)(2,1)S(1)} fusion(f32[2048,512]{1,0:T(8,128)S(1)} %get-tuple-element.24, f32[512]{0:T(512)S(1)} %get-tuple-element.23, f32[512]{0:T(512)S(1)} %fusion.17, f32[512,2048]{0,1:T(8,128)S(1)} %get-tuple-element.22, f32[512]{0:T(512)S(1)} %get-tuple-element.21), kind=kLoop, calls=%fused_computation.10 | loop fusion | flops 5242880 | bytes 10491904 | tf_op jit(solution)/shard_map/convert_element_type | solution.py:53
  47.7 0.8 fusion.29
  48.5 0.8 convolution_add_fusion.4
  49.3 0.8 fusion.20
  50.1 0.9 maximum_maximum_fusion
  51.0 8.7 %all-to-all-start = ((bf16[16,64,256]{2,1,0:T(8,128)(2,1)}), bf16[16,64,256]{2,1,0:T(8,128)(2,1)S(1)}, u32[]{:S(2)}, u32[]{:S(2)}) async-start(bf16[16,64,256]{2,1,0:T(8,128)(2,1)} %bitcast.12), calls=%async_computation | async-start | bytes 1048576 | tf_op jit(solution)/shard_map/all_to_all | solution.py:115
  59.9 2.0 %collective-permute-start.4 = (bf16[256,256]{0,1:T(8,128)(2,1)S(1)}, bf16[256,256]{0,1:T(8,128)(2,1)S(1)}, u32[]{:S(2)}, u32[]{:S(2)}) collective-permute-start(bf16[256,256]{0,1:T(8,128)(2,1)S(1)} %get-tuple-element.6), channel_id=1, source_target_pairs={{16,0},{32,16},{48,32},{64,48},{80,64},{96,80},{112,96},{128,112},... | collective-permute-start | bytes 393224 | tf_op jit(solution)/shard_map/ppermute | solution.py:13
  62.0 1.3 %collective-permute-start.7 = (bf16[256,256]{0,1:T(8,128)(2,1)S(1)}, bf16[256,256]{0,1:T(8,128)(2,1)S(1)}, u32[]{:S(2)}, u32[]{:S(2)}) collective-permute-start(bf16[256,256]{0,1:T(8,128)(2,1)S(1)} %get-tuple-element.3), channel_id=1, source_target_pairs={{128,0},{144,16},{160,32},{176,48},{192,64},{208,80},{224,96},{240... | collective-permute-start | bytes 393224 | tf_op jit(solution)/shard_map/ppermute | solution.py:13
  63.3 2.1 %collective-permute-start.6 = (bf16[256,256]{0,1:T(8,128)(2,1)S(1)}, bf16[256,256]{0,1:T(8,128)(2,1)S(1)}, u32[]{:S(2)}, u32[]{:S(2)}) collective-permute-start(bf16[256,256]{0,1:T(8,128)(2,1)S(1)} %get-tuple-element.4), channel_id=1, source_target_pairs={{64,0},{80,16},{96,32},{112,48},{128,64},{144,80},{160,96},{176,11... | collective-permute-start | bytes 393224 | tf_op jit(solution)/shard_map/ppermute | solution.py:13
  65.4 3.2 %collective-permute-start.5 = (bf16[256,256]{0,1:T(8,128)(2,1)S(1)}, bf16[256,256]{0,1:T(8,128)(2,1)S(1)}, u32[]{:S(2)}, u32[]{:S(2)}) collective-permute-start(bf16[256,256]{0,1:T(8,128)(2,1)S(1)} %get-tuple-element.5), channel_id=1, source_target_pairs={{32,0},{48,16},{64,32},{80,48},{96,64},{112,80},{128,96},{144,112}... | collective-permute-start | bytes 393224 | tf_op jit(solution)/shard_map/ppermute | solution.py:13
  68.7 9.4 %collective-permute-done.5 = bf16[256,256]{0,1:T(8,128)(2,1)S(1)} collective-permute-done((bf16[256,256]{0,1:T(8,128)(2,1)S(1)}, bf16[256,256]{0,1:T(8,128)(2,1)S(1)}, u32[]{:S(2)}, u32[]{:S(2)}) %collective-permute-start.5) | collective-permute-done | bytes 131104 | tf_op jit(solution)/shard_map/ppermute | solution.py:13
  78.2 1.7 %collective-permute-done.7 = bf16[256,256]{0,1:T(8,128)(2,1)S(1)} collective-permute-done((bf16[256,256]{0,1:T(8,128)(2,1)S(1)}, bf16[256,256]{0,1:T(8,128)(2,1)S(1)}, u32[]{:S(2)}, u32[]{:S(2)}) %collective-permute-start.7) | collective-permute-done | bytes 131104 | tf_op jit(solution)/shard_map/ppermute | solution.py:13
  80.0 1.0 copy.12
  81.0 6.6 %all-to-all-start.1 = ((bf16[16,64,256]{2,1,0:T(8,128)(2,1)}), bf16[16,64,256]{2,1,0:T(8,128)(2,1)S(1)}, u32[]{:S(2)}, u32[]{:S(2)}) async-start(bf16[16,64,256]{2,1,0:T(8,128)(2,1)} %bitcast.14), calls=%async_computation.1 | async-start | bytes 1048576 | tf_op jit(solution)/shard_map/all_to_all | solution.py:107
  87.7 0.8 copy.15
  88.5 14.9 %all-to-all-done.1 = bf16[16,64,256]{2,1,0:T(8,128)(2,1)S(1)} async-done(((bf16[16,64,256]{2,1,0:T(8,128)(2,1)}), bf16[16,64,256]{2,1,0:T(8,128)(2,1)S(1)}, u32[]{:S(2)}, u32[]{:S(2)}) %all-to-all-start.1) | async-done | bytes 524320 | tf_op jit(solution)/shard_map/all_to_all | solution.py:107
  103.6 0.7 copy.20
  104.3 0.7 copy.21
  (41 shorter events, 3.4 us)
Async XLA Ops:
  0.6 24.4 %copy-start = (bf16[1024,256]{1,0:T(8,128)(2,1)S(1)}, bf16[1024,256]{1,0:T(8,128)(2,1)}, u32[]{:S(2)}) copy-start(bf16[1024,256]{1,0:T(8,128)(2,1)} %param.5) | copy-start | bytes 1572868
  6.6 18.4 %collective-permute-start.3 = (bf16[256,256]{1,0:T(8,128)(2,1)S(1)}, bf16[256,256]{1,0:T(8,128)(2,1)S(1)}, u32[]{:S(2)}, u32[]{:S(2)}) collective-permute-start(bf16[256,256]{1,0:T(8,128)(2,1)S(1)} %get-tuple-element.7), channel_id=1, source_target_pairs={{0,128},{16,144},{32,160},{48,176},{64,192},{80,208},{96,224},{112... | collective-permute-start | bytes 393224 | tf_op jit(solution)/shard_map/ppermute | solution.py:13
  11.8 8.2 %collective-permute-start = (bf16[256,256]{1,0:T(8,128)(2,1)}, bf16[256,256]{1,0:T(8,128)(2,1)S(1)}, u32[]{:S(2)}, u32[]{:S(2)}) collective-permute-start(bf16[256,256]{1,0:T(8,128)(2,1)} %get-tuple-element.8), channel_id=1, source_target_pairs={{0,16},{16,32},{32,48},{48,64},{64,80},{80,96},{96,112},{112,128},... | collective-permute-start | bytes 393224 | tf_op jit(solution)/shard_map/ppermute | solution.py:13
  13.7 8.0 %collective-permute-start.1 = (bf16[256,256]{1,0:T(8,128)(2,1)S(1)}, bf16[256,256]{1,0:T(8,128)(2,1)S(1)}, u32[]{:S(2)}, u32[]{:S(2)}) collective-permute-start(bf16[256,256]{1,0:T(8,128)(2,1)S(1)} %get-tuple-element.9), channel_id=1, source_target_pairs={{0,32},{16,48},{32,64},{48,80},{64,96},{80,112},{96,128},{112,144}... | collective-permute-start | bytes 393224 | tf_op jit(solution)/shard_map/ppermute | solution.py:13
  15.6 9.4 %collective-permute-start.2 = (bf16[256,256]{1,0:T(8,128)(2,1)S(1)}, bf16[256,256]{1,0:T(8,128)(2,1)S(1)}, u32[]{:S(2)}, u32[]{:S(2)}) collective-permute-start(bf16[256,256]{1,0:T(8,128)(2,1)S(1)} %get-tuple-element.10), channel_id=1, source_target_pairs={{0,64},{16,80},{32,96},{48,112},{64,128},{80,144},{96,160},{112,17... | collective-permute-start | bytes 393224 | tf_op jit(solution)/shard_map/ppermute | solution.py:13
  25.1 17.7 %copy-start.1 = (bf16[2048,256]{1,0:T(8,128)(2,1)}, bf16[2048,256]{1,0:T(8,128)(2,1)S(1)}, u32[]{:S(2)}) copy-start(bf16[2048,256]{1,0:T(8,128)(2,1)S(1)} %constant_dynamic-update-slice_fusion) | copy-start | bytes 3145732
  27.6 1.5 %copy-start.3 = (bf16[1024,256]{1,0:T(8,128)(2,1)S(1)}, bf16[1024,256]{1,0:T(8,128)(2,1)}, u32[]{:S(2)}) copy-start(bf16[1024,256]{1,0:T(8,128)(2,1)} %param.8) | copy-start | bytes 1572868
  46.5 1.2 %copy-start.2 = (bf16[2048,256]{1,0:T(8,128)(2,1)S(1)}, bf16[2048,256]{1,0:T(8,128)(2,1)}, u32[]{:S(2)}) copy-start(bf16[2048,256]{1,0:T(8,128)(2,1)} %copy-done.1) | copy-start | bytes 3145732
  51.0 30.0 %all-to-all-start = ((bf16[16,64,256]{2,1,0:T(8,128)(2,1)}), bf16[16,64,256]{2,1,0:T(8,128)(2,1)S(1)}, u32[]{:S(2)}, u32[]{:S(2)}) async-start(bf16[16,64,256]{2,1,0:T(8,128)(2,1)} %bitcast.12), calls=%async_computation | async-start | bytes 1048576 | tf_op jit(solution)/shard_map/all_to_all | solution.py:115
  59.9 8.7 %collective-permute-start.4 = (bf16[256,256]{0,1:T(8,128)(2,1)S(1)}, bf16[256,256]{0,1:T(8,128)(2,1)S(1)}, u32[]{:S(2)}, u32[]{:S(2)}) collective-permute-start(bf16[256,256]{0,1:T(8,128)(2,1)S(1)} %get-tuple-element.6), channel_id=1, source_target_pairs={{16,0},{32,16},{48,32},{64,48},{80,64},{96,80},{112,96},{128,112},... | collective-permute-start | bytes 393224 | tf_op jit(solution)/shard_map/ppermute | solution.py:13
  62.0 17.9 %collective-permute-start.7 = (bf16[256,256]{0,1:T(8,128)(2,1)S(1)}, bf16[256,256]{0,1:T(8,128)(2,1)S(1)}, u32[]{:S(2)}, u32[]{:S(2)}) collective-permute-start(bf16[256,256]{0,1:T(8,128)(2,1)S(1)} %get-tuple-element.3), channel_id=1, source_target_pairs={{128,0},{144,16},{160,32},{176,48},{192,64},{208,80},{224,96},{240... | collective-permute-start | bytes 393224 | tf_op jit(solution)/shard_map/ppermute | solution.py:13
  63.3 14.8 %collective-permute-start.6 = (bf16[256,256]{0,1:T(8,128)(2,1)S(1)}, bf16[256,256]{0,1:T(8,128)(2,1)S(1)}, u32[]{:S(2)}, u32[]{:S(2)}) collective-permute-start(bf16[256,256]{0,1:T(8,128)(2,1)S(1)} %get-tuple-element.4), channel_id=1, source_target_pairs={{64,0},{80,16},{96,32},{112,48},{128,64},{144,80},{160,96},{176,11... | collective-permute-start | bytes 393224 | tf_op jit(solution)/shard_map/ppermute | solution.py:13
  65.4 12.7 %collective-permute-start.5 = (bf16[256,256]{0,1:T(8,128)(2,1)S(1)}, bf16[256,256]{0,1:T(8,128)(2,1)S(1)}, u32[]{:S(2)}, u32[]{:S(2)}) collective-permute-start(bf16[256,256]{0,1:T(8,128)(2,1)S(1)} %get-tuple-element.5), channel_id=1, source_target_pairs={{32,0},{48,16},{64,32},{80,48},{96,64},{112,80},{128,96},{144,112}... | collective-permute-start | bytes 393224 | tf_op jit(solution)/shard_map/ppermute | solution.py:13
  81.0 22.3 %all-to-all-start.1 = ((bf16[16,64,256]{2,1,0:T(8,128)(2,1)}), bf16[16,64,256]{2,1,0:T(8,128)(2,1)S(1)}, u32[]{:S(2)}, u32[]{:S(2)}) async-start(bf16[16,64,256]{2,1,0:T(8,128)(2,1)} %bitcast.14), calls=%async_computation.1 | async-start | bytes 1048576 | tf_op jit(solution)/shard_map/all_to_all | solution.py:107
where the time goes:
time: 106 us; the launch traced here: 105 us
  starting transfers between devices  36.4 us (34%)
  waiting for transfers between devices  31 us (29%)
  matrix products  17.6 us (17%)
  other arithmetic  10.2 us (10%)
  local copies, waits for them, and re-layouts  5.96 us (6%)
  between operations  3.78 us (4%)
    ppermute x8, starting transfers between devices, from_behind(): lax.ppermute(value, axis, [(source, source + steps) for source in range(l...  21.1 us
    ppermute x8, waiting for transfers between devices, from_behind(): lax.ppermute(value, axis, [(source, source + steps) for source in range(l...  16.1 us
    all_to_all x1, waiting for transfers between devices, on_device(): lax.all_to_all(owned.astype(jnp.bfloat16), 'head', split_axis=0, concat_a...  14.9 us
    all_to_all x1, starting transfers between devices, on_device(): lax.all_to_all(dq_local, 'head', split_axis=0, concat_axis=1, tiled=True)  8.68 us
    all_to_all x1, starting transfers between devices, on_device(): lax.all_to_all(owned.astype(jnp.bfloat16), 'head', split_axis=0, concat_a...  6.62 us
    convert_element_type x4, other arithmetic, attend(): scores_low = (probs * (grad_probs - delta)).astype(jnp.bfloat16)  4.78 us
    dot_general x4, matrix products, attend(): jnp.einsum('qd,kd->qk', grad_rows, value_all, preferred_element_type=jnp....  3.93 us
    dot_general x4, matrix products, attend(): jnp.einsum('qk,qd->kd', probs_low, grad_rows, preferred_element_type=jnp....  3.76 us
  transfers between devices with their start and end apart: 10, of which 5 were waited for; matrix products, arithmetic and copies ran while one was open for 3% of the time, Pallas kernels for 0%

commit v1 on v0

v1 whole, which is shorter than its diff:
```python
import jax
import jax.numpy as jnp
from jax import lax
from jax.experimental import pallas as pl
from jax.experimental.pallas import tpu as pltpu
from jax.sharding import PartitionSpec as P

HD = 128
BLK = 256
NEG = -1e30
SCALE = HD**-0.5
LOG2E = 1.4426950408889634
HBM = pl.BlockSpec(memory_space=pltpu.HBM)
VMEM = pl.BlockSpec(memory_space=pltpu.VMEM)
SMEM = pl.BlockSpec(memory_space=pltpu.SMEM)


def rotate(value, axis, steps):
    count = lax.axis_size(axis)
    return lax.ppermute(value, axis, [(source, (source + steps) % count) for source in range(count)])


def block_start(index_ref, ctx_index, level_num, ctx_count):
    target = jnp.minimum(ctx_index + 2**level_num, ctx_count - 1)
    return pl.multiple_of(index_ref[level_num, target] * BLK, BLK)


def gather_blocks(block_index, keys, values, ctx_count, levels):
    def body(index_ref, key_ref, value_ref, own_ref, *refs):
        sends, sems = refs[:levels], refs[levels]
        ctx_index = lax.axis_index("ctx")
        begin = pl.multiple_of(lax.axis_index("head") // 2 * HD, HD)
        copies = []
        for half, source in ((0, key_ref), (1, value_ref)):
            columns = slice(half * HD, (half + 1) * HD)
            for level_num in range(levels):
                start = block_start(index_ref, ctx_index, level_num, ctx_count)
                copies.append((source.at[pl.ds(start, BLK), pl.ds(begin, HD)], sends[level_num].at[:, columns]))
            copies.append((source.at[:, pl.ds(begin, HD)], own_ref.at[:, columns]))
        started = [
            pltpu.make_async_copy(source, target, sems.at[number])
            for number, (source, target) in enumerate(copies)
        ]
        for copy in started:
            copy.start()
        for copy in started:
            copy.wait()

    rows = keys.shape[0]
    return pl.pallas_call(
        body,
        out_shape=(jax.ShapeDtypeStruct((rows, 2 * HD), keys.dtype),)
        + (jax.ShapeDtypeStruct((BLK, 2 * HD), keys.dtype),) * levels,
        in_specs=[SMEM, HBM, HBM],
        out_specs=(VMEM,) * (levels + 1),
        scratch_shapes=[pltpu.SemaphoreType.DMA((2 * levels + 2,))],
        compiler_params=pltpu.CompilerParams(vmem_limit_bytes=4 << 20),
        name="gather_blocks",
    )(block_index, keys, values)


def dot(left, right):
    return jnp.dot(left, right, preferred_element_type=jnp.float32)


def attend(queries, grad_out, own, blocks):
    rows, width = queries.shape
    levels = len(blocks)
    row_tiles = rows // BLK
    factor = SCALE * LOG2E

    def body(q_ref, g_ref, own_ref, *refs):
        block_refs = refs[:levels]
        dq_ref, grad_ref = refs[levels : levels + 2]
        part_refs = refs[levels + 2 : 2 * levels + 2]
        kt_ref, acc_ref = refs[2 * levels + 2 :]
        ctx_index = lax.axis_index("ctx")

        def tile(number, half):
            columns = slice(half * HD, (half + 1) * HD)
            if number < row_tiles:
                return own_ref[number * BLK : (number + 1) * BLK, columns]
            return block_refs[number - row_tiles][:, columns]

        def spot(number):
            return slice(number * BLK, (number + 1) * BLK)

        for number in range(row_tiles + levels):
            kt_ref[:, spot(number)] = tile(number, 0).T
        key_at = lax.broadcasted_iota(jnp.int32, (BLK, BLK), 0)
        causal = key_at <= lax.broadcasted_iota(jnp.int32, (BLK, BLK), 1)
        live = [ctx_index >= 2**level_num for level_num in range(levels)]
        written = set()
        for head in range(width // HD):
            columns = slice(head * HD, (head + 1) * HD)
            for part in range(row_tiles):
                query = q_ref[spot(part), columns]
                grad = g_ref[spot(part), columns]
                query_t, grad_t = query.T, grad.T
                numbers = list(range(part + 1)) + [row_tiles + level_num for level_num in range(levels)]
                weights, grad_probs, tops, sums, products = {}, {}, {}, {}, {}
                for number in numbers:
                    scores = dot(tile(number, 0), query_t)
                    if number == part:
                        scores = jnp.where(causal, scores, NEG)
                    top = jnp.max(scores, axis=0, keepdims=True) * factor
                    shift = top
                    if number >= row_tiles:
                        shift = jnp.where(live[number - row_tiles], top, -NEG)
                        top = jnp.where(live[number - row_tiles], top, NEG)
                    weights[number] = jnp.exp2(scores * factor - shift)
                    grad_probs[number] = dot(tile(number, 1), grad_t)
                    tops[number] = top
                    sums[number] = jnp.sum(weights[number], axis=0, keepdims=True)
                    products[number] = jnp.sum(weights[number] * grad_probs[number], axis=0, keepdims=True)
                row_max = tops[numbers[0]]
                for number in numbers[1:]:
                    row_max = jnp.maximum(row_max, tops[number])
                ratios = {number: jnp.exp2(tops[number] - row_max) for number in numbers}
                inverse = 1.0 / sum(sums[number] * ratios[number] for number in numbers)
                delta = sum(products[number] * ratios[number] for number in numbers) * inverse
                dq_t = None
                for number in numbers:
                    probs = weights[number] * (ratios[number] * inverse)
                    scores_low = (probs * (grad_probs[number] - delta)).astype(jnp.bfloat16)
                    key_part = dot(scores_low, query)
                    value_part = dot(probs.astype(jnp.bfloat16), grad)
                    if number in written:
                        acc_ref[spot(number), :HD] += key_part
                        acc_ref[spot(number), HD:] += value_part
                    else:
                        written.add(number)
                        acc_ref[spot(number), :HD] = key_part
                        acc_ref[spot(number), HD:] = value_part
                    term = dot(kt_ref[:, spot(number)], scores_low)
                    dq_t = term if dq_t is None else dq_t + term
                dq_ref[spot(part), columns] = (dq_t * SCALE).T.astype(jnp.bfloat16)
        grad_ref[:, :HD] = acc_ref[:rows, :HD] * SCALE
        grad_ref[:, HD:] = acc_ref[:rows, HD:]
        for level_num in range(levels):
            at = spot(row_tiles + level_num)
            part_refs[level_num][:, :HD] = (acc_ref[at, :HD] * SCALE).astype(jnp.bfloat16)
            part_refs[level_num][:, HD:] = acc_ref[at, HD:].astype(jnp.bfloat16)

    keys = rows + levels * BLK
    return pl.pallas_call(
        body,
        out_shape=(
            jax.ShapeDtypeStruct(queries.shape, jnp.bfloat16),
            jax.ShapeDtypeStruct((rows, 2 * HD), jnp.float32),
        )
        + (jax.ShapeDtypeStruct((BLK, 2 * HD), jnp.bfloat16),) * levels,
        in_specs=[VMEM] * (3 + levels),
        out_specs=(VMEM,) * (2 + levels),
        scratch_shapes=[pltpu.VMEM((HD, keys), jnp.bfloat16), pltpu.VMEM((keys, 2 * HD), jnp.float32)],
        compiler_params=pltpu.CompilerParams(vmem_limit_bytes=48 << 20),
        cost_estimate=pl.CostEstimate(
            flops=10 * width * rows * keys, bytes_accessed=4 << 20, transcendentals=0
        ),
        name="attend",
    )(queries, grad_out, own, *blocks)


def add_returned(block_index, gradients, returned, ctx_count):
    levels = len(returned)

    def body(index_ref, grad_ref, *refs):
        out_ref, total_ref = refs[levels:]
        ctx_index = lax.axis_index("ctx")
        total_ref[...] = grad_ref[...]
        for level_num in range(levels):
            start = block_start(index_ref, ctx_index, level_num, ctx_count)
            total_ref[pl.ds(start, BLK), :] += refs[level_num][...].astype(jnp.float32)
        out_ref[...] = total_ref[...].astype(jnp.bfloat16)

    return pl.pallas_call(
        body,
        out_shape=jax.ShapeDtypeStruct(gradients.shape, jnp.bfloat16),
        in_specs=[SMEM] + [VMEM] * (levels + 1),
        out_specs=VMEM,
        scratch_shapes=[pltpu.VMEM(gradients.shape, jnp.float32)],
        compiler_params=pltpu.CompilerParams(vmem_limit_bytes=6 << 20),
        name="add_returned",
    )(block_index, gradients, *returned)


def lay_queries(gathered):
    count, token_rows, width = gathered.shape

    def body(in_ref, out_ref):
        for number in range(count):
            out_ref[:, number * width : (number + 1) * width] = in_ref[number]

    return pl.pallas_call(
        body,
        out_shape=jax.ShapeDtypeStruct((token_rows, count * width), gathered.dtype),
        in_specs=[VMEM],
        out_specs=VMEM,
        compiler_params=pltpu.CompilerParams(vmem_limit_bytes=4 << 20),
        name="lay_queries",
    )(gathered)


def lay_keys(gathered):
    count, token_rows, width = gathered.shape

    def body(in_ref, key_ref, value_ref):
        for number in range(count // 2):
            total = in_ref[2 * number].astype(jnp.float32) + in_ref[2 * number + 1].astype(jnp.float32)
            total = total.astype(jnp.bfloat16)
            key_ref[:, number * HD : (number + 1) * HD] = total[:, :HD]
            value_ref[:, number * HD : (number + 1) * HD] = total[:, HD:]

    shape = jax.ShapeDtypeStruct((token_rows, count // 2 * HD), gathered.dtype)
    return pl.pallas_call(
        body,
        out_shape=(shape, shape),
        in_specs=[VMEM],
        out_specs=(VMEM, VMEM),
        compiler_params=pltpu.CompilerParams(vmem_limit_bytes=4 << 20),
        name="lay_keys",
    )(gathered)


def spread(value, head_count):
    split = value.reshape(head_count, value.shape[0] // head_count, value.shape[1])
    return lax.all_to_all(split, "head", split_axis=0, concat_axis=0, tiled=True)


def on_device(queries, keys, values, grad_out, block_index):
    ctx_count = lax.axis_size("ctx")
    head_count = lax.axis_size("head")
    levels = ctx_count.bit_length() - 1
    block_index = block_index.T
    own, *sends = gather_blocks(block_index, keys, values, ctx_count, levels)
    blocks = [rotate(sends[level_num], "ctx", 2**level_num) for level_num in range(levels)]
    dq_local, gradients, *parts = attend(queries, grad_out, own, blocks)
    dq_gathered = spread(dq_local, head_count)
    returned = [rotate(parts[level_num], "ctx", -(2**level_num)) for level_num in range(levels)]
    summed = add_returned(block_index, gradients, returned, ctx_count)
    grad_queries = lay_queries(dq_gathered)
    grad_keys, grad_values = lay_keys(spread(summed, head_count))
    return (grad_queries, grad_keys, grad_values)


def solution(mesh):
    placed = (P("ctx", "head"), P("ctx", None), P("ctx", None), P("ctx", "head"), P())
    return jax.shard_map(
        on_device,
        mesh=mesh,
        in_specs=placed,
        out_specs=(P(("ctx", "head"), None), P(("ctx", "head"), None), P(("ctx", "head"), None)),
        check_vma=False,
    )
```

time: 106 us -> 87.5 us (0.83)
  Pallas kernels: 0 us -> 17.7 us
  matrix products: 17.6 us -> 0 us
  other arithmetic: 10.2 us -> 0 us
  starting transfers between devices: 36.4 us -> 30.8 us
  waiting for transfers between devices: 31 us -> 34.1 us
  between operations: 3.78 us -> 0.69 us
  local copies, waits for them, and re-layouts: 5.96 us -> 3.87 us
    pallas_call x0 -> x5, Pallas kernels: none -> 17.7 us  [the longest x1 13.5 us: attend(): pl.pallas_call(body, out_shape=(jax.ShapeDtypeStruct(queries.shape, jnp.b...]
    dot_general x20 -> x0, matrix products: 17.6 us -> none  [the longest x4 3.93 us: attend(): jnp.einsum('qd,kd->qk', grad_rows, value_all, preferred_element_type=jnp....]
    ppermute x8, starting transfers between devices: 21.1 us -> 15.2 us  [rotate(): lax.ppermute(value, axis, [(source, (source + steps) % count) for source...]
    convert_element_type x6 -> x0, other arithmetic: 4.96 us -> none  [the longest x4 4.78 us: attend(): scores_low = (probs * (grad_probs - delta)).astype(jnp.bfloat16)]
    unnamed x12, local copies, waits for them, and re-layouts: 0.12 us -> 3.87 us
    ppermute x8, waiting for transfers between devices: 16.1 us -> 19.3 us  [rotate(): lax.ppermute(value, axis, [(source, (source + steps) % count) for source...]
    dynamic_slice x2 -> x0, local copies, waits for them, and re-layouts: 2.59 us -> none  [the longest x1 1.51 us: block_start(): return block_index[target, level_num] * BLK]
    reduce_sum x4 -> x0, other arithmetic: 2.53 us -> none  [attend(): probs = weights / jnp.sum(weights, axis=-1, keepdims=True)]
  transfers between devices with their start and end apart: 10 -> 10, of which waited for: 5 -> 6; matrix products, arithmetic and copies ran while one was open for 3% -> 0% of each run, Pallas kernels for 0% -> 3%
where the time goes in v1:
time: 87.5 us; the launch traced here: 87.1 us
  waiting for transfers between devices  34.1 us (39%)
  starting transfers between devices  30.8 us (35%)
  Pallas kernels  17.7 us (20%)
  local copies, waits for them, and re-layouts  3.87 us (4%)
    ppermute x8, waiting for transfers between devices, rotate(): lax.ppermute(value, axis, [(source, (source + steps) % count) for source...  19.3 us
    all_to_all x2, starting transfers between devices, spread(): lax.all_to_all(split, 'head', split_axis=0, concat_axis=0, tiled=True)  15.6 us
    ppermute x8, starting transfers between devices, rotate(): lax.ppermute(value, axis, [(source, (source + steps) % count) for source...  15.2 us
    all_to_all x2, waiting for transfers between devices, spread(): lax.all_to_all(split, 'head', split_axis=0, concat_axis=0, tiled=True)  14.8 us
    pallas_call x1, Pallas kernels, attend(): pl.pallas_call(body, out_shape=(jax.ShapeDtypeStruct(queries.shape, jnp.b...  13.5 us
    unnamed x12, local copies, waits for them, and re-layouts  3.87 us
  transfers between devices with their start and end apart: 10, of which 6 were waited for; matrix products, arithmetic and copies ran while one was open for 0% of the time, Pallas kernels for 3%

profile of v1, /device:TPU:6, one launch (start us, length us, event | category | flops | bytes accessed | tf_op | source)
XLA Modules:
  0.0 87.1 jit_solution(18117061887071832287)
XLA Ops:
  0.6 0.0 copy-start
  0.6 1.6 %copy-done = bf16[1024,1024]{1,0:T(8,128)(2,1)S(1)} copy-done((bf16[1024,1024]{1,0:T(8,128)(2,1)S(1)}, bf16[1024,1024]{1,0:T(8,128)(2,1)}, u32[]{:S(2)}) %copy-start) | copy-done | bytes 2097176
  2.2 0.0 copy-start.1
  2.2 1.6 %copy-done.1 = bf16[1024,1024]{1,0:T(8,128)(2,1)S(1)} copy-done((bf16[1024,1024]{1,0:T(8,128)(2,1)S(1)}, bf16[1024,1024]{1,0:T(8,128)(2,1)}, u32[]{:S(2)}) %copy-start.1) | copy-done | bytes 2097176
  3.8 0.0 copy-start.2
  3.8 0.7 copy-done.2
  4.5 0.0 copy-start.4
  4.5 0.0 copy-start.5
  4.5 1.0 %gather_blocks.1 = (bf16[1024,256]{1,0:T(8,128)(2,1)S(1)}, bf16[256,256]{1,0:T(8,128)(2,1)S(1)}, bf16[256,256]{1,0:T(8,128)(2,1)S(1)}, bf16[256,256]{1,0:T(8,128)(2,1)S(1)}, bf16[256,256]{1,0:T(8,128)(2,1)S(1)}) custom-call(s32[4,16]{1,0:T(4,128)S(1)} %bitcast.3, bf16[1024,1024]{1,0:T(8,128)(2,1)S(1)} %copy-done, bf16[1024,1024]{1,0:T(8,128)(2,1)S(1)} %copy-done.1), custom_call_target="tpu_custom_call" | custom-call | tf_op jit(solution)/shard_map/gather_blocks/pallas_call | solution.py:50
  5.5 0.1 collective-permute-start
  5.6 3.2 %collective-permute-start.1 = (bf16[256,256]{1,0:T(8,128)(2,1)S(1)}, bf16[256,256]{1,0:T(8,128)(2,1)S(1)}, u32[]{:S(2)}, u32[]{:S(2)}) collective-permute-start(bf16[256,256]{1,0:T(8,128)(2,1)S(1)} %get-tuple-element.18), channel_id=1, source_target_pairs={{0,32},{16,48},{32,64},{48,80},{64,96},{80,112},{96,128},{112,144}... | collective-permute-start | bytes 393224 | tf_op jit(solution)/shard_map/ppermute | solution.py:20
  8.8 2.4 %collective-permute-start.2 = (bf16[256,256]{1,0:T(8,128)(2,1)S(1)}, bf16[256,256]{1,0:T(8,128)(2,1)S(1)}, u32[]{:S(2)}, u32[]{:S(2)}) collective-permute-start(bf16[256,256]{1,0:T(8,128)(2,1)S(1)} %get-tuple-element.19), channel_id=1, source_target_pairs={{0,64},{16,80},{32,96},{48,112},{64,128},{80,144},{96,160},{112,17... | collective-permute-start | bytes 393224 | tf_op jit(solution)/shard_map/ppermute | solution.py:20
  11.2 0.3 collective-permute-start.3
  11.5 0.0 collective-permute-done.refs_0_
  11.5 3.8 %collective-permute-done.1.refs_1_ = bf16[256,256]{1,0:T(8,128)(2,1)S(1)} collective-permute-done((bf16[256,256]{1,0:T(8,128)(2,1)S(1)}, bf16[256,256]{1,0:T(8,128)(2,1)S(1)}, u32[]{:S(2)}, u32[]{:S(2)}) %collective-permute-start.1) | collective-permute-done | bytes 131104 | tf_op jit(solution)/shard_map/ppermute | solution.py:20
  15.4 1.0 %collective-permute-done.2.refs_2_ = bf16[256,256]{1,0:T(8,128)(2,1)S(1)} collective-permute-done((bf16[256,256]{1,0:T(8,128)(2,1)S(1)}, bf16[256,256]{1,0:T(8,128)(2,1)S(1)}, u32[]{:S(2)}, u32[]{:S(2)}) %collective-permute-start.2) | collective-permute-done | bytes 131104 | tf_op jit(solution)/shard_map/ppermute | solution.py:20
  16.4 2.4 %collective-permute-done.3.refs_3_ = bf16[256,256]{1,0:T(8,128)(2,1)S(1)} collective-permute-done((bf16[256,256]{1,0:T(8,128)(2,1)S(1)}, bf16[256,256]{1,0:T(8,128)(2,1)S(1)}, u32[]{:S(2)}, u32[]{:S(2)}) %collective-permute-start.3) | collective-permute-done | bytes 131104 | tf_op jit(solution)/shard_map/ppermute | solution.py:20
  18.8 0.0 copy-done.4
  18.8 0.0 copy-done.5
  18.8 0.0 copy-start.3
  18.8 13.5 %attend.1 = (bf16[1024,256]{1,0:T(8,128)(2,1)}, f32[1024,256]{1,0:T(8,128)S(1)}, bf16[256,256]{1,0:T(8,128)(2,1)S(1)}, bf16[256,256]{1,0:T(8,128)(2,1)S(1)}, bf1...) custom-call(bf16[1024,256]{1,0:T(8,128)(2,1)S(1)} %copy-done.4, bf16[1024,256]{1,0:T(8,128)(2,1)S(1)} %copy-done.5, ...), custom_call_target="tpu_custom_call" | custom-call | flops 5368709120 | bytes 4194304 | tf_op jit(solution)/shard_map/attend/pallas_call | solution.py:146
  32.3 8.7 %all-to-all-start = ((bf16[16,64,256]{2,1,0:T(8,128)(2,1)}), bf16[16,64,256]{2,1,0:T(8,128)(2,1)S(1)}, u32[]{:S(2)}, u32[]{:S(2)}) async-start(bf16[16,64,256]{2,1,0:T(8,128)(2,1)} %bitcast.1), calls=%async_computation | async-start | bytes 1048576 | tf_op jit(solution)/shard_map/all_to_all | solution.py:227
  41.0 0.1 collective-permute-start.4
  41.1 3.1 %collective-permute-start.5 = (bf16[256,256]{1,0:T(8,128)(2,1)S(1)}, bf16[256,256]{1,0:T(8,128)(2,1)S(1)}, u32[]{:S(2)}, u32[]{:S(2)}) collective-permute-start(bf16[256,256]{1,0:T(8,128)(2,1)S(1)} %get-tuple-element.24), channel_id=1, source_target_pairs={{0,224},{16,240},{32,0},{48,16},{64,32},{80,48},{96,64},{112,80},{... | collective-permute-start | bytes 393224 | tf_op jit(solution)/shard_map/ppermute | solution.py:20
  44.2 3.0 %collective-permute-start.6 = (bf16[256,256]{1,0:T(8,128)(2,1)S(1)}, bf16[256,256]{1,0:T(8,128)(2,1)S(1)}, u32[]{:S(2)}, u32[]{:S(2)}) collective-permute-start(bf16[256,256]{1,0:T(8,128)(2,1)S(1)} %get-tuple-element.25), channel_id=1, source_target_pairs={{0,192},{16,208},{32,224},{48,240},{64,0},{80,16},{96,32},{112,48}... | collective-permute-start | bytes 393224 | tf_op jit(solution)/shard_map/ppermute | solution.py:20
  47.2 3.0 %collective-permute-start.7 = (bf16[256,256]{1,0:T(8,128)(2,1)S(1)}, bf16[256,256]{1,0:T(8,128)(2,1)S(1)}, u32[]{:S(2)}, u32[]{:S(2)}) collective-permute-start(bf16[256,256]{1,0:T(8,128)(2,1)S(1)} %get-tuple-element.26), channel_id=1, source_target_pairs={{0,128},{16,144},{32,160},{48,176},{64,192},{80,208},{96,224},{112... | collective-permute-start | bytes 393224 | tf_op jit(solution)/shard_map/ppermute | solution.py:20
  50.1 0.0 collective-permute-done.4.refs_0_
  50.1 9.3 %collective-permute-done.5.refs_1_ = bf16[256,256]{1,0:T(8,128)(2,1)S(1)} collective-permute-done((bf16[256,256]{1,0:T(8,128)(2,1)S(1)}, bf16[256,256]{1,0:T(8,128)(2,1)S(1)}, u32[]{:S(2)}, u32[]{:S(2)}) %collective-permute-start.5) | collective-permute-done | bytes 131104 | tf_op jit(solution)/shard_map/ppermute | solution.py:20
  59.5 0.0 collective-permute-done.6.refs_2_
  59.5 2.7 %collective-permute-done.7.refs_3_ = bf16[256,256]{1,0:T(8,128)(2,1)S(1)} collective-permute-done((bf16[256,256]{1,0:T(8,128)(2,1)S(1)}, bf16[256,256]{1,0:T(8,128)(2,1)S(1)}, u32[]{:S(2)}, u32[]{:S(2)}) %collective-permute-start.7) | collective-permute-done | bytes 131104 | tf_op jit(solution)/shard_map/ppermute | solution.py:20
  62.2 0.0 copy-done.3
  62.2 1.6 %add_returned.1 = bf16[1024,256]{1,0:T(8,128)(2,1)} custom-call(s32[4,16]{1,0:T(4,128)S(1)} %bitcast.4, f32[1024,256]{1,0:T(8,128)S(1)} %get-tuple-element.22.grad_ref, bf16[256,256]{1,0:T(8,128)(2,1)S(1)} %collective-permute-done.4.refs_0_, bf16[256,256]{1,0:T(8,128)(2,1)S(1)} %collective-permute-done.5.refs_1_, ...), custom_call_target="tpu_custom_call" | custom-call | tf_op jit(solution)/shard_map/add_returned/pallas_call | solution.py:176
  63.8 0.0 all-to-all-done.in_ref
  63.8 7.0 %all-to-all-start.1 = ((bf16[16,64,256]{2,1,0:T(8,128)(2,1)}), bf16[16,64,256]{2,1,0:T(8,128)(2,1)S(1)}, u32[]{:S(2)}, u32[]{:S(2)}) async-start(bf16[16,64,256]{2,1,0:T(8,128)(2,1)} %bitcast.2), calls=%async_computation.1 | async-start | bytes 1048576 | tf_op jit(solution)/shard_map/all_to_all | solution.py:227
  70.7 0.8 lay_queries.1
  71.6 14.8 %all-to-all-done.1.in_ref = bf16[16,64,256]{2,1,0:T(8,128)(2,1)S(1)} async-done(((bf16[16,64,256]{2,1,0:T(8,128)(2,1)}), bf16[16,64,256]{2,1,0:T(8,128)(2,1)S(1)}, u32[]{:S(2)}, u32[]{:S(2)}) %all-to-all-start.1) | async-done | bytes 524320 | tf_op jit(solution)/shard_map/all_to_all | solution.py:227
  86.4 0.8 lay_keys.1
Async XLA Ops:
  0.6 1.6 %copy-start = (bf16[1024,1024]{1,0:T(8,128)(2,1)S(1)}, bf16[1024,1024]{1,0:T(8,128)(2,1)}, u32[]{:S(2)}) copy-start(bf16[1024,1024]{1,0:T(8,128)(2,1)} %key_ref.1) | copy-start | bytes 6291460
  2.2 1.6 %copy-start.1 = (bf16[1024,1024]{1,0:T(8,128)(2,1)S(1)}, bf16[1024,1024]{1,0:T(8,128)(2,1)}, u32[]{:S(2)}) copy-start(bf16[1024,1024]{1,0:T(8,128)(2,1)} %value_ref.1) | copy-start | bytes 6291460
  3.8 0.7 copy-start.2
  4.5 14.3 %copy-start.4 = (bf16[1024,256]{1,0:T(8,128)(2,1)S(1)}, bf16[1024,256]{1,0:T(8,128)(2,1)}, u32[]{:S(2)}) copy-start(bf16[1024,256]{1,0:T(8,128)(2,1)} %q_ref.1) | copy-start | bytes 1572868
  4.5 14.3 %copy-start.5 = (bf16[1024,256]{1,0:T(8,128)(2,1)S(1)}, bf16[1024,256]{1,0:T(8,128)(2,1)}, u32[]{:S(2)}) copy-start(bf16[1024,256]{1,0:T(8,128)(2,1)} %g_ref.1) | copy-start | bytes 1572868
  5.5 6.0 %collective-permute-start = (bf16[256,256]{1,0:T(8,128)(2,1)S(1)}, bf16[256,256]{1,0:T(8,128)(2,1)S(1)}, u32[]{:S(2)}, u32[]{:S(2)}) collective-permute-start(bf16[256,256]{1,0:T(8,128)(2,1)S(1)} %get-tuple-element.17), channel_id=1, source_target_pairs={{0,16},{16,32},{32,48},{48,64},{64,80},{80,96},{96,112},{112,128},... | collective-permute-start | bytes 393224 | tf_op jit(solution)/shard_map/ppermute | solution.py:20
  5.6 9.8 %collective-permute-start.1 = (bf16[256,256]{1,0:T(8,128)(2,1)S(1)}, bf16[256,256]{1,0:T(8,128)(2,1)S(1)}, u32[]{:S(2)}, u32[]{:S(2)}) collective-permute-start(bf16[256,256]{1,0:T(8,128)(2,1)S(1)} %get-tuple-element.18), channel_id=1, source_target_pairs={{0,32},{16,48},{32,64},{48,80},{64,96},{80,112},{96,128},{112,144}... | collective-permute-start | bytes 393224 | tf_op jit(solution)/shard_map/ppermute | solution.py:20
  8.8 7.6 %collective-permute-start.2 = (bf16[256,256]{1,0:T(8,128)(2,1)S(1)}, bf16[256,256]{1,0:T(8,128)(2,1)S(1)}, u32[]{:S(2)}, u32[]{:S(2)}) collective-permute-start(bf16[256,256]{1,0:T(8,128)(2,1)S(1)} %get-tuple-element.19), channel_id=1, source_target_pairs={{0,64},{16,80},{32,96},{48,112},{64,128},{80,144},{96,160},{112,17... | collective-permute-start | bytes 393224 | tf_op jit(solution)/shard_map/ppermute | solution.py:20
  11.2 7.6 %collective-permute-start.3 = (bf16[256,256]{1,0:T(8,128)(2,1)S(1)}, bf16[256,256]{1,0:T(8,128)(2,1)S(1)}, u32[]{:S(2)}, u32[]{:S(2)}) collective-permute-start(bf16[256,256]{1,0:T(8,128)(2,1)S(1)} %get-tuple-element.20), channel_id=1, source_target_pairs={{0,128},{16,144},{32,160},{48,176},{64,192},{80,208},{96,224},{112... | collective-permute-start | bytes 393224 | tf_op jit(solution)/shard_map/ppermute | solution.py:20
  18.8 43.4 %copy-start.3 = (s32[16,4]{0,1:T(4,128)S(1)}, s32[16,4]{0,1:T(4,128)}, u32[]{:S(2)}) copy-start(s32[16,4]{0,1:T(4,128)} %param.9) | copy-start | bytes 772
  32.3 31.5 %all-to-all-start = ((bf16[16,64,256]{2,1,0:T(8,128)(2,1)}), bf16[16,64,256]{2,1,0:T(8,128)(2,1)S(1)}, u32[]{:S(2)}, u32[]{:S(2)}) async-start(bf16[16,64,256]{2,1,0:T(8,128)(2,1)} %bitcast.1), calls=%async_computation | async-start | bytes 1048576 | tf_op jit(solution)/shard_map/all_to_all | solution.py:227
  41.0 9.2 %collective-permute-start.4 = (bf16[256,256]{1,0:T(8,128)(2,1)S(1)}, bf16[256,256]{1,0:T(8,128)(2,1)S(1)}, u32[]{:S(2)}, u32[]{:S(2)}) collective-permute-start(bf16[256,256]{1,0:T(8,128)(2,1)S(1)} %get-tuple-element.23), channel_id=1, source_target_pairs={{0,240},{16,0},{32,16},{48,32},{64,48},{80,64},{96,80},{112,96},{1... | collective-permute-start | bytes 393224 | tf_op jit(solution)/shard_map/ppermute | solution.py:20
  41.1 18.4 %collective-permute-start.5 = (bf16[256,256]{1,0:T(8,128)(2,1)S(1)}, bf16[256,256]{1,0:T(8,128)(2,1)S(1)}, u32[]{:S(2)}, u32[]{:S(2)}) collective-permute-start(bf16[256,256]{1,0:T(8,128)(2,1)S(1)} %get-tuple-element.24), channel_id=1, source_target_pairs={{0,224},{16,240},{32,0},{48,16},{64,32},{80,48},{96,64},{112,80},{... | collective-permute-start | bytes 393224 | tf_op jit(solution)/shard_map/ppermute | solution.py:20
  44.2 15.2 %collective-permute-start.6 = (bf16[256,256]{1,0:T(8,128)(2,1)S(1)}, bf16[256,256]{1,0:T(8,128)(2,1)S(1)}, u32[]{:S(2)}, u32[]{:S(2)}) collective-permute-start(bf16[256,256]{1,0:T(8,128)(2,1)S(1)} %get-tuple-element.25), channel_id=1, source_target_pairs={{0,192},{16,208},{32,224},{48,240},{64,0},{80,16},{96,32},{112,48}... | collective-permute-start | bytes 393224 | tf_op jit(solution)/shard_map/ppermute | solution.py:20
  47.2 15.0 %collective-permute-start.7 = (bf16[256,256]{1,0:T(8,128)(2,1)S(1)}, bf16[256,256]{1,0:T(8,128)(2,1)S(1)}, u32[]{:S(2)}, u32[]{:S(2)}) collective-permute-start(bf16[256,256]{1,0:T(8,128)(2,1)S(1)} %get-tuple-element.26), channel_id=1, source_target_pairs={{0,128},{16,144},{32,160},{48,176},{64,192},{80,208},{96,224},{112... | collective-permute-start | bytes 393224 | tf_op jit(solution)/shard_map/ppermute | solution.py:20
  63.8 22.6 %all-to-all-start.1 = ((bf16[16,64,256]{2,1,0:T(8,128)(2,1)}), bf16[16,64,256]{2,1,0:T(8,128)(2,1)S(1)}, u32[]{:S(2)}, u32[]{:S(2)}) async-start(bf16[16,64,256]{2,1,0:T(8,128)(2,1)} %bitcast.2), calls=%async_computation.1 | async-start | bytes 1048576 | tf_op jit(solution)/shard_map/all_to_all | solution.py:227

commit v2 on v1

v2 whole, which is shorter than its diff:
```python
import jax
import jax.numpy as jnp
from jax import lax
from jax.experimental import pallas as pl
from jax.experimental.pallas import tpu as pltpu
from jax.sharding import PartitionSpec as P

HD = 128
BLK = 256
NEG = -1e30
SCALE = HD**-0.5
FACTOR = SCALE * 1.4426950408889634
HBM = pl.BlockSpec(memory_space=pltpu.HBM)
VMEM = pl.BlockSpec(memory_space=pltpu.VMEM)
SMEM = pl.BlockSpec(memory_space=pltpu.SMEM)


def rotate(value, axis, steps):
    count = lax.axis_size(axis)
    return lax.ppermute(value, axis, [(source, (source + steps) % count) for source in range(count)])


def block_start(index_ref, ctx_index, level_num, ctx_count):
    target = jnp.minimum(ctx_index + 2**level_num, ctx_count - 1)
    return pl.multiple_of(index_ref[level_num, target] * BLK, BLK)


def gather_blocks(block_index, keys, values, ctx_count, levels):
    def body(index_ref, key_ref, value_ref, own_ref, *refs):
        sends, sems = refs[:levels], refs[levels]
        ctx_index = lax.axis_index("ctx")
        begin = pl.multiple_of(lax.axis_index("head") // 2 * HD, HD)
        copies = []
        for half, source in ((0, key_ref), (1, value_ref)):
            columns = slice(half * HD, (half + 1) * HD)
            for level_num in range(levels):
                start = block_start(index_ref, ctx_index, level_num, ctx_count)
                copies.append((source.at[pl.ds(start, BLK), pl.ds(begin, HD)], sends[level_num].at[:, columns]))
            copies.append((source.at[:, pl.ds(begin, HD)], own_ref.at[:, columns]))
        started = [
            pltpu.make_async_copy(source, target, sems.at[number])
            for number, (source, target) in enumerate(copies)
        ]
        for copy in started:
            copy.start()
        for copy in started:
            copy.wait()

    rows = keys.shape[0]
    keys = pltpu.with_memory_space_constraint(keys, pltpu.HBM)
    values = pltpu.with_memory_space_constraint(values, pltpu.HBM)
    return pl.pallas_call(
        body,
        out_shape=(jax.ShapeDtypeStruct((rows, 2 * HD), keys.dtype),)
        + (jax.ShapeDtypeStruct((BLK, 2 * HD), keys.dtype),) * levels,
        in_specs=[SMEM, HBM, HBM],
        out_specs=(VMEM,) * (levels + 1),
        scratch_shapes=[pltpu.SemaphoreType.DMA((2 * levels + 2,))],
        compiler_params=pltpu.CompilerParams(vmem_limit_bytes=4 << 20),
        name="gather_blocks",
    )(block_index, keys, values)


def dot(left, right):
    return jnp.dot(left, right, preferred_element_type=jnp.float32)


def spot(number):
    return slice(number * BLK, (number + 1) * BLK)


def params(mib):
    return pltpu.CompilerParams(vmem_limit_bytes=mib << 20)


def cost(dots, nbytes):
    return pl.CostEstimate(flops=dots * 2 * BLK * BLK * HD, bytes_accessed=nbytes, transcendentals=0)


def pairs(row_tiles):
    return [(part, number) for part in range(row_tiles) for number in range(part + 1)]


def own_scores(queries, grad_out, own):
    rows, width = queries.shape
    row_tiles, heads = rows // BLK, width // HD
    places = pairs(row_tiles)
    total = heads * len(places)

    def body(q_ref, g_ref, own_ref, weight_ref, prob_ref, stat_ref):
        key_at = lax.broadcasted_iota(jnp.int32, (BLK, BLK), 0)
        causal = key_at <= lax.broadcasted_iota(jnp.int32, (BLK, BLK), 1)
        for head in range(heads):
            columns = slice(head * HD, (head + 1) * HD)
            for part in range(row_tiles):
                query_t, grad_t = q_ref[spot(part), columns].T, g_ref[spot(part), columns].T
                for number in range(part + 1):
                    place = head * len(places) + places.index((part, number))
                    scores = dot(own_ref[spot(number), :HD], query_t)
                    if number == part:
                        scores = jnp.where(causal, scores, NEG)
                    top = jnp.max(scores, axis=0, keepdims=True) * FACTOR
                    weights = jnp.exp2(scores * FACTOR - top)
                    grad_probs = dot(own_ref[spot(number), HD:], grad_t)
                    weight_ref[place] = weights
                    prob_ref[place] = grad_probs
                    stat_ref[0, place : place + 1] = top
                    stat_ref[1, place : place + 1] = jnp.sum(weights, axis=0, keepdims=True)
                    stat_ref[2, place : place + 1] = jnp.sum(weights * grad_probs, axis=0, keepdims=True)

    tiles = jax.ShapeDtypeStruct((total, BLK, BLK), jnp.float32)
    return pl.pallas_call(
        body,
        out_shape=(tiles, tiles, jax.ShapeDtypeStruct((3, total, BLK), jnp.float32)),
        in_specs=[VMEM] * 3,
        out_specs=(VMEM,) * 3,
        compiler_params=params(16),
        cost_estimate=cost(2 * total, 2 << 20),
        name="own_scores",
    )(queries, grad_out, own)


def partner_part(queries, grad_out, blocks, stats):
    rows, width = queries.shape
    levels, row_tiles, heads = len(blocks), rows // BLK, width // HD
    places = pairs(row_tiles)
    total = heads * len(places)

    def body(q_ref, g_ref, stat_ref, *refs):
        block_refs, part_refs = refs[:levels], refs[levels : 2 * levels]
        low_ref, coef_ref, acc_ref = refs[2 * levels :]
        ctx_index = lax.axis_index("ctx")
        live = [ctx_index >= 2**level_num for level_num in range(levels)]
        for head in range(heads):
            columns = slice(head * HD, (head + 1) * HD)
            for part in range(row_tiles):
                query, grad = q_ref[spot(part), columns], g_ref[spot(part), columns]
                query_t, grad_t = query.T, grad.T
                weights, grad_probs, tops, sums, products = [], [], [], [], []
                for level_num in range(levels):
                    scores = dot(block_refs[level_num][:, :HD], query_t)
                    top = jnp.max(scores, axis=0, keepdims=True) * FACTOR
                    weight = jnp.exp2(scores * FACTOR - jnp.where(live[level_num], top, -NEG))
                    grad_prob = dot(block_refs[level_num][:, HD:], grad_t)
                    weights.append(weight)
                    grad_probs.append(grad_prob)
                    tops.append(jnp.where(live[level_num], top, NEG))
                    sums.append(jnp.sum(weight, axis=0, keepdims=True))
                    products.append(jnp.sum(weight * grad_prob, axis=0, keepdims=True))
                first = head * len(places) + places.index((part, 0))
                for place in range(first, first + part + 1):
                    tops.append(stat_ref[0, place : place + 1])
                    sums.append(stat_ref[1, place : place + 1])
                    products.append(stat_ref[2, place : place + 1])
                row_max = tops[0]
                for top in tops[1:]:
                    row_max = jnp.maximum(row_max, top)
                ratios = [jnp.exp2(top - row_max) for top in tops]
                inverse = 1.0 / sum(each * ratio for each, ratio in zip(sums, ratios))
                delta = sum(each * ratio for each, ratio in zip(products, ratios)) * inverse
                for number in range(part + 1):
                    place = first + number
                    coef_ref[place : place + 1] = ratios[levels + number] * inverse
                at = total + head * row_tiles + part
                coef_ref[at : at + 1] = delta
                for level_num in range(levels):
                    probs = weights[level_num] * (ratios[level_num] * inverse)
                    low = (probs * (grad_probs[level_num] - delta)).astype(jnp.bfloat16)
                    low_ref[head * row_tiles + part, spot(level_num)] = low
                    key_part, value_part = dot(low, query), dot(probs.astype(jnp.bfloat16), grad)
                    if head == 0 and part == 0:
                        acc_ref[spot(level_num), :HD] = key_part
                        acc_ref[spot(level_num), HD:] = value_part
                    elif head == heads - 1 and part == row_tiles - 1:
                        key_part = (acc_ref[spot(level_num), :HD] + key_part) * SCALE
                        part_refs[level_num][:, :HD] = key_part.astype(jnp.bfloat16)
                        value_part = acc_ref[spot(level_num), HD:] + value_part
                        part_refs[level_num][:, HD:] = value_part.astype(jnp.bfloat16)
                    else:
                        acc_ref[spot(level_num), :HD] += key_part
                        acc_ref[spot(level_num), HD:] += value_part

    held = total + heads * row_tiles
    return pl.pallas_call(
        body,
        out_shape=(jax.ShapeDtypeStruct((BLK, 2 * HD), jnp.bfloat16),) * levels
        + (
            jax.ShapeDtypeStruct((heads * row_tiles, levels * BLK, BLK), jnp.bfloat16),
            jax.ShapeDtypeStruct((held, BLK), jnp.float32),
        ),
        in_specs=[VMEM] * (3 + levels),
        out_specs=(VMEM,) * (2 + levels),
        scratch_shapes=[pltpu.VMEM((levels * BLK, 2 * HD), jnp.float32)],
        compiler_params=params(16),
        cost_estimate=cost(4 * heads * row_tiles * levels, 2 << 20),
        name="partner_part",
    )(queries, grad_out, stats, *blocks)


def own_part(queries, grad_out, own, blocks, weights, grad_probs, low, coef):
    rows, width = queries.shape
    levels, row_tiles, heads = len(blocks), rows // BLK, width // HD
    places = pairs(row_tiles)
    total = heads * len(places)

    def body(q_ref, g_ref, own_ref, weight_ref, prob_ref, low_ref, coef_ref, *refs):
        block_refs = refs[:levels]
        dq_ref, grad_ref, kt_ref = refs[levels:]
        for number in range(row_tiles):
            kt_ref[:, spot(number)] = own_ref[spot(number), :HD].T
        for level_num in range(levels):
            kt_ref[:, spot(row_tiles + level_num)] = block_refs[level_num][:, :HD].T
        for head in range(heads):
            columns = slice(head * HD, (head + 1) * HD)
            for part in range(row_tiles):
                query, grad = q_ref[spot(part), columns], g_ref[spot(part), columns]
                at = total + head * row_tiles + part
                delta = coef_ref[at : at + 1]
                dq_t = dot(kt_ref[:, rows:], low_ref[head * row_tiles + part])
                for number in range(part + 1):
                    place = head * len(places) + places.index((part, number))
                    probs = weight_ref[place] * coef_ref[place : place + 1]
                    scores_low = (probs * (prob_ref[place] - delta)).astype(jnp.bfloat16)
                    key_part, value_part = dot(scores_low, query), dot(probs.astype(jnp.bfloat16), grad)
                    dq_t += dot(kt_ref[:, spot(number)], scores_low)
                    if head == 0 and number == part:
                        grad_ref[spot(number), :HD] = key_part
                        grad_ref[spot(number), HD:] = value_part
                    else:
                        grad_ref[spot(number), :HD] += key_part
                        grad_ref[spot(number), HD:] += value_part
                dq_ref[spot(part), columns] = (dq_t * SCALE).T.astype(jnp.bfloat16)

    return pl.pallas_call(
        body,
        out_shape=(
            jax.ShapeDtypeStruct(queries.shape, jnp.bfloat16),
            jax.ShapeDtypeStruct((rows, 2 * HD), jnp.float32),
        ),
        in_specs=[VMEM] * (7 + levels),
        out_specs=(VMEM,) * 2,
        scratch_shapes=[pltpu.VMEM((HD, rows + levels * BLK), jnp.bfloat16)],
        compiler_params=params(16),
        cost_estimate=cost(3 * total + heads * row_tiles * levels, 2 << 20),
        name="own_part",
    )(queries, grad_out, own, weights, grad_probs, low, coef, *blocks)


def add_returned(block_index, dq_local, gradients, returned, ctx_count):
    levels, width = len(returned), dq_local.shape[1]

    def body(index_ref, dq_ref, grad_ref, *refs):
        out_ref, total_ref = refs[levels:]
        ctx_index = lax.axis_index("ctx")
        total_ref[:, :HD] = grad_ref[:, :HD] * SCALE
        total_ref[:, HD:] = grad_ref[:, HD:]
        for level_num in range(levels):
            start = block_start(index_ref, ctx_index, level_num, ctx_count)
            total_ref[pl.ds(start, BLK), :] += refs[level_num][...].astype(jnp.float32)
        out_ref[:, :width] = dq_ref[...]
        out_ref[:, width:] = total_ref[...].astype(jnp.bfloat16)

    rows = dq_local.shape[0]
    return pl.pallas_call(
        body,
        out_shape=jax.ShapeDtypeStruct((rows, width + 2 * HD), jnp.bfloat16),
        in_specs=[SMEM] + [VMEM] * (levels + 2),
        out_specs=VMEM,
        scratch_shapes=[pltpu.VMEM(gradients.shape, jnp.float32)],
        compiler_params=params(6),
        name="add_returned",
    )(block_index, dq_local, gradients, *returned)


def lay_out(gathered, width):
    count, token_rows, _ = gathered.shape

    def body(in_ref, query_ref, key_ref, value_ref):
        for number in range(count):
            query_ref[:, number * width : (number + 1) * width] = in_ref[number, :, :width]
        for number in range(count // 2):
            total = in_ref[2 * number, :, width:].astype(jnp.float32)
            total += in_ref[2 * number + 1, :, width:].astype(jnp.float32)
            total = total.astype(jnp.bfloat16)
            key_ref[:, number * HD : (number + 1) * HD] = total[:, :HD]
            value_ref[:, number * HD : (number + 1) * HD] = total[:, HD:]

    shape = jax.ShapeDtypeStruct((token_rows, count // 2 * HD), gathered.dtype)
    return pl.pallas_call(
        body,
        out_shape=(jax.ShapeDtypeStruct((token_rows, count * width), gathered.dtype), shape, shape),
        in_specs=[VMEM],
        out_specs=(VMEM,) * 3,
        compiler_params=params(6),
        name="lay_out",
    )(gathered)


def on_device(queries, keys, values, grad_out, block_index):
    ctx_count = lax.axis_size("ctx")
    head_count = lax.axis_size("head")
    levels = ctx_count.bit_length() - 1
    rows, width = queries.shape
    block_index = block_index.T
    own, *sends = gather_blocks(block_index, keys, values, ctx_count, levels)
    blocks = [rotate(sends[level_num], "ctx", 2**level_num) for level_num in range(levels)]
    weights, grad_probs, stats = own_scores(queries, grad_out, own)
    *parts, low, coef = partner_part(queries, grad_out, blocks, stats)
    returned = [rotate(parts[level_num], "ctx", -(2**level_num)) for level_num in range(levels)]
    dq_local, gradients = own_part(queries, grad_out, own, blocks, weights, grad_probs, low, coef)
    joined = add_returned(block_index, dq_local, gradients, returned, ctx_count)
    split = joined.reshape(head_count, rows // head_count, joined.shape[1])
    gathered = lax.all_to_all(split, "head", split_axis=0, concat_axis=0, tiled=True)
    return tuple(lay_out(gathered, width))


def solution(mesh):
    placed = (P("ctx", "head"), P("ctx", None), P("ctx", None), P("ctx", "head"), P())
    return jax.shard_map(
        on_device,
        mesh=mesh,
        in_specs=placed,
        out_specs=(P(("ctx", "head"), None), P(("ctx", "head"), None), P(("ctx", "head"), None)),
        check_vma=False,
    )
```

time: 87.5 us -> 79.5 us (0.909)
  blocking collectives: 0 us -> 35.3 us
  waiting for transfers between devices: 34.1 us -> 11.3 us
  starting transfers between devices: 30.8 us -> 14.6 us
  local copies, waits for them, and re-layouts: 3.87 us -> 0.77 us
  Pallas kernels: 17.7 us -> 16.7 us
    all_to_all x0 -> x1, blocking collectives: none -> 35.3 us  [on_device(): lax.all_to_all(split, 'head', split_axis=0, concat_axis=0, tiled=True)]
    all_to_all x2 -> x0, starting transfers between devices: 15.6 us -> none  [spread(): lax.all_to_all(split, 'head', split_axis=0, concat_axis=0, tiled=True)]
    all_to_all x2 -> x0, waiting for transfers between devices: 14.8 us -> none  [spread(): lax.all_to_all(split, 'head', split_axis=0, concat_axis=0, tiled=True)]
    ppermute x8, waiting for transfers between devices: 19.3 us -> 11.3 us  [rotate(): lax.ppermute(value, axis, [(source, (source + steps) % count) for source...]
    unnamed x12 -> x8, local copies, waits for them, and re-layouts: 3.87 us -> 0.77 us
    pallas_call x4 -> x5, Pallas kernels: 16.7 us -> 14.7 us  [the longest x1 7.9 us: partner_part(): pl.pallas_call(body, out_shape=(jax.ShapeDtypeStruct((BLK, 2 * HD), jnp.b...]
    pallas_call x1, Pallas kernels: 0.98 us -> 1.94 us  [gather_blocks(): pl.pallas_call(body, out_shape=(jax.ShapeDtypeStruct((rows, 2 * HD), keys...]
  transfers between devices with their start and end apart: 10 -> 8, of which waited for: 6 -> 6; matrix products, arithmetic and copies ran while one was open for 0% -> 0% of each run, Pallas kernels for 3% -> 6%
where the time goes in v2:
time: 79.5 us; the launch traced here: 79.4 us
  blocking collectives  35.3 us (44%)
  Pallas kernels  16.7 us (21%)
  starting transfers between devices  14.6 us (18%)
  waiting for transfers between devices  11.3 us (14%)
    all_to_all x1, blocking collectives, on_device(): lax.all_to_all(split, 'head', split_axis=0, concat_axis=0, tiled=True)  35.3 us
    ppermute x8, starting transfers between devices, rotate(): lax.ppermute(value, axis, [(source, (source + steps) % count) for source...  14.6 us
    ppermute x8, waiting for transfers between devices, rotate(): lax.ppermute(value, axis, [(source, (source + steps) % count) for source...  11.3 us
    pallas_call x1, Pallas kernels, partner_part(): pl.pallas_call(body, out_shape=(jax.ShapeDtypeStruct((BLK, 2 * HD), jnp.b...  7.9 us
    pallas_call x1, Pallas kernels, own_part(): pl.pallas_call(body, out_shape=(jax.ShapeDtypeStruct(queries.shape, jnp.b...  2.87 us
    pallas_call x1, Pallas kernels, own_scores(): pl.pallas_call(body, out_shape=(tiles, tiles, jax.ShapeDtypeStruct((3, to...  2.16 us
    pallas_call x1, Pallas kernels, gather_blocks(): pl.pallas_call(body, out_shape=(jax.ShapeDtypeStruct((rows, 2 * HD), keys...  1.94 us
  transfers between devices with their start and end apart: 8, of which 6 were waited for; matrix products, arithmetic and copies ran while one was open for 0% of the time, Pallas kernels for 6%

profile of v2, /device:TPU:6, one launch (start us, length us, event | category | flops | bytes accessed | tf_op | source)
XLA Modules:
  0.0 79.4 jit_solution(17965927786048753354)
XLA Ops:
  0.6 0.0 copy-start.1
  0.6 0.0 copy-start
  0.7 0.0 copy-start.2
  0.7 0.8 copy-done.2
  1.4 1.9 %gather_blocks.1 = (bf16[1024,256]{1,0:T(8,128)(2,1)S(1)}, bf16[256,256]{1,0:T(8,128)(2,1)S(1)}, bf16[256,256]{1,0:T(8,128)(2,1)S(1)}, bf16[256,256]{1,0:T(8,128)(2,1)S(1)}, bf16[256,256]{1,0:T(8,128)(2,1)S(1)}) custom-call(s32[4,16]{1,0:T(4,128)S(1)} %bitcast.3, bf16[1024,1024]{1,0:T(8,128)(2,1)} %key_ref.1, bf16[1024,1024]{1,0:T(8,128)(2,1)} %value_ref.1), custom_call_target="tpu_custom_call" | custom-call | tf_op jit(solution)/shard_map/gather_blocks/pallas_call | solution.py:52
  3.4 0.1 collective-permute-start
  3.5 3.3 %collective-permute-start.1 = (bf16[256,256]{1,0:T(8,128)(2,1)S(1)}, bf16[256,256]{1,0:T(8,128)(2,1)S(1)}, u32[]{:S(2)}, u32[]{:S(2)}) collective-permute-start(bf16[256,256]{1,0:T(8,128)(2,1)S(1)} %get-tuple-element.24), channel_id=1, source_target_pairs={{0,32},{16,48},{32,64},{48,80},{64,96},{80,112},{96,128},{112,144}... | collective-permute-start | bytes 393224 | tf_op jit(solution)/shard_map/ppermute | solution.py:20
  6.8 2.3 %collective-permute-start.2 = (bf16[256,256]{1,0:T(8,128)(2,1)S(1)}, bf16[256,256]{1,0:T(8,128)(2,1)S(1)}, u32[]{:S(2)}, u32[]{:S(2)}) collective-permute-start(bf16[256,256]{1,0:T(8,128)(2,1)S(1)} %get-tuple-element.25), channel_id=1, source_target_pairs={{0,64},{16,80},{32,96},{48,112},{64,128},{80,144},{96,160},{112,17... | collective-permute-start | bytes 393224 | tf_op jit(solution)/shard_map/ppermute | solution.py:20
  9.1 0.4 collective-permute-start.3
  9.4 0.0 copy-done.1
  9.4 0.0 copy-done
  9.4 2.2 %own_scores.1 = (f32[20,256,256]{2,1,0:T(8,128)S(1)}, f32[20,256,256]{2,1,0:T(8,128)S(1)}, f32[3,20,256]{2,1,0:T(8,128)S(1)}) custom-call(bf16[1024,256]{1,0:T(8,128)(2,1)S(1)} %copy-done, bf16[1024,256]{1,0:T(8,128)(2,1)S(1)} %copy-done.1, bf16[1024,256]{1,0:T(8,128)(2,1)S(1)} %get-tuple-element.19.own_ref), custom_call_target="tpu_custom_call" | custom-call | flops 671088640 | bytes 2097152 | tf_op jit(solution)/shard_map/own_scores/pallas_call | solution.py:112
  11.6 0.0 collective-permute-done.refs_0_
  11.6 1.8 %collective-permute-done.1.refs_1_ = bf16[256,256]{1,0:T(8,128)(2,1)S(1)} collective-permute-done((bf16[256,256]{1,0:T(8,128)(2,1)S(1)}, bf16[256,256]{1,0:T(8,128)(2,1)S(1)}, u32[]{:S(2)}, u32[]{:S(2)}) %collective-permute-start.1) | collective-permute-done | bytes 131104 | tf_op jit(solution)/shard_map/ppermute | solution.py:20
  13.4 1.1 %collective-permute-done.2.refs_2_ = bf16[256,256]{1,0:T(8,128)(2,1)S(1)} collective-permute-done((bf16[256,256]{1,0:T(8,128)(2,1)S(1)}, bf16[256,256]{1,0:T(8,128)(2,1)S(1)}, u32[]{:S(2)}, u32[]{:S(2)}) %collective-permute-start.2) | collective-permute-done | bytes 131104 | tf_op jit(solution)/shard_map/ppermute | solution.py:20
  14.5 2.2 %collective-permute-done.3.refs_3_ = bf16[256,256]{1,0:T(8,128)(2,1)S(1)} collective-permute-done((bf16[256,256]{1,0:T(8,128)(2,1)S(1)}, bf16[256,256]{1,0:T(8,128)(2,1)S(1)}, u32[]{:S(2)}, u32[]{:S(2)}) %collective-permute-start.3) | collective-permute-done | bytes 131104 | tf_op jit(solution)/shard_map/ppermute | solution.py:20
  16.7 7.9 %partner_part.1 = (bf16[256,256]{1,0:T(8,128)(2,1)S(1)}, bf16[256,256]{1,0:T(8,128)(2,1)S(1)}, bf16[256,256]{1,0:T(8,128)(2,1)S(1)}, bf16[256,256]{1,0:T(8,128)(...) custom-call(bf16[1024,256]{1,0:T(8,128)(2,1)S(1)} %copy-done, bf16[1024,256]{1,0:T(8,128)(2,1)S(1)} %copy-done.1, ...), custom_call_target="tpu_custom_call" | custom-call | flops 2147483648 | bytes 2097152 | tf_op jit(solution)/shard_map/partner_part/pallas_call | solution.py:184
  24.6 0.1 collective-permute-start.4
  24.7 2.4 %collective-permute-start.5 = (bf16[256,256]{1,0:T(8,128)(2,1)S(1)}, bf16[256,256]{1,0:T(8,128)(2,1)S(1)}, u32[]{:S(2)}, u32[]{:S(2)}) collective-permute-start(bf16[256,256]{1,0:T(8,128)(2,1)S(1)} %get-tuple-element.32), channel_id=1, source_target_pairs={{0,224},{16,240},{32,0},{48,16},{64,32},{80,48},{96,64},{112,80},{... | collective-permute-start | bytes 393224 | tf_op jit(solution)/shard_map/ppermute | solution.py:20
  27.2 4.4 %collective-permute-start.6 = (bf16[256,256]{1,0:T(8,128)(2,1)S(1)}, bf16[256,256]{1,0:T(8,128)(2,1)S(1)}, u32[]{:S(2)}, u32[]{:S(2)}) collective-permute-start(bf16[256,256]{1,0:T(8,128)(2,1)S(1)} %get-tuple-element.33), channel_id=1, source_target_pairs={{0,192},{16,208},{32,224},{48,240},{64,0},{80,16},{96,32},{112,48}... | collective-permute-start | bytes 393224 | tf_op jit(solution)/shard_map/ppermute | solution.py:20
  31.6 1.6 %collective-permute-start.7 = (bf16[256,256]{1,0:T(8,128)(2,1)S(1)}, bf16[256,256]{1,0:T(8,128)(2,1)S(1)}, u32[]{:S(2)}, u32[]{:S(2)}) collective-permute-start(bf16[256,256]{1,0:T(8,128)(2,1)S(1)} %get-tuple-element.34), channel_id=1, source_target_pairs={{0,128},{16,144},{32,160},{48,176},{64,192},{80,208},{96,224},{112... | collective-permute-start | bytes 393224 | tf_op jit(solution)/shard_map/ppermute | solution.py:20
  33.2 0.0 copy-start.3
  33.2 2.9 %own_part.1 = (bf16[1024,256]{1,0:T(8,128)(2,1)S(1)}, f32[1024,256]{1,0:T(8,128)S(1)}) custom-call(bf16[1024,256]{1,0:T(8,128)(2,1)S(1)} %copy-done, bf16[1024,256]{1,0:T(8,128)(2,1)S(1)} %copy-done.1, bf16[1024,256]{1,0:T(8,128)(2,1)S(1)} %get-tuple-element.19.own_ref, f32[20,256,256]{2,1,0:T(8,128)S(1)} %get-tuple-element.20.weight_ref, ...), custom_call_target="tpu_custom_call" | custom-call | flops 1543503872 | bytes 2097152 | tf_op jit(solution)/shard_map/own_part/pallas_call | solution.py:234
  36.1 0.0 collective-permute-done.4.refs_0_
  36.1 1.1 %collective-permute-done.5.refs_1_ = bf16[256,256]{1,0:T(8,128)(2,1)S(1)} collective-permute-done((bf16[256,256]{1,0:T(8,128)(2,1)S(1)}, bf16[256,256]{1,0:T(8,128)(2,1)S(1)}, u32[]{:S(2)}, u32[]{:S(2)}) %collective-permute-start.5) | collective-permute-done | bytes 131104 | tf_op jit(solution)/shard_map/ppermute | solution.py:20
  37.2 3.5 %collective-permute-done.6.refs_2_ = bf16[256,256]{1,0:T(8,128)(2,1)S(1)} collective-permute-done((bf16[256,256]{1,0:T(8,128)(2,1)S(1)}, bf16[256,256]{1,0:T(8,128)(2,1)S(1)}, u32[]{:S(2)}, u32[]{:S(2)}) %collective-permute-start.6) | collective-permute-done | bytes 131104 | tf_op jit(solution)/shard_map/ppermute | solution.py:20
  40.7 1.6 %collective-permute-done.7.refs_3_ = bf16[256,256]{1,0:T(8,128)(2,1)S(1)} collective-permute-done((bf16[256,256]{1,0:T(8,128)(2,1)S(1)}, bf16[256,256]{1,0:T(8,128)(2,1)S(1)}, u32[]{:S(2)}, u32[]{:S(2)}) %collective-permute-start.7) | collective-permute-done | bytes 131104 | tf_op jit(solution)/shard_map/ppermute | solution.py:20
  42.3 0.0 copy-done.3
  42.3 0.8 %add_returned.1 = bf16[1024,512]{1,0:T(8,128)(2,1)S(1)} custom-call(s32[4,16]{1,0:T(4,128)S(1)} %bitcast.4, bf16[1024,256]{1,0:T(8,128)(2,1)S(1)} %get-tuple-element.29.dq_ref, f32[1024,256]{1,0:T(8,128)S(1)} %get-tuple-element.30.grad_ref, bf16[256,256]{1,0:T(8,128)(2,1)S(1)} %collective-permute-done.4.refs_0_, ...), custom_call_target="tpu_custom_call" | custom-call | tf_op jit(solution)/shard_map/add_returned/pallas_call | solution.py:264
  43.1 35.3 %all_to_all.5.in_ref = bf16[16,64,512]{2,1,0:T(8,128)(2,1)S(1)} all-to-all(bf16[16,64,512]{2,1,0:T(8,128)(2,1)S(1)} %bitcast.2), channel_id=1, replica_groups=mesh['ctx'=16,'head'=16] {'head'}, dimensions={0} | all-to-all | bytes 2097152 | tf_op jit(solution)/shard_map/all_to_all | solution.py:313
  78.4 1.0 %lay_out.1 = (bf16[64,4096]{1,0:T(8,128)(2,1)}, bf16[64,1024]{1,0:T(8,128)(2,1)}, bf16[64,1024]{1,0:T(8,128)(2,1)}) custom-call(bf16[16,64,512]{2,1,0:T(8,128)(2,1)S(1)} %all_to_all.5.in_ref), custom_call_target="tpu_custom_call" | custom-call | tf_op jit(solution)/shard_map/lay_out/pallas_call | solution.py:289
Async XLA Ops:
  0.6 8.8 %copy-start.1 = (bf16[1024,256]{1,0:T(8,128)(2,1)S(1)}, bf16[1024,256]{1,0:T(8,128)(2,1)}, u32[]{:S(2)}) copy-start(bf16[1024,256]{1,0:T(8,128)(2,1)} %g_ref.5) | copy-start | bytes 1572868
  0.6 8.8 %copy-start = (bf16[1024,256]{1,0:T(8,128)(2,1)S(1)}, bf16[1024,256]{1,0:T(8,128)(2,1)}, u32[]{:S(2)}) copy-start(bf16[1024,256]{1,0:T(8,128)(2,1)} %q_ref.5) | copy-start | bytes 1572868
  0.7 0.8 copy-start.2
  3.4 8.2 %collective-permute-start = (bf16[256,256]{1,0:T(8,128)(2,1)S(1)}, bf16[256,256]{1,0:T(8,128)(2,1)S(1)}, u32[]{:S(2)}, u32[]{:S(2)}) collective-permute-start(bf16[256,256]{1,0:T(8,128)(2,1)S(1)} %get-tuple-element.23), channel_id=1, source_target_pairs={{0,16},{16,32},{32,48},{48,64},{64,80},{80,96},{96,112},{112,128},... | collective-permute-start | bytes 393224 | tf_op jit(solution)/shard_map/ppermute | solution.py:20
  3.5 9.9 %collective-permute-start.1 = (bf16[256,256]{1,0:T(8,128)(2,1)S(1)}, bf16[256,256]{1,0:T(8,128)(2,1)S(1)}, u32[]{:S(2)}, u32[]{:S(2)}) collective-permute-start(bf16[256,256]{1,0:T(8,128)(2,1)S(1)} %get-tuple-element.24), channel_id=1, source_target_pairs={{0,32},{16,48},{32,64},{48,80},{64,96},{80,112},{96,128},{112,144}... | collective-permute-start | bytes 393224 | tf_op jit(solution)/shard_map/ppermute | solution.py:20
  6.8 7.7 %collective-permute-start.2 = (bf16[256,256]{1,0:T(8,128)(2,1)S(1)}, bf16[256,256]{1,0:T(8,128)(2,1)S(1)}, u32[]{:S(2)}, u32[]{:S(2)}) collective-permute-start(bf16[256,256]{1,0:T(8,128)(2,1)S(1)} %get-tuple-element.25), channel_id=1, source_target_pairs={{0,64},{16,80},{32,96},{48,112},{64,128},{80,144},{96,160},{112,17... | collective-permute-start | bytes 393224 | tf_op jit(solution)/shard_map/ppermute | solution.py:20
  9.1 7.7 %collective-permute-start.3 = (bf16[256,256]{1,0:T(8,128)(2,1)S(1)}, bf16[256,256]{1,0:T(8,128)(2,1)S(1)}, u32[]{:S(2)}, u32[]{:S(2)}) collective-permute-start(bf16[256,256]{1,0:T(8,128)(2,1)S(1)} %get-tuple-element.26), channel_id=1, source_target_pairs={{0,128},{16,144},{32,160},{48,176},{64,192},{80,208},{96,224},{112... | collective-permute-start | bytes 393224 | tf_op jit(solution)/shard_map/ppermute | solution.py:20
  24.6 11.4 %collective-permute-start.4 = (bf16[256,256]{1,0:T(8,128)(2,1)S(1)}, bf16[256,256]{1,0:T(8,128)(2,1)S(1)}, u32[]{:S(2)}, u32[]{:S(2)}) collective-permute-start(bf16[256,256]{1,0:T(8,128)(2,1)S(1)} %get-tuple-element.31), channel_id=1, source_target_pairs={{0,240},{16,0},{32,16},{48,32},{64,48},{80,64},{96,80},{112,96},{1... | collective-permute-start | bytes 393224 | tf_op jit(solution)/shard_map/ppermute | solution.py:20
  24.7 12.4 %collective-permute-start.5 = (bf16[256,256]{1,0:T(8,128)(2,1)S(1)}, bf16[256,256]{1,0:T(8,128)(2,1)S(1)}, u32[]{:S(2)}, u32[]{:S(2)}) collective-permute-start(bf16[256,256]{1,0:T(8,128)(2,1)S(1)} %get-tuple-element.32), channel_id=1, source_target_pairs={{0,224},{16,240},{32,0},{48,16},{64,32},{80,48},{96,64},{112,80},{... | collective-permute-start | bytes 393224 | tf_op jit(solution)/shard_map/ppermute | solution.py:20
  27.2 13.5 %collective-permute-start.6 = (bf16[256,256]{1,0:T(8,128)(2,1)S(1)}, bf16[256,256]{1,0:T(8,128)(2,1)S(1)}, u32[]{:S(2)}, u32[]{:S(2)}) collective-permute-start(bf16[256,256]{1,0:T(8,128)(2,1)S(1)} %get-tuple-element.33), channel_id=1, source_target_pairs={{0,192},{16,208},{32,224},{48,240},{64,0},{80,16},{96,32},{112,48}... | collective-permute-start | bytes 393224 | tf_op jit(solution)/shard_map/ppermute | solution.py:20
  31.6 10.7 %collective-permute-start.7 = (bf16[256,256]{1,0:T(8,128)(2,1)S(1)}, bf16[256,256]{1,0:T(8,128)(2,1)S(1)}, u32[]{:S(2)}, u32[]{:S(2)}) collective-permute-start(bf16[256,256]{1,0:T(8,128)(2,1)S(1)} %get-tuple-element.34), channel_id=1, source_target_pairs={{0,128},{16,144},{32,160},{48,176},{64,192},{80,208},{96,224},{112... | collective-permute-start | bytes 393224 | tf_op jit(solution)/shard_map/ppermute | solution.py:20
  33.2 9.1 %copy-start.3 = (s32[16,4]{0,1:T(4,128)S(1)}, s32[16,4]{0,1:T(4,128)}, u32[]{:S(2)}) copy-start(s32[16,4]{0,1:T(4,128)} %param.9) | copy-start | bytes 772

commit v3 on v2

--- a/solution.py
+++ b/solution.py
@@ -25,39 +25,40 @@
     return pl.multiple_of(index_ref[level_num, target] * BLK, BLK)
 
 
-def gather_blocks(block_index, keys, values, ctx_count, levels):
-    def body(index_ref, key_ref, value_ref, own_ref, *refs):
-        sends, sems = refs[:levels], refs[levels]
+def send_blocks(block_index, keys, values, ctx_count, levels):
+    def body(index_hbm, key_ref, value_ref, *refs):
+        sends, index_ref, sems = refs[:levels], refs[levels], refs[levels + 1]
+        fetch = pltpu.make_async_copy(index_hbm, index_ref, sems.at[2 * levels])
+        fetch.start()
         ctx_index = lax.axis_index("ctx")
         begin = pl.multiple_of(lax.axis_index("head") // 2 * HD, HD)
-        copies = []
-        for half, source in ((0, key_ref), (1, value_ref)):
-            columns = slice(half * HD, (half + 1) * HD)
-            for level_num in range(levels):
-                start = block_start(index_ref, ctx_index, level_num, ctx_count)
-                copies.append((source.at[pl.ds(start, BLK), pl.ds(begin, HD)], sends[level_num].at[:, columns]))
-            copies.append((source.at[:, pl.ds(begin, HD)], own_ref.at[:, columns]))
-        started = [
-            pltpu.make_async_copy(source, target, sems.at[number])
-            for number, (source, target) in enumerate(copies)
-        ]
-        for copy in started:
-            copy.start()
+        fetch.wait()
+        started = []
+        for level_num in range(levels):
+            start = block_start(index_ref, ctx_index, level_num, ctx_count)
+            for half, source in ((0, key_ref), (1, value_ref)):
+                started.append(
+                    pltpu.make_async_copy(
+                        source.at[pl.ds(start, BLK), pl.ds(begin, HD)],
+                        sends[level_num].at[:, half * HD : (half + 1) * HD],
+                        sems.at[2 * level_num + half],
+                    )
+                )
+                started[-1].start()
         for copy in started:
             copy.wait()
 
-    rows = keys.shape[0]
-    keys = pltpu.with_memory_space_constraint(keys, pltpu.HBM)
-    values = pltpu.with_memory_space_constraint(values, pltpu.HBM)
-    return pl.pallas_call(
-        body,
-        out_shape=(jax.ShapeDtypeStruct((rows, 2 * HD), keys.dtype),)
-        + (jax.ShapeDtypeStruct((BLK, 2 * HD), keys.dtype),) * levels,
-        in_specs=[SMEM, HBM, HBM],
-        out_specs=(VMEM,) * (levels + 1),
-        scratch_shapes=[pltpu.SemaphoreType.DMA((2 * levels + 2,))],
-        compiler_params=pltpu.CompilerParams(vmem_limit_bytes=4 << 20),
-        name="gather_blocks",
+    return pl.pallas_call(
+        body,
+        out_shape=(jax.ShapeDtypeStruct((BLK, 2 * HD), keys.dtype),) * levels,
+        in_specs=[HBM, HBM, HBM],
+        out_specs=(VMEM,) * levels,
+        scratch_shapes=[
+            pltpu.SMEM(block_index.shape, jnp.int32),
+            pltpu.SemaphoreType.DMA((2 * levels + 1,)),
+        ],
+        compiler_params=params(4),
+        name="send_blocks",
     )(block_index, keys, values)
 
 
@@ -81,77 +82,134 @@
     return [(part, number) for part in range(row_tiles) for number in range(part + 1)]
 
 
-def own_scores(queries, grad_out, own):
+def score_tile(key_tile, value_tile, query_t, grad_t, seen=None):
+    scores = dot(key_tile, query_t)
+    if seen is not None:
+        scores = jnp.where(seen, scores, NEG)
+    top = jnp.max(scores, axis=0, keepdims=True) * FACTOR
+    weights = jnp.exp2(scores * FACTOR - top)
+    grad_probs = dot(value_tile, grad_t)
+    total = jnp.sum(weights, axis=0, keepdims=True)
+    product = jnp.sum(weights * grad_probs, axis=0, keepdims=True)
+    return weights, grad_probs, (top, total, product)
+
+
+def own_scores(queries, grad_out, keys, values):
     rows, width = queries.shape
     row_tiles, heads = rows // BLK, width // HD
     places = pairs(row_tiles)
     total = heads * len(places)
 
-    def body(q_ref, g_ref, own_ref, weight_ref, prob_ref, stat_ref):
+    def body(q_ref, g_ref, key_ref, value_ref, own_ref, qt_ref, gt_ref, weight_ref, prob_ref, stat_ref, sems):
+        begin = pl.multiple_of(lax.axis_index("head") // 2 * HD, HD)
+        started = []
+        for half, source in ((0, key_ref), (1, value_ref)):
+            started.append(
+                pltpu.make_async_copy(
+                    source.at[:, pl.ds(begin, HD)], own_ref.at[:, half * HD : (half + 1) * HD], sems.at[half]
+                )
+            )
+            started[-1].start()
+        for head in range(heads):
+            columns = slice(head * HD, (head + 1) * HD)
+            for part in range(row_tiles):
+                qt_ref[columns, spot(part)] = q_ref[spot(part), columns].T
+                gt_ref[columns, spot(part)] = g_ref[spot(part), columns].T
+        for copy in started:
+            copy.wait()
         key_at = lax.broadcasted_iota(jnp.int32, (BLK, BLK), 0)
         causal = key_at <= lax.broadcasted_iota(jnp.int32, (BLK, BLK), 1)
         for head in range(heads):
             columns = slice(head * HD, (head + 1) * HD)
             for part in range(row_tiles):
-                query_t, grad_t = q_ref[spot(part), columns].T, g_ref[spot(part), columns].T
+                query_t, grad_t = qt_ref[columns, spot(part)], gt_ref[columns, spot(part)]
                 for number in range(part + 1):
                     place = head * len(places) + places.index((part, number))
-                    scores = dot(own_ref[spot(number), :HD], query_t)
-                    if number == part:
-                        scores = jnp.where(causal, scores, NEG)
-                    top = jnp.max(scores, axis=0, keepdims=True) * FACTOR
-                    weights = jnp.exp2(scores * FACTOR - top)
-                    grad_probs = dot(own_ref[spot(number), HD:], grad_t)
-                    weight_ref[place] = weights
-                    prob_ref[place] = grad_probs
-                    stat_ref[0, place : place + 1] = top
-                    stat_ref[1, place : place + 1] = jnp.sum(weights, axis=0, keepdims=True)
-                    stat_ref[2, place : place + 1] = jnp.sum(weights * grad_probs, axis=0, keepdims=True)
+                    weight_ref[place], prob_ref[place], found = score_tile(
+                        own_ref[spot(number), :HD],
+                        own_ref[spot(number), HD:],
+                        query_t,
+                        grad_t,
+                        causal if number == part else None,
+                    )
+                    for row, each in enumerate(found):
+                        stat_ref[row, place : place + 1] = each
 
     tiles = jax.ShapeDtypeStruct((total, BLK, BLK), jnp.float32)
-    return pl.pallas_call(
-        body,
-        out_shape=(tiles, tiles, jax.ShapeDtypeStruct((3, total, BLK), jnp.float32)),
+    turned = jax.ShapeDtypeStruct((width, rows), jnp.bfloat16)
+    return pl.pallas_call(
+        body,
+        out_shape=(
+            jax.ShapeDtypeStruct((rows, 2 * HD), keys.dtype),
+            turned,
+            turned,
+            tiles,
+            tiles,
+            jax.ShapeDtypeStruct((3, total, BLK), jnp.float32),
+        ),
+        in_specs=[VMEM, VMEM, HBM, HBM],
+        out_specs=(VMEM,) * 6,
+        scratch_shapes=[pltpu.SemaphoreType.DMA((2,))],
+        compiler_params=params(8),
+        cost_estimate=cost(2 * total, 2 << 20),
+        name="own_scores",
+    )(queries, grad_out, keys, values)
+
+
+def block_scores(queries_t, grad_t, block):
+    width, rows = queries_t.shape
+    row_tiles, heads = rows // BLK, width // HD
+
+    def body(qt_ref, gt_ref, block_ref, weight_ref, prob_ref, stat_ref):
+        for head in range(heads):
+            columns = slice(head * HD, (head + 1) * HD)
+            for part in range(row_tiles):
+                place = head * row_tiles + part
+                weight_ref[place], prob_ref[place], found = score_tile(
+                    block_ref[:, :HD], block_ref[:, HD:], qt_ref[columns, spot(part)], gt_ref[columns, spot(part)]
+                )
+                for row, each in enumerate(found):
+                    stat_ref[row, place : place + 1] = each
+
+    tiles = jax.ShapeDtypeStruct((heads * row_tiles, BLK, BLK), jnp.float32)
+    return pl.pallas_call(
+        body,
+        out_shape=(tiles, tiles, jax.ShapeDtypeStruct((3, heads * row_tiles, BLK), jnp.float32)),
         in_specs=[VMEM] * 3,
         out_specs=(VMEM,) * 3,
-        compiler_params=params(16),
-        cost_estimate=cost(2 * total, 2 << 20),
-        name="own_scores",
-    )(queries, grad_out, own)
-
-
-def partner_part(queries, grad_out, blocks, stats):
+        compiler_params=params(8),
+        cost_estimate=cost(2 * heads * row_tiles, 2 << 20),
+        name="block_scores",
+    )(queries_t, grad_t, block)
+
+
+def partner_part(queries, grad_out, own_stats, scored):
     rows, width = queries.shape
-    levels, row_tiles, heads = len(blocks), rows // BLK, width // HD
+    levels, row_tiles, heads = len(scored), rows // BLK, width // HD
     places = pairs(row_tiles)
     total = heads * len(places)
 
-    def body(q_ref, g_ref, stat_ref, *refs):
-        block_refs, part_refs = refs[:levels], refs[levels : 2 * levels]
-        low_ref, coef_ref, acc_ref = refs[2 * levels :]
+    def body(q_ref, g_ref, own_ref, *refs):
+        scored_refs = [refs[3 * level_num : 3 * level_num + 3] for level_num in range(levels)]
+        part_refs = refs[3 * levels : 4 * levels]
+        low_ref, coef_ref, acc_ref = refs[4 * levels :]
         ctx_index = lax.axis_index("ctx")
         live = [ctx_index >= 2**level_num for level_num in range(levels)]
-        for head in range(heads):
-            columns = slice(head * HD, (head + 1) * HD)
-            for part in range(row_tiles):
-                query, grad = q_ref[spot(part), columns], g_ref[spot(part), columns]
-                query_t, grad_t = query.T, grad.T
-                weights, grad_probs, tops, sums, products = [], [], [], [], []
+        ratio_of = {}
+        for head in range(heads):
+            for part in range(row_tiles):
+                at = head * row_tiles + part
+                tops, sums, products = [], [], []
                 for level_num in range(levels):
-                    scores = dot(block_refs[level_num][:, :HD], query_t)
-                    top = jnp.max(scores, axis=0, keepdims=True) * FACTOR
-                    weight = jnp.exp2(scores * FACTOR - jnp.where(live[level_num], top, -NEG))
-                    grad_prob = dot(block_refs[level_num][:, HD:], grad_t)
-                    weights.append(weight)
-                    grad_probs.append(grad_prob)
-                    tops.append(jnp.where(live[level_num], top, NEG))
-                    sums.append(jnp.sum(weight, axis=0, keepdims=True))
-                    products.append(jnp.sum(weight * grad_prob, axis=0, keepdims=True))
+                    stat_ref = scored_refs[level_num][2]
+                    tops.append(jnp.where(live[level_num], stat_ref[0, at : at + 1], NEG))
+                    sums.append(stat_ref[1, at : at + 1])
+                    products.append(stat_ref[2, at : at + 1])
                 first = head * len(places) + places.index((part, 0))
                 for place in range(first, first + part + 1):
-                    tops.append(stat_ref[0, place : place + 1])
-                    sums.append(stat_ref[1, place : place + 1])
-                    products.append(stat_ref[2, place : place + 1])
+                    tops.append(own_ref[0, place : place + 1])
+                    sums.append(own_ref[1, place : place + 1])
+                    products.append(own_ref[2, place : place + 1])
                 row_max = tops[0]
                 for top in tops[1:]:
                     row_max = jnp.maximum(row_max, top)
@@ -159,14 +217,20 @@
                 inverse = 1.0 / sum(each * ratio for each, ratio in zip(sums, ratios))
                 delta = sum(each * ratio for each, ratio in zip(products, ratios)) * inverse
                 for number in range(part + 1):
-                    place = first + number
-                    coef_ref[place : place + 1] = ratios[levels + number] * inverse
-                at = total + head * row_tiles + part
-                coef_ref[at : at + 1] = delta
-                for level_num in range(levels):
-                    probs = weights[level_num] * (ratios[level_num] * inverse)
-                    low = (probs * (grad_probs[level_num] - delta)).astype(jnp.bfloat16)
-                    low_ref[head * row_tiles + part, spot(level_num)] = low
+                    coef_ref[first + number : first + number + 1] = ratios[levels + number] * inverse
+                coef_ref[total + at : total + at + 1] = delta
+                ratio_of[at] = [ratio * inverse for ratio in ratios[:levels]], delta
+        for level_num in range(levels):
+            weight_ref, prob_ref, _ = scored_refs[level_num]
+            for head in range(heads):
+                columns = slice(head * HD, (head + 1) * HD)
+                for part in range(row_tiles):
+                    at = head * row_tiles + part
+                    ratios, delta = ratio_of[at]
+                    query, grad = q_ref[spot(part), columns], g_ref[spot(part), columns]
+                    probs = weight_ref[at] * ratios[level_num]
+                    low = (probs * (prob_ref[at] - delta)).astype(jnp.bfloat16)
+                    low_ref[at, spot(level_num)] = low
                     key_part, value_part = dot(low, query), dot(probs.astype(jnp.bfloat16), grad)
                     if head == 0 and part == 0:
                         acc_ref[spot(level_num), :HD] = key_part
@@ -188,13 +252,13 @@
             jax.ShapeDtypeStruct((heads * row_tiles, levels * BLK, BLK), jnp.bfloat16),
             jax.ShapeDtypeStruct((held, BLK), jnp.float32),
         ),
-        in_specs=[VMEM] * (3 + levels),
+        in_specs=[VMEM] * (3 + 3 * levels),
         out_specs=(VMEM,) * (2 + levels),
         scratch_shapes=[pltpu.VMEM((levels * BLK, 2 * HD), jnp.float32)],
-        compiler_params=params(16),
-        cost_estimate=cost(4 * heads * row_tiles * levels, 2 << 20),
+        compiler_params=params(8),
+        cost_estimate=cost(2 * heads * row_tiles * levels, 2 << 20),
         name="partner_part",
-    )(queries, grad_out, stats, *blocks)
+    )(queries, grad_out, own_stats, *[each for level in scored for each in level])
 
 
 def own_part(queries, grad_out, own, blocks, weights, grad_probs, low, coef):
@@ -240,7 +304,7 @@
         in_specs=[VMEM] * (7 + levels),
         out_specs=(VMEM,) * 2,
         scratch_shapes=[pltpu.VMEM((HD, rows + levels * BLK), jnp.bfloat16)],
-        compiler_params=params(16),
+        compiler_params=params(8),
         cost_estimate=cost(3 * total + heads * row_tiles * levels, 2 << 20),
         name="own_part",
     )(queries, grad_out, own, weights, grad_probs, low, coef, *blocks)
@@ -302,10 +366,12 @@
     levels = ctx_count.bit_length() - 1
     rows, width = queries.shape
     block_index = block_index.T
-    own, *sends = gather_blocks(block_index, keys, values, ctx_count, levels)
+    hbm = [pltpu.with_memory_space_constraint(each, pltpu.HBM) for each in (block_index, keys, values)]
+    sends = send_blocks(*hbm, ctx_count, levels)
     blocks = [rotate(sends[level_num], "ctx", 2**level_num) for level_num in range(levels)]
-    weights, grad_probs, stats = own_scores(queries, grad_out, own)
-    *parts, low, coef = partner_part(queries, grad_out, blocks, stats)
+    own, queries_t, grad_t, weights, grad_probs, stats = own_scores(queries, grad_out, *hbm[1:])
+    scored = [block_scores(queries_t, grad_t, block) for block in blocks]
+    *parts, low, coef = partner_part(queries, grad_out, stats, scored)
     returned = [rotate(parts[level_num], "ctx", -(2**level_num)) for level_num in range(levels)]
     dq_local, gradients = own_part(queries, grad_out, own, blocks, weights, grad_probs, low, coef)
     joined = add_returned(block_index, dq_local, gradients, returned, ctx_count)

time: 79.5 us -> 74.8 us (0.941)
  waiting for transfers between devices: 11.3 us -> 6.01 us
  blocking collectives: 35.3 us -> 36.3 us
    ppermute x8, waiting for transfers between devices: 11.3 us -> 6.01 us  [rotate(): lax.ppermute(value, axis, [(source, (source + steps) % count) for source...]
    pallas_call x2 -> x6, Pallas kernels: 4.1 us -> 8.97 us  [the longest x4 3.81 us: block_scores(): pl.pallas_call(body, out_shape=(tiles, tiles, jax.ShapeDtypeStruct((3, he...]
    pallas_call x1, Pallas kernels: 7.9 us -> 3.19 us  [partner_part(): pl.pallas_call(body, out_shape=(jax.ShapeDtypeStruct((BLK, 2 * HD), jnp.b...]
    all_to_all x1, blocking collectives: 35.3 us -> 36.3 us  [on_device(): lax.all_to_all(split, 'head', split_axis=0, concat_axis=0, tiled=True)]
  transfers between devices with their start and end apart: 8 -> 8, of which waited for: 6 -> 2; matrix products, arithmetic and copies ran while one was open for 0% -> 0% of each run, Pallas kernels for 6% -> 12%
where the time goes in v3:
time: 74.8 us; the launch traced here: 74.6 us
  blocking collectives  36.3 us (49%)
  Pallas kernels  16.8 us (22%)
  starting transfers between devices  14.8 us (20%)
  waiting for transfers between devices  6.01 us (8%)
  between operations  0.75 us (1%)
    all_to_all x1, blocking collectives, on_device(): lax.all_to_all(split, 'head', split_axis=0, concat_axis=0, tiled=True)  36.3 us
    ppermute x8, starting transfers between devices, rotate(): lax.ppermute(value, axis, [(source, (source + steps) % count) for source...  14.8 us
    ppermute x8, waiting for transfers between devices, rotate(): lax.ppermute(value, axis, [(source, (source + steps) % count) for source...  6.01 us
    pallas_call x4, Pallas kernels, block_scores(): pl.pallas_call(body, out_shape=(tiles, tiles, jax.ShapeDtypeStruct((3, he...  3.81 us
    pallas_call x1, Pallas kernels, partner_part(): pl.pallas_call(body, out_shape=(jax.ShapeDtypeStruct((BLK, 2 * HD), jnp.b...  3.19 us
    pallas_call x1, Pallas kernels, own_scores(): pl.pallas_call(body, out_shape=(jax.ShapeDtypeStruct((rows, 2 * HD), keys...  3.18 us
    pallas_call x1, Pallas kernels, own_part(): pl.pallas_call(body, out_shape=(jax.ShapeDtypeStruct(queries.shape, jnp.b...  2.84 us
    pallas_call x1, Pallas kernels, send_blocks(): pl.pallas_call(body, out_shape=(jax.ShapeDtypeStruct((BLK, 2 * HD), keys....  1.99 us
  transfers between devices with their start and end apart: 8, of which 2 were waited for; matrix products, arithmetic and copies ran while one was open for 0% of the time, Pallas kernels for 12%

profile of v3, /device:TPU:6, one launch (start us, length us, event | category | flops | bytes accessed | tf_op | source)
XLA Modules:
  0.0 74.6 jit_solution(1526355937927355140)
XLA Ops:
  0.6 0.0 copy-start
  0.6 0.0 copy-start.1
  0.6 2.0 %send_blocks.1 = (bf16[256,256]{1,0:T(8,128)(2,1)S(1)}, bf16[256,256]{1,0:T(8,128)(2,1)S(1)}, bf16[256,256]{1,0:T(8,128)(2,1)S(1)}, bf16[256,256]{1,0:T(8,128)(2,1)S(1)}) custom-call(s32[4,16]{1,0:T(4,128)} %bitcast.3, bf16[1024,1024]{1,0:T(8,128)(2,1)} %key_ref.3, bf16[1024,1024]{1,0:T(8,128)(2,1)} %value_ref.3), custom_call_target="tpu_custom_call" | custom-call | tf_op jit(solution)/shard_map/send_blocks/pallas_call | solution.py:51
  2.6 3.3 %collective-permute-start.3 = (bf16[256,256]{1,0:T(8,128)(2,1)S(1)}, bf16[256,256]{1,0:T(8,128)(2,1)S(1)}, u32[]{:S(2)}, u32[]{:S(2)}) collective-permute-start(bf16[256,256]{1,0:T(8,128)(2,1)S(1)} %get-tuple-element.51), channel_id=1, source_target_pairs={{0,128},{16,144},{32,160},{48,176},{64,192},{80,208},{96,224},{112... | collective-permute-start | bytes 393224 | tf_op jit(solution)/shard_map/ppermute | solution.py:20
  6.0 1.2 %collective-permute-start.2 = (bf16[256,256]{1,0:T(8,128)(2,1)S(1)}, bf16[256,256]{1,0:T(8,128)(2,1)S(1)}, u32[]{:S(2)}, u32[]{:S(2)}) collective-permute-start(bf16[256,256]{1,0:T(8,128)(2,1)S(1)} %get-tuple-element.47), channel_id=1, source_target_pairs={{0,64},{16,80},{32,96},{48,112},{64,128},{80,144},{96,160},{112,17... | collective-permute-start | bytes 393224 | tf_op jit(solution)/shard_map/ppermute | solution.py:20
  7.1 2.1 %collective-permute-start.1 = (bf16[256,256]{1,0:T(8,128)(2,1)S(1)}, bf16[256,256]{1,0:T(8,128)(2,1)S(1)}, u32[]{:S(2)}, u32[]{:S(2)}) collective-permute-start(bf16[256,256]{1,0:T(8,128)(2,1)S(1)} %get-tuple-element.43), channel_id=1, source_target_pairs={{0,32},{16,48},{32,64},{48,80},{64,96},{80,112},{96,128},{112,144}... | collective-permute-start | bytes 393224 | tf_op jit(solution)/shard_map/ppermute | solution.py:20
  9.2 0.0 collective-permute-start
  9.2 0.0 copy-done
  9.2 0.0 copy-done.1
  9.2 3.2 %own_scores.1 = (bf16[1024,256]{1,0:T(8,128)(2,1)S(1)}, bf16[256,1024]{1,0:T(8,128)(2,1)S(1)}, bf16[256,1024]{1,0:T(8,128)(2,1)S(1)}, f32[20,256,256]{2,1,0:T(8,...) custom-call(bf16[1024,256]{1,0:T(8,128)(2,1)S(1)} %copy-done, bf16[1024,256]{1,0:T(8,128)(2,1)S(1)} %copy-done.1, ...), custom_call_target="tpu_custom_call" | custom-call | flops 671088640 | bytes 2097152 | tf_op jit(solution)/shard_map/own_scores/pallas_call | solution.py:140
  12.4 0.0 collective-permute-done.3.block_ref.refs_3_
  12.4 1.0 %block_scores.7 = (f32[8,256,256]{2,1,0:T(8,128)S(1)}, f32[8,256,256]{2,1,0:T(8,128)S(1)}, f32[3,8,256]{2,1,0:T(8,128)S(1)}) custom-call(bf16[256,1024]{1,0:T(8,128)(2,1)S(1)} %get-tuple-element.37.qt_ref, bf16[256,1024]{1,0:T(8,128)(2,1)S(1)} %get-tuple-element.38.gt_ref, bf16[256,256]{1,0:T(8,128)(2,1)S(1)} %collective-permute-done.3.block_ref.refs_3_), custom_call_target="tpu_custom_call" | custom-call | flops 268435456 | bytes 2097152 | tf_op jit(solution)/shard_map/block_scores/pallas_call | solution.py:175
  13.4 0.0 collective-permute-done.2.block_ref.refs_2_
  13.4 1.0 %block_scores.6 = (f32[8,256,256]{2,1,0:T(8,128)S(1)}, f32[8,256,256]{2,1,0:T(8,128)S(1)}, f32[3,8,256]{2,1,0:T(8,128)S(1)}) custom-call(bf16[256,1024]{1,0:T(8,128)(2,1)S(1)} %get-tuple-element.37.qt_ref, bf16[256,1024]{1,0:T(8,128)(2,1)S(1)} %get-tuple-element.38.gt_ref, bf16[256,256]{1,0:T(8,128)(2,1)S(1)} %collective-permute-done.2.block_ref.refs_2_), custom_call_target="tpu_custom_call" | custom-call | flops 268435456 | bytes 2097152 | tf_op jit(solution)/shard_map/block_scores/pallas_call | solution.py:175
  14.3 0.0 collective-permute-done.1.block_ref.refs_1_
  14.3 1.0 %block_scores.5 = (f32[8,256,256]{2,1,0:T(8,128)S(1)}, f32[8,256,256]{2,1,0:T(8,128)S(1)}, f32[3,8,256]{2,1,0:T(8,128)S(1)}) custom-call(bf16[256,1024]{1,0:T(8,128)(2,1)S(1)} %get-tuple-element.37.qt_ref, bf16[256,1024]{1,0:T(8,128)(2,1)S(1)} %get-tuple-element.38.gt_ref, bf16[256,256]{1,0:T(8,128)(2,1)S(1)} %collective-permute-done.1.block_ref.refs_1_), custom_call_target="tpu_custom_call" | custom-call | flops 268435456 | bytes 2097152 | tf_op jit(solution)/shard_map/block_scores/pallas_call | solution.py:175
  15.3 0.0 collective-permute-done.block_ref.refs_0_
  15.3 0.9 %block_scores.4 = (f32[8,256,256]{2,1,0:T(8,128)S(1)}, f32[8,256,256]{2,1,0:T(8,128)S(1)}, f32[3,8,256]{2,1,0:T(8,128)S(1)}) custom-call(bf16[256,1024]{1,0:T(8,128)(2,1)S(1)} %get-tuple-element.37.qt_ref, bf16[256,1024]{1,0:T(8,128)(2,1)S(1)} %get-tuple-element.38.gt_ref, bf16[256,256]{1,0:T(8,128)(2,1)S(1)} %collective-permute-done.block_ref.refs_0_), custom_call_target="tpu_custom_call" | custom-call | flops 268435456 | bytes 2097152 | tf_op jit(solution)/shard_map/block_scores/pallas_call | solution.py:175
  16.3 3.2 %partner_part.1 = (bf16[256,256]{1,0:T(8,128)(2,1)S(1)}, bf16[256,256]{1,0:T(8,128)(2,1)S(1)}, bf16[256,256]{1,0:T(8,128)(2,1)S(1)}, bf16[256,256]{1,0:T(8,128)(...) custom-call(bf16[1024,256]{1,0:T(8,128)(2,1)S(1)} %copy-done, bf16[1024,256]{1,0:T(8,128)(2,1)S(1)} %copy-done.1, ...), custom_call_target="tpu_custom_call" | custom-call | flops 1073741824 | bytes 2097152 | tf_op jit(solution)/shard_map/partner_part/pallas_call | solution.py:248
  19.5 2.0 %collective-permute-start.4 = (bf16[256,256]{1,0:T(8,128)(2,1)S(1)}, bf16[256,256]{1,0:T(8,128)(2,1)S(1)}, u32[]{:S(2)}, u32[]{:S(2)}) collective-permute-start(bf16[256,256]{1,0:T(8,128)(2,1)S(1)} %get-tuple-element.59), channel_id=1, source_target_pairs={{0,240},{16,0},{32,16},{48,32},{64,48},{80,64},{96,80},{112,96},{1... | collective-permute-start | bytes 393224 | tf_op jit(solution)/shard_map/ppermute | solution.py:20
  21.5 0.4 collective-permute-start.5
  21.8 5.6 %collective-permute-start.6 = (bf16[256,256]{1,0:T(8,128)(2,1)S(1)}, bf16[256,256]{1,0:T(8,128)(2,1)S(1)}, u32[]{:S(2)}, u32[]{:S(2)}) collective-permute-start(bf16[256,256]{1,0:T(8,128)(2,1)S(1)} %get-tuple-element.61), channel_id=1, source_target_pairs={{0,192},{16,208},{32,224},{48,240},{64,0},{80,16},{96,32},{112,48}... | collective-permute-start | bytes 393224 | tf_op jit(solution)/shard_map/ppermute | solution.py:20
  27.4 0.3 collective-permute-start.7
  27.7 0.0 copy-start.2
  27.7 2.8 %own_part.1 = (bf16[1024,256]{1,0:T(8,128)(2,1)S(1)}, f32[1024,256]{1,0:T(8,128)S(1)}) custom-call(bf16[1024,256]{1,0:T(8,128)(2,1)S(1)} %copy-done, bf16[1024,256]{1,0:T(8,128)(2,1)S(1)} %copy-done.1, bf16[1024,256]{1,0:T(8,128)(2,1)S(1)} %get-tuple-element.33.own_ref, f32[20,256,256]{2,1,0:T(8,128)S(1)} %get-tuple-element.34.weight_ref, ...), custom_call_target="tpu_custom_call" | custom-call | flops 1543503872 | bytes 2097152 | tf_op jit(solution)/shard_map/own_part/pallas_call | solution.py:298
  30.5 0.0 collective-permute-done.4.refs_0_
  30.5 3.3 %collective-permute-done.5.refs_1_ = bf16[256,256]{1,0:T(8,128)(2,1)S(1)} collective-permute-done((bf16[256,256]{1,0:T(8,128)(2,1)S(1)}, bf16[256,256]{1,0:T(8,128)(2,1)S(1)}, u32[]{:S(2)}, u32[]{:S(2)}) %collective-permute-start.5) | collective-permute-done | bytes 131104 | tf_op jit(solution)/shard_map/ppermute | solution.py:20
  33.8 0.0 collective-permute-done.6.refs_2_
  33.8 2.7 %collective-permute-done.7.refs_3_ = bf16[256,256]{1,0:T(8,128)(2,1)S(1)} collective-permute-done((bf16[256,256]{1,0:T(8,128)(2,1)S(1)}, bf16[256,256]{1,0:T(8,128)(2,1)S(1)}, u32[]{:S(2)}, u32[]{:S(2)}) %collective-permute-start.7) | collective-permute-done | bytes 131104 | tf_op jit(solution)/shard_map/ppermute | solution.py:20
  36.5 0.0 copy-done.2
  36.5 0.8 %add_returned.1 = bf16[1024,512]{1,0:T(8,128)(2,1)S(1)} custom-call(s32[4,16]{1,0:T(4,128)S(1)} %bitcast.4, bf16[1024,256]{1,0:T(8,128)(2,1)S(1)} %get-tuple-element.57.dq_ref, f32[1024,256]{1,0:T(8,128)S(1)} %get-tuple-element.58.grad_ref, bf16[256,256]{1,0:T(8,128)(2,1)S(1)} %collective-permute-done.4.refs_0_, ...), custom_call_target="tpu_custom_call" | custom-call | tf_op jit(solution)/shard_map/add_returned/pallas_call | solution.py:328
  37.4 36.3 %all_to_all.5.in_ref = bf16[16,64,512]{2,1,0:T(8,128)(2,1)S(1)} all-to-all(bf16[16,64,512]{2,1,0:T(8,128)(2,1)S(1)} %bitcast.2), channel_id=1, replica_groups=mesh['ctx'=16,'head'=16] {'head'}, dimensions={0} | all-to-all | bytes 2097152 | tf_op jit(solution)/shard_map/all_to_all | solution.py:379
  73.6 1.0 %lay_out.1 = (bf16[64,4096]{1,0:T(8,128)(2,1)}, bf16[64,1024]{1,0:T(8,128)(2,1)}, bf16[64,1024]{1,0:T(8,128)(2,1)}) custom-call(bf16[16,64,512]{2,1,0:T(8,128)(2,1)S(1)} %all_to_all.5.in_ref), custom_call_target="tpu_custom_call" | custom-call | tf_op jit(solution)/shard_map/lay_out/pallas_call | solution.py:353
Async XLA Ops:
  0.6 8.6 %copy-start = (bf16[1024,256]{1,0:T(8,128)(2,1)S(1)}, bf16[1024,256]{1,0:T(8,128)(2,1)}, u32[]{:S(2)}) copy-start(bf16[1024,256]{1,0:T(8,128)(2,1)} %q_ref.5) | copy-start | bytes 1572868
  0.6 8.6 %copy-start.1 = (bf16[1024,256]{1,0:T(8,128)(2,1)S(1)}, bf16[1024,256]{1,0:T(8,128)(2,1)}, u32[]{:S(2)}) copy-start(bf16[1024,256]{1,0:T(8,128)(2,1)} %g_ref.5) | copy-start | bytes 1572868
  2.6 9.8 %collective-permute-start.3 = (bf16[256,256]{1,0:T(8,128)(2,1)S(1)}, bf16[256,256]{1,0:T(8,128)(2,1)S(1)}, u32[]{:S(2)}, u32[]{:S(2)}) collective-permute-start(bf16[256,256]{1,0:T(8,128)(2,1)S(1)} %get-tuple-element.51), channel_id=1, source_target_pairs={{0,128},{16,144},{32,160},{48,176},{64,192},{80,208},{96,224},{112... | collective-permute-start | bytes 393224 | tf_op jit(solution)/shard_map/ppermute | solution.py:20
  6.0 7.4 %collective-permute-start.2 = (bf16[256,256]{1,0:T(8,128)(2,1)S(1)}, bf16[256,256]{1,0:T(8,128)(2,1)S(1)}, u32[]{:S(2)}, u32[]{:S(2)}) collective-permute-start(bf16[256,256]{1,0:T(8,128)(2,1)S(1)} %get-tuple-element.47), channel_id=1, source_target_pairs={{0,64},{16,80},{32,96},{48,112},{64,128},{80,144},{96,160},{112,17... | collective-permute-start | bytes 393224 | tf_op jit(solution)/shard_map/ppermute | solution.py:20
  7.1 7.2 %collective-permute-start.1 = (bf16[256,256]{1,0:T(8,128)(2,1)S(1)}, bf16[256,256]{1,0:T(8,128)(2,1)S(1)}, u32[]{:S(2)}, u32[]{:S(2)}) collective-permute-start(bf16[256,256]{1,0:T(8,128)(2,1)S(1)} %get-tuple-element.43), channel_id=1, source_target_pairs={{0,32},{16,48},{32,64},{48,80},{64,96},{80,112},{96,128},{112,144}... | collective-permute-start | bytes 393224 | tf_op jit(solution)/shard_map/ppermute | solution.py:20
  9.2 6.1 %collective-permute-start = (bf16[256,256]{1,0:T(8,128)(2,1)S(1)}, bf16[256,256]{1,0:T(8,128)(2,1)S(1)}, u32[]{:S(2)}, u32[]{:S(2)}) collective-permute-start(bf16[256,256]{1,0:T(8,128)(2,1)S(1)} %get-tuple-element.39), channel_id=1, source_target_pairs={{0,16},{16,32},{32,48},{48,64},{64,80},{80,96},{96,112},{112,128},... | collective-permute-start | bytes 393224 | tf_op jit(solution)/shard_map/ppermute | solution.py:20
  19.5 11.1 %collective-permute-start.4 = (bf16[256,256]{1,0:T(8,128)(2,1)S(1)}, bf16[256,256]{1,0:T(8,128)(2,1)S(1)}, u32[]{:S(2)}, u32[]{:S(2)}) collective-permute-start(bf16[256,256]{1,0:T(8,128)(2,1)S(1)} %get-tuple-element.59), channel_id=1, source_target_pairs={{0,240},{16,0},{32,16},{48,32},{64,48},{80,64},{96,80},{112,96},{1... | collective-permute-start | bytes 393224 | tf_op jit(solution)/shard_map/ppermute | solution.py:20
  21.5 12.4 %collective-permute-start.5 = (bf16[256,256]{1,0:T(8,128)(2,1)S(1)}, bf16[256,256]{1,0:T(8,128)(2,1)S(1)}, u32[]{:S(2)}, u32[]{:S(2)}) collective-permute-start(bf16[256,256]{1,0:T(8,128)(2,1)S(1)} %get-tuple-element.60), channel_id=1, source_target_pairs={{0,224},{16,240},{32,0},{48,16},{64,32},{80,48},{96,64},{112,80},{... | collective-permute-start | bytes 393224 | tf_op jit(solution)/shard_map/ppermute | solution.py:20
  21.8 12.0 %collective-permute-start.6 = (bf16[256,256]{1,0:T(8,128)(2,1)S(1)}, bf16[256,256]{1,0:T(8,128)(2,1)S(1)}, u32[]{:S(2)}, u32[]{:S(2)}) collective-permute-start(bf16[256,256]{1,0:T(8,128)(2,1)S(1)} %get-tuple-element.61), channel_id=1, source_target_pairs={{0,192},{16,208},{32,224},{48,240},{64,0},{80,16},{96,32},{112,48}... | collective-permute-start | bytes 393224 | tf_op jit(solution)/shard_map/ppermute | solution.py:20
  27.4 9.2 %collective-permute-start.7 = (bf16[256,256]{1,0:T(8,128)(2,1)S(1)}, bf16[256,256]{1,0:T(8,128)(2,1)S(1)}, u32[]{:S(2)}, u32[]{:S(2)}) collective-permute-start(bf16[256,256]{1,0:T(8,128)(2,1)S(1)} %get-tuple-element.62), channel_id=1, source_target_pairs={{0,128},{16,144},{32,160},{48,176},{64,192},{80,208},{96,224},{112... | collective-permute-start | bytes 393224 | tf_op jit(solution)/shard_map/ppermute | solution.py:20
  27.7 8.9 %copy-start.2 = (s32[16,4]{0,1:T(4,128)S(1)}, s32[16,4]{0,1:T(4,128)}, u32[]{:S(2)}) copy-start(s32[16,4]{0,1:T(4,128)} %param.9) | copy-start | bytes 772

commit v4 on v3

--- a/solution.py
+++ b/solution.py
@@ -25,40 +25,35 @@
     return pl.multiple_of(index_ref[level_num, target] * BLK, BLK)
 
 
-def send_blocks(block_index, keys, values, ctx_count, levels):
-    def body(index_hbm, key_ref, value_ref, *refs):
+def gather_blocks(block_index, keys, values, ctx_count, levels):
+    def body(index_hbm, key_ref, value_ref, own_ref, *refs):
         sends, index_ref, sems = refs[:levels], refs[levels], refs[levels + 1]
-        fetch = pltpu.make_async_copy(index_hbm, index_ref, sems.at[2 * levels])
-        fetch.start()
+        begin = pl.multiple_of(lax.axis_index("head") // 2 * HD, HD)
+        started = [pltpu.make_async_copy(index_hbm, index_ref, sems.at[2])]
+        for half, source in ((0, key_ref), (1, value_ref)):
+            started.append(
+                pltpu.make_async_copy(
+                    source.at[:, pl.ds(begin, HD)], own_ref.at[:, half * HD : (half + 1) * HD], sems.at[half]
+                )
+            )
+        for copy in started:
+            copy.start()
+        for copy in started:
+            copy.wait()
         ctx_index = lax.axis_index("ctx")
-        begin = pl.multiple_of(lax.axis_index("head") // 2 * HD, HD)
-        fetch.wait()
-        started = []
         for level_num in range(levels):
             start = block_start(index_ref, ctx_index, level_num, ctx_count)
-            for half, source in ((0, key_ref), (1, value_ref)):
-                started.append(
-                    pltpu.make_async_copy(
-                        source.at[pl.ds(start, BLK), pl.ds(begin, HD)],
-                        sends[level_num].at[:, half * HD : (half + 1) * HD],
-                        sems.at[2 * level_num + half],
-                    )
-                )
-                started[-1].start()
-        for copy in started:
-            copy.wait()
-
-    return pl.pallas_call(
-        body,
-        out_shape=(jax.ShapeDtypeStruct((BLK, 2 * HD), keys.dtype),) * levels,
+            sends[level_num][...] = own_ref[pl.ds(start, BLK), :]
+
+    return pl.pallas_call(
+        body,
+        out_shape=(jax.ShapeDtypeStruct((keys.shape[0], 2 * HD), keys.dtype),)
+        + (jax.ShapeDtypeStruct((BLK, 2 * HD), keys.dtype),) * levels,
         in_specs=[HBM, HBM, HBM],
-        out_specs=(VMEM,) * levels,
-        scratch_shapes=[
-            pltpu.SMEM(block_index.shape, jnp.int32),
-            pltpu.SemaphoreType.DMA((2 * levels + 1,)),
-        ],
+        out_specs=(VMEM,) * (levels + 1),
+        scratch_shapes=[pltpu.SMEM(block_index.shape, jnp.int32), pltpu.SemaphoreType.DMA((3,))],
         compiler_params=params(4),
-        name="send_blocks",
+        name="gather_blocks",
     )(block_index, keys, values)
 
 
@@ -94,35 +89,21 @@
     return weights, grad_probs, (top, total, product)
 
 
-def own_scores(queries, grad_out, keys, values):
+def own_scores(queries, grad_out, own):
     rows, width = queries.shape
     row_tiles, heads = rows // BLK, width // HD
     places = pairs(row_tiles)
     total = heads * len(places)
 
-    def body(q_ref, g_ref, key_ref, value_ref, own_ref, qt_ref, gt_ref, weight_ref, prob_ref, stat_ref, sems):
-        begin = pl.multiple_of(lax.axis_index("head") // 2 * HD, HD)
-        started = []
-        for half, source in ((0, key_ref), (1, value_ref)):
-            started.append(
-                pltpu.make_async_copy(
-                    source.at[:, pl.ds(begin, HD)], own_ref.at[:, half * HD : (half + 1) * HD], sems.at[half]
-                )
-            )
-            started[-1].start()
-        for head in range(heads):
-            columns = slice(head * HD, (head + 1) * HD)
-            for part in range(row_tiles):
-                qt_ref[columns, spot(part)] = q_ref[spot(part), columns].T
-                gt_ref[columns, spot(part)] = g_ref[spot(part), columns].T
-        for copy in started:
-            copy.wait()
+    def body(q_ref, g_ref, own_ref, qt_ref, gt_ref, weight_ref, prob_ref, stat_ref):
         key_at = lax.broadcasted_iota(jnp.int32, (BLK, BLK), 0)
         causal = key_at <= lax.broadcasted_iota(jnp.int32, (BLK, BLK), 1)
         for head in range(heads):
             columns = slice(head * HD, (head + 1) * HD)
             for part in range(row_tiles):
-                query_t, grad_t = qt_ref[columns, spot(part)], gt_ref[columns, spot(part)]
+                query_t, grad_t = q_ref[spot(part), columns].T, g_ref[spot(part), columns].T
+                qt_ref[columns, spot(part)] = query_t
+                gt_ref[columns, spot(part)] = grad_t
                 for number in range(part + 1):
                     place = head * len(places) + places.index((part, number))
                     weight_ref[place], prob_ref[place], found = score_tile(
@@ -139,21 +120,13 @@
     turned = jax.ShapeDtypeStruct((width, rows), jnp.bfloat16)
     return pl.pallas_call(
         body,
-        out_shape=(
-            jax.ShapeDtypeStruct((rows, 2 * HD), keys.dtype),
-            turned,
-            turned,
-            tiles,
-            tiles,
-            jax.ShapeDtypeStruct((3, total, BLK), jnp.float32),
-        ),
-        in_specs=[VMEM, VMEM, HBM, HBM],
-        out_specs=(VMEM,) * 6,
-        scratch_shapes=[pltpu.SemaphoreType.DMA((2,))],
+        out_shape=(turned, turned, tiles, tiles, jax.ShapeDtypeStruct((3, total, BLK), jnp.float32)),
+        in_specs=[VMEM] * 3,
+        out_specs=(VMEM,) * 5,
         compiler_params=params(8),
         cost_estimate=cost(2 * total, 2 << 20),
         name="own_scores",
-    )(queries, grad_out, keys, values)
+    )(queries, grad_out, own)
 
 
 def block_scores(queries_t, grad_t, block):
@@ -192,7 +165,7 @@
     def body(q_ref, g_ref, own_ref, *refs):
         scored_refs = [refs[3 * level_num : 3 * level_num + 3] for level_num in range(levels)]
         part_refs = refs[3 * levels : 4 * levels]
-        low_ref, coef_ref, acc_ref = refs[4 * levels :]
+        low_ref, coef_ref, high_ref = refs[4 * levels :]
         ctx_index = lax.axis_index("ctx")
         live = [ctx_index >= 2**level_num for level_num in range(levels)]
         ratio_of = {}
@@ -222,39 +195,32 @@
                 ratio_of[at] = [ratio * inverse for ratio in ratios[:levels]], delta
         for level_num in range(levels):
             weight_ref, prob_ref, _ = scored_refs[level_num]
+            key_part = value_part = 0.0
             for head in range(heads):
                 columns = slice(head * HD, (head + 1) * HD)
                 for part in range(row_tiles):
                     at = head * row_tiles + part
                     ratios, delta = ratio_of[at]
-                    query, grad = q_ref[spot(part), columns], g_ref[spot(part), columns]
                     probs = weight_ref[at] * ratios[level_num]
                     low = (probs * (prob_ref[at] - delta)).astype(jnp.bfloat16)
-                    low_ref[at, spot(level_num)] = low
-                    key_part, value_part = dot(low, query), dot(probs.astype(jnp.bfloat16), grad)
-                    if head == 0 and part == 0:
-                        acc_ref[spot(level_num), :HD] = key_part
-                        acc_ref[spot(level_num), HD:] = value_part
-                    elif head == heads - 1 and part == row_tiles - 1:
-                        key_part = (acc_ref[spot(level_num), :HD] + key_part) * SCALE
-                        part_refs[level_num][:, :HD] = key_part.astype(jnp.bfloat16)
-                        value_part = acc_ref[spot(level_num), HD:] + value_part
-                        part_refs[level_num][:, HD:] = value_part.astype(jnp.bfloat16)
-                    else:
-                        acc_ref[spot(level_num), :HD] += key_part
-                        acc_ref[spot(level_num), HD:] += value_part
+                    low_ref[head, spot(level_num), spot(part)] = low
+                    high_ref[head, spot(level_num), spot(part)] = probs.astype(jnp.bfloat16)
+                key_part += dot(low_ref[head, spot(level_num)], q_ref[:, columns])
+                value_part += dot(high_ref[head, spot(level_num)], g_ref[:, columns])
+            part_refs[level_num][:, :HD] = (key_part * SCALE).astype(jnp.bfloat16)
+            part_refs[level_num][:, HD:] = value_part.astype(jnp.bfloat16)
 
     held = total + heads * row_tiles
     return pl.pallas_call(
         body,
         out_shape=(jax.ShapeDtypeStruct((BLK, 2 * HD), jnp.bfloat16),) * levels
         + (
-            jax.ShapeDtypeStruct((heads * row_tiles, levels * BLK, BLK), jnp.bfloat16),
+            jax.ShapeDtypeStruct((heads, levels * BLK, rows), jnp.bfloat16),
             jax.ShapeDtypeStruct((held, BLK), jnp.float32),
         ),
         in_specs=[VMEM] * (3 + 3 * levels),
         out_specs=(VMEM,) * (2 + levels),
-        scratch_shapes=[pltpu.VMEM((levels * BLK, 2 * HD), jnp.float32)],
+        scratch_shapes=[pltpu.VMEM((heads, levels * BLK, rows), jnp.bfloat16)],
         compiler_params=params(8),
         cost_estimate=cost(2 * heads * row_tiles * levels, 2 << 20),
         name="partner_part",
@@ -269,7 +235,7 @@
 
     def body(q_ref, g_ref, own_ref, weight_ref, prob_ref, low_ref, coef_ref, *refs):
         block_refs = refs[:levels]
-        dq_ref, grad_ref, kt_ref = refs[levels:]
+        joined_ref, grad_ref, kt_ref, own_low_ref, high_ref = refs[levels:]
         for number in range(row_tiles):
             kt_ref[:, spot(number)] = own_ref[spot(number), :HD].T
         for level_num in range(levels):
@@ -277,63 +243,64 @@
         for head in range(heads):
             columns = slice(head * HD, (head + 1) * HD)
             for part in range(row_tiles):
-                query, grad = q_ref[spot(part), columns], g_ref[spot(part), columns]
                 at = total + head * row_tiles + part
                 delta = coef_ref[at : at + 1]
-                dq_t = dot(kt_ref[:, rows:], low_ref[head * row_tiles + part])
                 for number in range(part + 1):
                     place = head * len(places) + places.index((part, number))
                     probs = weight_ref[place] * coef_ref[place : place + 1]
-                    scores_low = (probs * (prob_ref[place] - delta)).astype(jnp.bfloat16)
-                    key_part, value_part = dot(scores_low, query), dot(probs.astype(jnp.bfloat16), grad)
-                    dq_t += dot(kt_ref[:, spot(number)], scores_low)
-                    if head == 0 and number == part:
-                        grad_ref[spot(number), :HD] = key_part
-                        grad_ref[spot(number), HD:] = value_part
-                    else:
-                        grad_ref[spot(number), :HD] += key_part
-                        grad_ref[spot(number), HD:] += value_part
-                dq_ref[spot(part), columns] = (dq_t * SCALE).T.astype(jnp.bfloat16)
-
+                    low = (probs * (prob_ref[place] - delta)).astype(jnp.bfloat16)
+                    own_low_ref[head, spot(number), spot(part)] = low
+                    high_ref[head, spot(number), spot(part)] = probs.astype(jnp.bfloat16)
+                dq_t = dot(kt_ref[:, rows:], low_ref[head, :, spot(part)])
+                seen = slice(0, (part + 1) * BLK)
+                dq_t += dot(kt_ref[:, seen], own_low_ref[head, seen, spot(part)])
+                joined_ref[spot(part), columns] = (dq_t * SCALE).T.astype(jnp.bfloat16)
+        for number in range(row_tiles):
+            key_part = value_part = 0.0
+            seeing = slice(number * BLK, rows)
+            for head in range(heads):
+                columns = slice(head * HD, (head + 1) * HD)
+                key_part += dot(own_low_ref[head, spot(number), seeing], q_ref[seeing, columns])
+                value_part += dot(high_ref[head, spot(number), seeing], g_ref[seeing, columns])
+            grad_ref[spot(number), :HD] = key_part * SCALE
+            grad_ref[spot(number), HD:] = value_part
+
+    square = pltpu.VMEM((heads, rows, rows), jnp.bfloat16)
     return pl.pallas_call(
         body,
         out_shape=(
-            jax.ShapeDtypeStruct(queries.shape, jnp.bfloat16),
+            jax.ShapeDtypeStruct((rows, width + 2 * HD), jnp.bfloat16),
             jax.ShapeDtypeStruct((rows, 2 * HD), jnp.float32),
         ),
         in_specs=[VMEM] * (7 + levels),
         out_specs=(VMEM,) * 2,
-        scratch_shapes=[pltpu.VMEM((HD, rows + levels * BLK), jnp.bfloat16)],
-        compiler_params=params(8),
+        scratch_shapes=[pltpu.VMEM((HD, rows + levels * BLK), jnp.bfloat16), square, square],
+        compiler_params=params(14),
         cost_estimate=cost(3 * total + heads * row_tiles * levels, 2 << 20),
         name="own_part",
     )(queries, grad_out, own, weights, grad_probs, low, coef, *blocks)
 
 
-def add_returned(block_index, dq_local, gradients, returned, ctx_count):
-    levels, width = len(returned), dq_local.shape[1]
-
-    def body(index_ref, dq_ref, grad_ref, *refs):
+def add_returned(block_index, joined, gradients, returned, ctx_count):
+    levels, width = len(returned), joined.shape[1] - gradients.shape[1]
+
+    def body(index_ref, joined_ref, grad_ref, *refs):
         out_ref, total_ref = refs[levels:]
         ctx_index = lax.axis_index("ctx")
-        total_ref[:, :HD] = grad_ref[:, :HD] * SCALE
-        total_ref[:, HD:] = grad_ref[:, HD:]
         for level_num in range(levels):
             start = block_start(index_ref, ctx_index, level_num, ctx_count)
             total_ref[pl.ds(start, BLK), :] += refs[level_num][...].astype(jnp.float32)
-        out_ref[:, :width] = dq_ref[...]
         out_ref[:, width:] = total_ref[...].astype(jnp.bfloat16)
 
-    rows = dq_local.shape[0]
-    return pl.pallas_call(
-        body,
-        out_shape=jax.ShapeDtypeStruct((rows, width + 2 * HD), jnp.bfloat16),
+    return pl.pallas_call(
+        body,
+        out_shape=tuple(jax.ShapeDtypeStruct(each.shape, each.dtype) for each in (joined, gradients)),
         in_specs=[SMEM] + [VMEM] * (levels + 2),
-        out_specs=VMEM,
-        scratch_shapes=[pltpu.VMEM(gradients.shape, jnp.float32)],
+        out_specs=(VMEM, VMEM),
+        input_output_aliases={1: 0, 2: 1},
         compiler_params=params(6),
         name="add_returned",
-    )(block_index, dq_local, gradients, *returned)
+    )(block_index, joined, gradients, *returned)[0]
 
 
 def lay_out(gathered, width):
@@ -367,14 +334,14 @@
     rows, width = queries.shape
     block_index = block_index.T
     hbm = [pltpu.with_memory_space_constraint(each, pltpu.HBM) for each in (block_index, keys, values)]
-    sends = send_blocks(*hbm, ctx_count, levels)
+    own, *sends = gather_blocks(*hbm, ctx_count, levels)
     blocks = [rotate(sends[level_num], "ctx", 2**level_num) for level_num in range(levels)]
-    own, queries_t, grad_t, weights, grad_probs, stats = own_scores(queries, grad_out, *hbm[1:])
+    queries_t, grad_t, weights, grad_probs, stats = own_scores(queries, grad_out, own)
     scored = [block_scores(queries_t, grad_t, block) for block in blocks]
     *parts, low, coef = partner_part(queries, grad_out, stats, scored)
     returned = [rotate(parts[level_num], "ctx", -(2**level_num)) for level_num in range(levels)]
-    dq_local, gradients = own_part(queries, grad_out, own, blocks, weights, grad_probs, low, coef)
-    joined = add_returned(block_index, dq_local, gradients, returned, ctx_count)
+    joined, gradients = own_part(queries, grad_out, own, blocks, weights, grad_probs, low, coef)
+    joined = add_returned(block_index, joined, gradients, returned, ctx_count)
     split = joined.reshape(head_count, rows // head_count, joined.shape[1])
     gathered = lax.all_to_all(split, "head", split_axis=0, concat_axis=0, tiled=True)
     return tuple(lay_out(gathered, width))

time: 74.8 us -> 73 us (0.976)
  Pallas kernels: 16.8 us -> 14.7 us
  waiting for transfers between devices: 6.01 us -> 7.3 us
    pallas_call x4, Pallas kernels: 8.83 us -> 6.88 us  [the longest x1 2.78 us: own_part(): pl.pallas_call(body, out_shape=(jax.ShapeDtypeStruct((rows, width + 2 * H...]
    ppermute x8, waiting for transfers between devices: 6.01 us -> 7.3 us  [rotate(): lax.ppermute(value, axis, [(source, (source + steps) % count) for source...]
  transfers between devices with their start and end apart: 8 -> 8, of which waited for: 2 -> 3; matrix products, arithmetic and copies ran while one was open for 0% -> 0% of each run, Pallas kernels for 12% -> 11%
where the time goes in v4:
time: 73 us; the launch traced here: 72.8 us
  blocking collectives  35.6 us (49%)
  Pallas kernels  14.7 us (20%)
  starting transfers between devices  14.4 us (20%)
  waiting for transfers between devices  7.3 us (10%)
  between operations  0.74 us (1%)
    all_to_all x1, blocking collectives, on_device(): lax.all_to_all(split, 'head', split_axis=0, concat_axis=0, tiled=True)  35.6 us
    ppermute x8, starting transfers between devices, rotate(): lax.ppermute(value, axis, [(source, (source + steps) % count) for source...  14.4 us
    ppermute x8, waiting for transfers between devices, rotate(): lax.ppermute(value, axis, [(source, (source + steps) % count) for source...  7.3 us
    pallas_call x4, Pallas kernels, block_scores(): pl.pallas_call(body, out_shape=(tiles, tiles, jax.ShapeDtypeStruct((3, he...  3.79 us
    pallas_call x1, Pallas kernels, partner_part(): pl.pallas_call(body, out_shape=(jax.ShapeDtypeStruct((BLK, 2 * HD), jnp.b...  3.12 us
    pallas_call x1, Pallas kernels, own_part(): pl.pallas_call(body, out_shape=(jax.ShapeDtypeStruct((rows, width + 2 * H...  2.78 us
    pallas_call x1, Pallas kernels, own_scores(): pl.pallas_call(body, out_shape=(turned, turned, tiles, tiles, jax.ShapeDt...  2.18 us
  transfers between devices with their start and end apart: 8, of which 3 were waited for; matrix products, arithmetic and copies ran while one was open for 0% of the time, Pallas kernels for 11%

profile of v4, /device:TPU:6, one launch (start us, length us, event | category | flops | bytes accessed | tf_op | source)
XLA Modules:
  0.0 72.8 jit_solution(4683634693466326327)
XLA Ops:
  0.6 0.0 copy-start
  0.6 0.0 copy-start.1
  0.7 1.2 %gather_blocks.1 = (bf16[1024,256]{1,0:T(8,128)(2,1)S(1)}, bf16[256,256]{1,0:T(8,128)(2,1)S(1)}, bf16[256,256]{1,0:T(8,128)(2,1)S(1)}, bf16[256,256]{1,0:T(8,128)(2,1)S(1)}, bf16[256,256]{1,0:T(8,128)(2,1)S(1)}) custom-call(s32[4,16]{1,0:T(4,128)} %bitcast.3, bf16[1024,1024]{1,0:T(8,128)(2,1)} %key_ref.1, bf16[1024,1024]{1,0:T(8,128)(2,1)} %value_ref.1), custom_call_target="tpu_custom_call" | custom-call | tf_op jit(solution)/shard_map/gather_blocks/pallas_call | solution.py:48
  1.9 3.3 %collective-permute-start.3 = (bf16[256,256]{1,0:T(8,128)(2,1)S(1)}, bf16[256,256]{1,0:T(8,128)(2,1)S(1)}, u32[]{:S(2)}, u32[]{:S(2)}) collective-permute-start(bf16[256,256]{1,0:T(8,128)(2,1)S(1)} %get-tuple-element.52), channel_id=1, source_target_pairs={{0,128},{16,144},{32,160},{48,176},{64,192},{80,208},{96,224},{112... | collective-permute-start | bytes 393224 | tf_op jit(solution)/shard_map/ppermute | solution.py:20
  5.1 1.2 %collective-permute-start.2 = (bf16[256,256]{1,0:T(8,128)(2,1)S(1)}, bf16[256,256]{1,0:T(8,128)(2,1)S(1)}, u32[]{:S(2)}, u32[]{:S(2)}) collective-permute-start(bf16[256,256]{1,0:T(8,128)(2,1)S(1)} %get-tuple-element.48), channel_id=1, source_target_pairs={{0,64},{16,80},{32,96},{48,112},{64,128},{80,144},{96,160},{112,17... | collective-permute-start | bytes 393224 | tf_op jit(solution)/shard_map/ppermute | solution.py:20
  6.3 2.1 %collective-permute-start.1 = (bf16[256,256]{1,0:T(8,128)(2,1)S(1)}, bf16[256,256]{1,0:T(8,128)(2,1)S(1)}, u32[]{:S(2)}, u32[]{:S(2)}) collective-permute-start(bf16[256,256]{1,0:T(8,128)(2,1)S(1)} %get-tuple-element.44), channel_id=1, source_target_pairs={{0,32},{16,48},{32,64},{48,80},{64,96},{80,112},{96,128},{112,144}... | collective-permute-start | bytes 393224 | tf_op jit(solution)/shard_map/ppermute | solution.py:20
  8.4 0.0 collective-permute-start
  8.4 0.0 copy-done
  8.4 0.0 copy-done.1
  8.4 2.2 %own_scores.1 = (bf16[256,1024]{1,0:T(8,128)(2,1)S(1)}, bf16[256,1024]{1,0:T(8,128)(2,1)S(1)}, f32[20,256,256]{2,1,0:T(8,128)S(1)}, f32[20,256,256]{2,1,0:T(8,128)S(1)}, f32[3,20,256]{2,1,0:T(8,128)S(1)}) custom-call(bf16[1024,256]{1,0:T(8,128)(2,1)S(1)} %copy-done, bf16[1024,256]{1,0:T(8,128)(2,1)S(1)} %copy-done.1, ...), custom_call_target="tpu_custom_call" | custom-call | flops 671088640 | bytes 2097152 | tf_op jit(solution)/shard_map/own_scores/pallas_call | solution.py:121
  10.6 0.0 collective-permute-done.3.block_ref.refs_3_
  10.6 0.9 %block_scores.7 = (f32[8,256,256]{2,1,0:T(8,128)S(1)}, f32[8,256,256]{2,1,0:T(8,128)S(1)}, f32[3,8,256]{2,1,0:T(8,128)S(1)}) custom-call(bf16[256,1024]{1,0:T(8,128)(2,1)S(1)} %get-tuple-element.38.qt_ref, bf16[256,1024]{1,0:T(8,128)(2,1)S(1)} %get-tuple-element.39.gt_ref, bf16[256,256]{1,0:T(8,128)(2,1)S(1)} %collective-permute-done.3.block_ref.refs_3_), custom_call_target="tpu_custom_call" | custom-call | flops 268435456 | bytes 2097152 | tf_op jit(solution)/shard_map/block_scores/pallas_call | solution.py:148
  11.6 0.0 collective-permute-done.2.block_ref.refs_2_
  11.6 1.0 %block_scores.6 = (f32[8,256,256]{2,1,0:T(8,128)S(1)}, f32[8,256,256]{2,1,0:T(8,128)S(1)}, f32[3,8,256]{2,1,0:T(8,128)S(1)}) custom-call(bf16[256,1024]{1,0:T(8,128)(2,1)S(1)} %get-tuple-element.38.qt_ref, bf16[256,1024]{1,0:T(8,128)(2,1)S(1)} %get-tuple-element.39.gt_ref, bf16[256,256]{1,0:T(8,128)(2,1)S(1)} %collective-permute-done.2.block_ref.refs_2_), custom_call_target="tpu_custom_call" | custom-call | flops 268435456 | bytes 2097152 | tf_op jit(solution)/shard_map/block_scores/pallas_call | solution.py:148
  12.6 1.0 %collective-permute-done.1.block_ref.refs_1_ = bf16[256,256]{1,0:T(8,128)(2,1)S(1)} collective-permute-done((bf16[256,256]{1,0:T(8,128)(2,1)S(1)}, bf16[256,256]{1,0:T(8,128)(2,1)S(1)}, u32[]{:S(2)}, u32[]{:S(2)}) %collective-permute-start.1) | collective-permute-done | bytes 131104 | tf_op jit(solution)/shard_map/ppermute | solution.py:20
  13.6 1.0 %block_scores.5 = (f32[8,256,256]{2,1,0:T(8,128)S(1)}, f32[8,256,256]{2,1,0:T(8,128)S(1)}, f32[3,8,256]{2,1,0:T(8,128)S(1)}) custom-call(bf16[256,1024]{1,0:T(8,128)(2,1)S(1)} %get-tuple-element.38.qt_ref, bf16[256,1024]{1,0:T(8,128)(2,1)S(1)} %get-tuple-element.39.gt_ref, bf16[256,256]{1,0:T(8,128)(2,1)S(1)} %collective-permute-done.1.block_ref.refs_1_), custom_call_target="tpu_custom_call" | custom-call | flops 268435456 | bytes 2097152 | tf_op jit(solution)/shard_map/block_scores/pallas_call | solution.py:148
  14.5 0.0 collective-permute-done.block_ref.refs_0_
  14.5 0.9 %block_scores.4 = (f32[8,256,256]{2,1,0:T(8,128)S(1)}, f32[8,256,256]{2,1,0:T(8,128)S(1)}, f32[3,8,256]{2,1,0:T(8,128)S(1)}) custom-call(bf16[256,1024]{1,0:T(8,128)(2,1)S(1)} %get-tuple-element.38.qt_ref, bf16[256,1024]{1,0:T(8,128)(2,1)S(1)} %get-tuple-element.39.gt_ref, bf16[256,256]{1,0:T(8,128)(2,1)S(1)} %collective-permute-done.block_ref.refs_0_), custom_call_target="tpu_custom_call" | custom-call | flops 268435456 | bytes 2097152 | tf_op jit(solution)/shard_map/block_scores/pallas_call | solution.py:148
  15.5 3.1 %partner_part.1 = (bf16[256,256]{1,0:T(8,128)(2,1)S(1)}, bf16[256,256]{1,0:T(8,128)(2,1)S(1)}, bf16[256,256]{1,0:T(8,128)(2,1)S(1)}, bf16[256,256]{1,0:T(8,128)(...) custom-call(bf16[1024,256]{1,0:T(8,128)(2,1)S(1)} %copy-done, bf16[1024,256]{1,0:T(8,128)(2,1)S(1)} %copy-done.1, ...), custom_call_target="tpu_custom_call" | custom-call | flops 1073741824 | bytes 2097152 | tf_op jit(solution)/shard_map/partner_part/pallas_call | solution.py:214
  18.6 1.0 %collective-permute-start.4 = (bf16[256,256]{1,0:T(8,128)(2,1)S(1)}, bf16[256,256]{1,0:T(8,128)(2,1)S(1)}, u32[]{:S(2)}, u32[]{:S(2)}) collective-permute-start(bf16[256,256]{1,0:T(8,128)(2,1)S(1)} %get-tuple-element.60), channel_id=1, source_target_pairs={{0,240},{16,0},{32,16},{48,32},{64,48},{80,64},{96,80},{112,96},{1... | collective-permute-start | bytes 393224 | tf_op jit(solution)/shard_map/ppermute | solution.py:20
  19.6 1.3 %collective-permute-start.5 = (bf16[256,256]{1,0:T(8,128)(2,1)S(1)}, bf16[256,256]{1,0:T(8,128)(2,1)S(1)}, u32[]{:S(2)}, u32[]{:S(2)}) collective-permute-start(bf16[256,256]{1,0:T(8,128)(2,1)S(1)} %get-tuple-element.61), channel_id=1, source_target_pairs={{0,224},{16,240},{32,0},{48,16},{64,32},{80,48},{96,64},{112,80},{... | collective-permute-start | bytes 393224 | tf_op jit(solution)/shard_map/ppermute | solution.py:20
  20.9 4.6 %collective-permute-start.6 = (bf16[256,256]{1,0:T(8,128)(2,1)S(1)}, bf16[256,256]{1,0:T(8,128)(2,1)S(1)}, u32[]{:S(2)}, u32[]{:S(2)}) collective-permute-start(bf16[256,256]{1,0:T(8,128)(2,1)S(1)} %get-tuple-element.62), channel_id=1, source_target_pairs={{0,192},{16,208},{32,224},{48,240},{64,0},{80,16},{96,32},{112,48}... | collective-permute-start | bytes 393224 | tf_op jit(solution)/shard_map/ppermute | solution.py:20
  25.5 0.9 %collective-permute-start.7 = (bf16[256,256]{1,0:T(8,128)(2,1)S(1)}, bf16[256,256]{1,0:T(8,128)(2,1)S(1)}, u32[]{:S(2)}, u32[]{:S(2)}) collective-permute-start(bf16[256,256]{1,0:T(8,128)(2,1)S(1)} %get-tuple-element.63), channel_id=1, source_target_pairs={{0,128},{16,144},{32,160},{48,176},{64,192},{80,208},{96,224},{112... | collective-permute-start | bytes 393224 | tf_op jit(solution)/shard_map/ppermute | solution.py:20
  26.4 0.0 copy-start.2
  26.4 2.8 %own_part.1 = (bf16[1024,512]{1,0:T(8,128)(2,1)S(1)}, f32[1024,256]{1,0:T(8,128)S(1)}) custom-call(bf16[1024,256]{1,0:T(8,128)(2,1)S(1)} %copy-done, bf16[1024,256]{1,0:T(8,128)(2,1)S(1)} %copy-done.1, bf16[1024,256]{1,0:T(8,128)(2,1)S(1)} %get-tuple-element.34.own_ref, f32[20,256,256]{2,1,0:T(8,128)S(1)} %get-tuple-element.35.weight_ref, ...), custom_call_target="tpu_custom_call" | custom-call | flops 1543503872 | bytes 2097152 | tf_op jit(solution)/shard_map/own_part/pallas_call | solution.py:269
  29.2 0.0 collective-permute-done.4.refs_0_
  29.2 3.6 %collective-permute-done.5.refs_1_ = bf16[256,256]{1,0:T(8,128)(2,1)S(1)} collective-permute-done((bf16[256,256]{1,0:T(8,128)(2,1)S(1)}, bf16[256,256]{1,0:T(8,128)(2,1)S(1)}, u32[]{:S(2)}, u32[]{:S(2)}) %collective-permute-start.5) | collective-permute-done | bytes 131104 | tf_op jit(solution)/shard_map/ppermute | solution.py:20
  32.8 0.0 collective-permute-done.6.refs_2_
  32.8 2.7 %collective-permute-done.7.refs_3_ = bf16[256,256]{1,0:T(8,128)(2,1)S(1)} collective-permute-done((bf16[256,256]{1,0:T(8,128)(2,1)S(1)}, bf16[256,256]{1,0:T(8,128)(2,1)S(1)}, u32[]{:S(2)}, u32[]{:S(2)}) %collective-permute-start.7) | collective-permute-done | bytes 131104 | tf_op jit(solution)/shard_map/ppermute | solution.py:20
  35.5 0.0 copy-done.2
  35.5 0.7 add_returned.1
  36.2 35.6 %all_to_all.5.in_ref = bf16[16,64,512]{2,1,0:T(8,128)(2,1)S(1)} all-to-all(bf16[16,64,512]{2,1,0:T(8,128)(2,1)S(1)} %bitcast.2), channel_id=1, replica_groups=mesh['ctx'=16,'head'=16] {'head'}, dimensions={0} | all-to-all | bytes 2097152 | tf_op jit(solution)/shard_map/all_to_all | solution.py:346
  71.9 1.0 %lay_out.1 = (bf16[64,4096]{1,0:T(8,128)(2,1)}, bf16[64,1024]{1,0:T(8,128)(2,1)}, bf16[64,1024]{1,0:T(8,128)(2,1)}) custom-call(bf16[16,64,512]{2,1,0:T(8,128)(2,1)S(1)} %all_to_all.5.in_ref), custom_call_target="tpu_custom_call" | custom-call | tf_op jit(solution)/shard_map/lay_out/pallas_call | solution.py:320
Async XLA Ops:
  0.6 7.8 %copy-start = (bf16[1024,256]{1,0:T(8,128)(2,1)S(1)}, bf16[1024,256]{1,0:T(8,128)(2,1)}, u32[]{:S(2)}) copy-start(bf16[1024,256]{1,0:T(8,128)(2,1)} %q_ref.5) | copy-start | bytes 1572868
  0.6 7.8 %copy-start.1 = (bf16[1024,256]{1,0:T(8,128)(2,1)S(1)}, bf16[1024,256]{1,0:T(8,128)(2,1)}, u32[]{:S(2)}) copy-start(bf16[1024,256]{1,0:T(8,128)(2,1)} %g_ref.5) | copy-start | bytes 1572868
  1.9 8.8 %collective-permute-start.3 = (bf16[256,256]{1,0:T(8,128)(2,1)S(1)}, bf16[256,256]{1,0:T(8,128)(2,1)S(1)}, u32[]{:S(2)}, u32[]{:S(2)}) collective-permute-start(bf16[256,256]{1,0:T(8,128)(2,1)S(1)} %get-tuple-element.52), channel_id=1, source_target_pairs={{0,128},{16,144},{32,160},{48,176},{64,192},{80,208},{96,224},{112... | collective-permute-start | bytes 393224 | tf_op jit(solution)/shard_map/ppermute | solution.py:20
  5.1 6.5 %collective-permute-start.2 = (bf16[256,256]{1,0:T(8,128)(2,1)S(1)}, bf16[256,256]{1,0:T(8,128)(2,1)S(1)}, u32[]{:S(2)}, u32[]{:S(2)}) collective-permute-start(bf16[256,256]{1,0:T(8,128)(2,1)S(1)} %get-tuple-element.48), channel_id=1, source_target_pairs={{0,64},{16,80},{32,96},{48,112},{64,128},{80,144},{96,160},{112,17... | collective-permute-start | bytes 393224 | tf_op jit(solution)/shard_map/ppermute | solution.py:20
  6.3 7.2 %collective-permute-start.1 = (bf16[256,256]{1,0:T(8,128)(2,1)S(1)}, bf16[256,256]{1,0:T(8,128)(2,1)S(1)}, u32[]{:S(2)}, u32[]{:S(2)}) collective-permute-start(bf16[256,256]{1,0:T(8,128)(2,1)S(1)} %get-tuple-element.44), channel_id=1, source_target_pairs={{0,32},{16,48},{32,64},{48,80},{64,96},{80,112},{96,128},{112,144}... | collective-permute-start | bytes 393224 | tf_op jit(solution)/shard_map/ppermute | solution.py:20
  8.4 6.1 %collective-permute-start = (bf16[256,256]{1,0:T(8,128)(2,1)S(1)}, bf16[256,256]{1,0:T(8,128)(2,1)S(1)}, u32[]{:S(2)}, u32[]{:S(2)}) collective-permute-start(bf16[256,256]{1,0:T(8,128)(2,1)S(1)} %get-tuple-element.40), channel_id=1, source_target_pairs={{0,16},{16,32},{32,48},{48,64},{64,80},{80,96},{96,112},{112,128},... | collective-permute-start | bytes 393224 | tf_op jit(solution)/shard_map/ppermute | solution.py:20
  18.6 10.6 %collective-permute-start.4 = (bf16[256,256]{1,0:T(8,128)(2,1)S(1)}, bf16[256,256]{1,0:T(8,128)(2,1)S(1)}, u32[]{:S(2)}, u32[]{:S(2)}) collective-permute-start(bf16[256,256]{1,0:T(8,128)(2,1)S(1)} %get-tuple-element.60), channel_id=1, source_target_pairs={{0,240},{16,0},{32,16},{48,32},{64,48},{80,64},{96,80},{112,96},{1... | collective-permute-start | bytes 393224 | tf_op jit(solution)/shard_map/ppermute | solution.py:20
  19.6 13.2 %collective-permute-start.5 = (bf16[256,256]{1,0:T(8,128)(2,1)S(1)}, bf16[256,256]{1,0:T(8,128)(2,1)S(1)}, u32[]{:S(2)}, u32[]{:S(2)}) collective-permute-start(bf16[256,256]{1,0:T(8,128)(2,1)S(1)} %get-tuple-element.61), channel_id=1, source_target_pairs={{0,224},{16,240},{32,0},{48,16},{64,32},{80,48},{96,64},{112,80},{... | collective-permute-start | bytes 393224 | tf_op jit(solution)/shard_map/ppermute | solution.py:20
  20.9 11.9 %collective-permute-start.6 = (bf16[256,256]{1,0:T(8,128)(2,1)S(1)}, bf16[256,256]{1,0:T(8,128)(2,1)S(1)}, u32[]{:S(2)}, u32[]{:S(2)}) collective-permute-start(bf16[256,256]{1,0:T(8,128)(2,1)S(1)} %get-tuple-element.62), channel_id=1, source_target_pairs={{0,192},{16,208},{32,224},{48,240},{64,0},{80,16},{96,32},{112,48}... | collective-permute-start | bytes 393224 | tf_op jit(solution)/shard_map/ppermute | solution.py:20
  25.5 10.0 %collective-permute-start.7 = (bf16[256,256]{1,0:T(8,128)(2,1)S(1)}, bf16[256,256]{1,0:T(8,128)(2,1)S(1)}, u32[]{:S(2)}, u32[]{:S(2)}) collective-permute-start(bf16[256,256]{1,0:T(8,128)(2,1)S(1)} %get-tuple-element.63), channel_id=1, source_target_pairs={{0,128},{16,144},{32,160},{48,176},{64,192},{80,208},{96,224},{112... | collective-permute-start | bytes 393224 | tf_op jit(solution)/shard_map/ppermute | solution.py:20
  26.4 9.1 %copy-start.2 = (s32[16,4]{0,1:T(4,128)S(1)}, s32[16,4]{0,1:T(4,128)}, u32[]{:S(2)}) copy-start(s32[16,4]{0,1:T(4,128)} %param.9) | copy-start | bytes 772

commit v5 on v4

--- a/solution.py
+++ b/solution.py
@@ -18,6 +18,10 @@
 def rotate(value, axis, steps):
     count = lax.axis_size(axis)
     return lax.ppermute(value, axis, [(source, (source + steps) % count) for source in range(count)])
+
+
+def swap(value, axis):
+    return lax.ppermute(value, axis, [(source, source ^ 1) for source in range(lax.axis_size(axis))])
 
 
 def block_start(index_ref, ctx_index, level_num, ctx_count):
@@ -95,7 +99,8 @@
     places = pairs(row_tiles)
     total = heads * len(places)
 
-    def body(q_ref, g_ref, own_ref, qt_ref, gt_ref, weight_ref, prob_ref, stat_ref):
+    def body(q_ref, g_ref, own_ref, both_ref, qt_ref, gt_ref, weight_ref, prob_ref, stat_ref):
+        both_ref[0], both_ref[1] = q_ref[...], g_ref[...]
         key_at = lax.broadcasted_iota(jnp.int32, (BLK, BLK), 0)
         causal = key_at <= lax.broadcasted_iota(jnp.int32, (BLK, BLK), 1)
         for head in range(heads):
@@ -120,9 +125,16 @@
     turned = jax.ShapeDtypeStruct((width, rows), jnp.bfloat16)
     return pl.pallas_call(
         body,
-        out_shape=(turned, turned, tiles, tiles, jax.ShapeDtypeStruct((3, total, BLK), jnp.float32)),
+        out_shape=(
+            jax.ShapeDtypeStruct((2, rows, width), jnp.bfloat16),
+            turned,
+            turned,
+            tiles,
+            tiles,
+            jax.ShapeDtypeStruct((3, total, BLK), jnp.float32),
+        ),
         in_specs=[VMEM] * 3,
-        out_specs=(VMEM,) * 5,
+        out_specs=(VMEM,) * 6,
         compiler_params=params(8),
         cost_estimate=cost(2 * total, 2 << 20),
         name="own_scores",
@@ -156,16 +168,21 @@
     )(queries_t, grad_t, block)
 
 
-def partner_part(queries, grad_out, own_stats, scored):
-    rows, width = queries.shape
+def kinds():
+    keep = lax.axis_index("head") % 2
+    scales = [jnp.where(kind == 0, SCALE, 1.0) for kind in (keep, 1 - keep)]
+    return keep, 1 - keep, scales[0], scales[1]
+
+
+def partner_part(both, own_stats, scored):
+    _, rows, width = both.shape
     levels, row_tiles, heads = len(scored), rows // BLK, width // HD
     places = pairs(row_tiles)
     total = heads * len(places)
 
-    def body(q_ref, g_ref, own_ref, *refs):
+    def body(both_ref, own_ref, *refs):
         scored_refs = [refs[3 * level_num : 3 * level_num + 3] for level_num in range(levels)]
-        part_refs = refs[3 * levels : 4 * levels]
-        low_ref, coef_ref, high_ref = refs[4 * levels :]
+        send_ref, held_ref, coef_ref = refs[3 * levels :]
         ctx_index = lax.axis_index("ctx")
         live = [ctx_index >= 2**level_num for level_num in range(levels)]
         ratio_of = {}
@@ -193,49 +210,53 @@
                     coef_ref[first + number : first + number + 1] = ratios[levels + number] * inverse
                 coef_ref[total + at : total + at + 1] = delta
                 ratio_of[at] = [ratio * inverse for ratio in ratios[:levels]], delta
+        _, send, _, scale = kinds()
         for level_num in range(levels):
             weight_ref, prob_ref, _ = scored_refs[level_num]
-            key_part = value_part = 0.0
+            sent = 0.0
             for head in range(heads):
-                columns = slice(head * HD, (head + 1) * HD)
                 for part in range(row_tiles):
                     at = head * row_tiles + part
                     ratios, delta = ratio_of[at]
                     probs = weight_ref[at] * ratios[level_num]
                     low = (probs * (prob_ref[at] - delta)).astype(jnp.bfloat16)
-                    low_ref[head, spot(level_num), spot(part)] = low
-                    high_ref[head, spot(level_num), spot(part)] = probs.astype(jnp.bfloat16)
-                key_part += dot(low_ref[head, spot(level_num)], q_ref[:, columns])
-                value_part += dot(high_ref[head, spot(level_num)], g_ref[:, columns])
-            part_refs[level_num][:, :HD] = (key_part * SCALE).astype(jnp.bfloat16)
-            part_refs[level_num][:, HD:] = value_part.astype(jnp.bfloat16)
-
-    held = total + heads * row_tiles
-    return pl.pallas_call(
-        body,
-        out_shape=(jax.ShapeDtypeStruct((BLK, 2 * HD), jnp.bfloat16),) * levels
-        + (
-            jax.ShapeDtypeStruct((heads, levels * BLK, rows), jnp.bfloat16),
-            jax.ShapeDtypeStruct((held, BLK), jnp.float32),
+                    held_ref[0, head, spot(level_num), spot(part)] = low
+                    held_ref[1, head, spot(level_num), spot(part)] = probs.astype(jnp.bfloat16)
+                columns = slice(head * HD, (head + 1) * HD)
+                sent += dot(held_ref[send, head, spot(level_num)], both_ref[send, :, columns])
+            send_ref[spot(level_num)] = (sent * scale).astype(jnp.bfloat16)
+
+    return pl.pallas_call(
+        body,
+        out_shape=(
+            jax.ShapeDtypeStruct((levels * BLK, HD), jnp.bfloat16),
+            jax.ShapeDtypeStruct((2, heads, levels * BLK, rows), jnp.bfloat16),
+            jax.ShapeDtypeStruct((total + heads * row_tiles, BLK), jnp.float32),
         ),
-        in_specs=[VMEM] * (3 + 3 * levels),
-        out_specs=(VMEM,) * (2 + levels),
-        scratch_shapes=[pltpu.VMEM((heads, levels * BLK, rows), jnp.bfloat16)],
-        compiler_params=params(8),
+        in_specs=[VMEM] * (2 + 3 * levels),
+        out_specs=(VMEM,) * 3,
+        compiler_params=params(6),
         cost_estimate=cost(2 * heads * row_tiles * levels, 2 << 20),
         name="partner_part",
-    )(queries, grad_out, own_stats, *[each for level in scored for each in level])
-
-
-def own_part(queries, grad_out, own, blocks, weights, grad_probs, low, coef):
-    rows, width = queries.shape
+    )(both, own_stats, *[each for level in scored for each in level])
+
+
+def own_part(both, own, blocks, weights, grad_probs, held, coef):
+    _, rows, width = both.shape
     levels, row_tiles, heads = len(blocks), rows // BLK, width // HD
     places = pairs(row_tiles)
     total = heads * len(places)
 
-    def body(q_ref, g_ref, own_ref, weight_ref, prob_ref, low_ref, coef_ref, *refs):
+    def body(both_ref, own_ref, weight_ref, prob_ref, held_ref, coef_ref, *refs):
         block_refs = refs[:levels]
-        joined_ref, grad_ref, kt_ref, own_low_ref, high_ref = refs[levels:]
+        part_ref, keep_ref, send_ref, joined_ref, kt_ref, own_held_ref = refs[levels:]
+        keep, send, keep_scale, send_scale = kinds()
+        for level_num in range(levels):
+            kept = 0.0
+            for head in range(heads):
+                columns = slice(head * HD, (head + 1) * HD)
+                kept += dot(held_ref[keep, head, spot(level_num)], both_ref[keep, :, columns])
+            part_ref[spot(level_num)] = kept * keep_scale
         for number in range(row_tiles):
             kt_ref[:, spot(number)] = own_ref[spot(number), :HD].T
         for level_num in range(levels):
@@ -249,44 +270,65 @@
                     place = head * len(places) + places.index((part, number))
                     probs = weight_ref[place] * coef_ref[place : place + 1]
                     low = (probs * (prob_ref[place] - delta)).astype(jnp.bfloat16)
-                    own_low_ref[head, spot(number), spot(part)] = low
-                    high_ref[head, spot(number), spot(part)] = probs.astype(jnp.bfloat16)
-                dq_t = dot(kt_ref[:, rows:], low_ref[head, :, spot(part)])
+                    own_held_ref[0, head, spot(number), spot(part)] = low
+                    own_held_ref[1, head, spot(number), spot(part)] = probs.astype(jnp.bfloat16)
+                dq_t = dot(kt_ref[:, rows:], held_ref[0, head, :, spot(part)])
                 seen = slice(0, (part + 1) * BLK)
-                dq_t += dot(kt_ref[:, seen], own_low_ref[head, seen, spot(part)])
+                dq_t += dot(kt_ref[:, seen], own_held_ref[0, head, seen, spot(part)])
                 joined_ref[spot(part), columns] = (dq_t * SCALE).T.astype(jnp.bfloat16)
         for number in range(row_tiles):
-            key_part = value_part = 0.0
+            kept = sent = 0.0
             seeing = slice(number * BLK, rows)
             for head in range(heads):
                 columns = slice(head * HD, (head + 1) * HD)
-                key_part += dot(own_low_ref[head, spot(number), seeing], q_ref[seeing, columns])
-                value_part += dot(high_ref[head, spot(number), seeing], g_ref[seeing, columns])
-            grad_ref[spot(number), :HD] = key_part * SCALE
-            grad_ref[spot(number), HD:] = value_part
-
-    square = pltpu.VMEM((heads, rows, rows), jnp.bfloat16)
+                kept += dot(own_held_ref[keep, head, spot(number), seeing], both_ref[keep, seeing, columns])
+                sent += dot(own_held_ref[send, head, spot(number), seeing], both_ref[send, seeing, columns])
+            keep_ref[spot(number)] = kept * keep_scale
+            send_ref[spot(number)] = (sent * send_scale).astype(jnp.bfloat16)
+
     return pl.pallas_call(
         body,
         out_shape=(
-            jax.ShapeDtypeStruct((rows, width + 2 * HD), jnp.bfloat16),
-            jax.ShapeDtypeStruct((rows, 2 * HD), jnp.float32),
+            jax.ShapeDtypeStruct((levels * BLK, HD), jnp.float32),
+            jax.ShapeDtypeStruct((rows, HD), jnp.float32),
+            jax.ShapeDtypeStruct((rows, HD), jnp.bfloat16),
+            jax.ShapeDtypeStruct((rows, width + HD), jnp.bfloat16),
         ),
-        in_specs=[VMEM] * (7 + levels),
-        out_specs=(VMEM,) * 2,
-        scratch_shapes=[pltpu.VMEM((HD, rows + levels * BLK), jnp.bfloat16), square, square],
+        in_specs=[VMEM] * (6 + levels),
+        out_specs=(VMEM,) * 4,
+        scratch_shapes=[
+            pltpu.VMEM((HD, rows + levels * BLK), jnp.bfloat16),
+            pltpu.VMEM((2, heads, rows, rows), jnp.bfloat16),
+        ],
         compiler_params=params(14),
-        cost_estimate=cost(3 * total + heads * row_tiles * levels, 2 << 20),
+        cost_estimate=cost(3 * total + 2 * heads * row_tiles * levels, 2 << 20),
         name="own_part",
-    )(queries, grad_out, own, weights, grad_probs, low, coef, *blocks)
-
-
-def add_returned(block_index, joined, gradients, returned, ctx_count):
-    levels, width = len(returned), joined.shape[1] - gradients.shape[1]
-
-    def body(index_ref, joined_ref, grad_ref, *refs):
+    )(both, own, weights, grad_probs, held, coef, *blocks)
+
+
+def pair_parts(kept, received, levels):
+    def body(kept_ref, received_ref, *part_refs):
+        for level_num in range(levels):
+            total = kept_ref[spot(level_num)] + received_ref[spot(level_num)].astype(jnp.float32)
+            part_refs[level_num][...] = total.astype(jnp.bfloat16)
+
+    return pl.pallas_call(
+        body,
+        out_shape=(jax.ShapeDtypeStruct((BLK, HD), jnp.bfloat16),) * levels,
+        in_specs=[VMEM] * 2,
+        out_specs=(VMEM,) * levels,
+        compiler_params=params(6),
+        name="pair_parts",
+    )(kept, received)
+
+
+def add_returned(block_index, joined, kept, received, returned, ctx_count):
+    levels, width = len(returned), joined.shape[1] - HD
+
+    def body(index_ref, joined_ref, kept_ref, received_ref, *refs):
         out_ref, total_ref = refs[levels:]
         ctx_index = lax.axis_index("ctx")
+        total_ref[...] = kept_ref[...] + received_ref[...].astype(jnp.float32)
         for level_num in range(levels):
             start = block_start(index_ref, ctx_index, level_num, ctx_count)
             total_ref[pl.ds(start, BLK), :] += refs[level_num][...].astype(jnp.float32)
@@ -294,13 +336,14 @@
 
     return pl.pallas_call(
         body,
-        out_shape=tuple(jax.ShapeDtypeStruct(each.shape, each.dtype) for each in (joined, gradients)),
-        in_specs=[SMEM] + [VMEM] * (levels + 2),
-        out_specs=(VMEM, VMEM),
-        input_output_aliases={1: 0, 2: 1},
+        out_shape=jax.ShapeDtypeStruct(joined.shape, joined.dtype),
+        in_specs=[SMEM] + [VMEM] * (levels + 3),
+        out_specs=VMEM,
+        scratch_shapes=[pltpu.VMEM(kept.shape, jnp.float32)],
+        input_output_aliases={1: 0},
         compiler_params=params(6),
         name="add_returned",
-    )(block_index, joined, gradients, *returned)[0]
+    )(block_index, joined, kept, received, *returned)
 
 
 def lay_out(gathered, width):
@@ -309,12 +352,9 @@
     def body(in_ref, query_ref, key_ref, value_ref):
         for number in range(count):
             query_ref[:, number * width : (number + 1) * width] = in_ref[number, :, :width]
-        for number in range(count // 2):
-            total = in_ref[2 * number, :, width:].astype(jnp.float32)
-            total += in_ref[2 * number + 1, :, width:].astype(jnp.float32)
-            total = total.astype(jnp.bfloat16)
-            key_ref[:, number * HD : (number + 1) * HD] = total[:, :HD]
-            value_ref[:, number * HD : (number + 1) * HD] = total[:, HD:]
+            kind_ref = key_ref if number % 2 == 0 else value_ref
+            group = number // 2
+            kind_ref[:, group * HD : (group + 1) * HD] = in_ref[number, :, width:]
 
     shape = jax.ShapeDtypeStruct((token_rows, count // 2 * HD), gathered.dtype)
     return pl.pallas_call(
@@ -336,12 +376,15 @@
     hbm = [pltpu.with_memory_space_constraint(each, pltpu.HBM) for each in (block_index, keys, values)]
     own, *sends = gather_blocks(*hbm, ctx_count, levels)
     blocks = [rotate(sends[level_num], "ctx", 2**level_num) for level_num in range(levels)]
-    queries_t, grad_t, weights, grad_probs, stats = own_scores(queries, grad_out, own)
+    both, queries_t, grad_t, weights, grad_probs, stats = own_scores(queries, grad_out, own)
     scored = [block_scores(queries_t, grad_t, block) for block in blocks]
-    *parts, low, coef = partner_part(queries, grad_out, stats, scored)
+    sent, held, coef = partner_part(both, stats, scored)
+    received = swap(sent, "head")
+    part_kept, own_kept, own_sent, joined = own_part(both, own, blocks, weights, grad_probs, held, coef)
+    own_received = swap(own_sent, "head")
+    parts = pair_parts(part_kept, received, levels)
     returned = [rotate(parts[level_num], "ctx", -(2**level_num)) for level_num in range(levels)]
-    joined, gradients = own_part(queries, grad_out, own, blocks, weights, grad_probs, low, coef)
-    joined = add_returned(block_index, joined, gradients, returned, ctx_count)
+    joined = add_returned(block_index, joined, own_kept, own_received, returned, ctx_count)
     split = joined.reshape(head_count, rows // head_count, joined.shape[1])
     gathered = lax.all_to_all(split, "head", split_axis=0, concat_axis=0, tiled=True)
     return tuple(lay_out(gathered, width))

time: 73 us -> 71.1 us (0.974)
  blocking collectives: 35.6 us -> 28.7 us
  Pallas kernels: 14.7 us -> 16.5 us
  starting transfers between devices: 14.4 us -> 16 us
  waiting for transfers between devices: 7.3 us -> 8.4 us
    all_to_all x1, blocking collectives: 35.6 us -> 28.7 us  [on_device(): lax.all_to_all(split, 'head', split_axis=0, concat_axis=0, tiled=True)]
    ppermute x0 -> x2, starting transfers between devices: none -> 2.38 us  [swap(): lax.ppermute(value, axis, [(source, source ^ 1) for source in range(lax.a...]
    pallas_call x4 -> x5, Pallas kernels: 8.8 us -> 10.5 us  [the longest x1 4.37 us: own_part(): pl.pallas_call(body, out_shape=(jax.ShapeDtypeStruct((levels * BLK, HD),...]
    ppermute x0 -> x2, waiting for transfers between devices: none -> 1.66 us  [swap(): lax.ppermute(value, axis, [(source, source ^ 1) for source in range(lax.a...]
    ppermute x8, starting transfers between devices: 14.4 us -> 13.6 us  [rotate(): lax.ppermute(value, axis, [(source, (source + steps) % count) for source...]
  transfers between devices with their start and end apart: 8 -> 10, of which waited for: 3 -> 5; matrix products, arithmetic and copies ran while one was open for 0% -> 0% of each run, Pallas kernels for 11% -> 13%
where the time goes in v5:
time: 71.1 us; the launch traced here: 70.3 us
  blocking collectives  28.7 us (40%)
  Pallas kernels  16.5 us (23%)
  starting transfers between devices  16 us (23%)
  waiting for transfers between devices  8.4 us (12%)
  between operations  0.75 us (1%)
    all_to_all x1, blocking collectives, on_device(): lax.all_to_all(split, 'head', split_axis=0, concat_axis=0, tiled=True)  28.7 us
    ppermute x8, starting transfers between devices, rotate(): lax.ppermute(value, axis, [(source, (source + steps) % count) for source...  13.6 us
    ppermute x8, waiting for transfers between devices, rotate(): lax.ppermute(value, axis, [(source, (source + steps) % count) for source...  6.74 us
    pallas_call x1, Pallas kernels, own_part(): pl.pallas_call(body, out_shape=(jax.ShapeDtypeStruct((levels * BLK, HD),...  4.37 us
    pallas_call x4, Pallas kernels, block_scores(): pl.pallas_call(body, out_shape=(tiles, tiles, jax.ShapeDtypeStruct((3, he...  3.79 us
    pallas_call x1, Pallas kernels, partner_part(): pl.pallas_call(body, out_shape=(jax.ShapeDtypeStruct((levels * BLK, HD),...  3.2 us
    ppermute x2, starting transfers between devices, swap(): lax.ppermute(value, axis, [(source, source ^ 1) for source in range(lax.a...  2.38 us
    pallas_call x1, Pallas kernels, own_scores(): pl.pallas_call(body, out_shape=(jax.ShapeDtypeStruct((2, rows, width), jn...  2.2 us
  transfers between devices with their start and end apart: 10, of which 5 were waited for; matrix products, arithmetic and copies ran while one was open for 0% of the time, Pallas kernels for 13%

profile of v5, /device:TPU:6, one launch (start us, length us, event | category | flops | bytes accessed | tf_op | source)
XLA Modules:
  0.0 70.3 jit_solution(4124357883583624726)
XLA Ops:
  0.6 0.0 copy-start.1
  0.6 0.0 copy-start.2
  0.7 1.2 %gather_blocks.1 = (bf16[1024,256]{1,0:T(8,128)(2,1)S(1)}, bf16[256,256]{1,0:T(8,128)(2,1)S(1)}, bf16[256,256]{1,0:T(8,128)(2,1)S(1)}, bf16[256,256]{1,0:T(8,128)(2,1)S(1)}, bf16[256,256]{1,0:T(8,128)(2,1)S(1)}) custom-call(s32[4,16]{1,0:T(4,128)} %bitcast.3, bf16[1024,1024]{1,0:T(8,128)(2,1)} %key_ref.1, bf16[1024,1024]{1,0:T(8,128)(2,1)} %value_ref.1), custom_call_target="tpu_custom_call" | custom-call | tf_op jit(solution)/shard_map/gather_blocks/pallas_call | solution.py:52
  1.9 3.3 %collective-permute-start.3 = (bf16[256,256]{1,0:T(8,128)(2,1)S(1)}, bf16[256,256]{1,0:T(8,128)(2,1)S(1)}, u32[]{:S(2)}, u32[]{:S(2)}) collective-permute-start(bf16[256,256]{1,0:T(8,128)(2,1)S(1)} %get-tuple-element.56), channel_id=1, source_target_pairs={{0,128},{16,144},{32,160},{48,176},{64,192},{80,208},{96,224},{112... | collective-permute-start | bytes 393224 | tf_op jit(solution)/shard_map/ppermute | solution.py:20
  5.1 1.2 %collective-permute-start.2 = (bf16[256,256]{1,0:T(8,128)(2,1)S(1)}, bf16[256,256]{1,0:T(8,128)(2,1)S(1)}, u32[]{:S(2)}, u32[]{:S(2)}) collective-permute-start(bf16[256,256]{1,0:T(8,128)(2,1)S(1)} %get-tuple-element.52), channel_id=1, source_target_pairs={{0,64},{16,80},{32,96},{48,112},{64,128},{80,144},{96,160},{112,17... | collective-permute-start | bytes 393224 | tf_op jit(solution)/shard_map/ppermute | solution.py:20
  6.3 2.1 %collective-permute-start.1 = (bf16[256,256]{1,0:T(8,128)(2,1)S(1)}, bf16[256,256]{1,0:T(8,128)(2,1)S(1)}, u32[]{:S(2)}, u32[]{:S(2)}) collective-permute-start(bf16[256,256]{1,0:T(8,128)(2,1)S(1)} %get-tuple-element.48), channel_id=1, source_target_pairs={{0,32},{16,48},{32,64},{48,80},{64,96},{80,112},{96,128},{112,144}... | collective-permute-start | bytes 393224 | tf_op jit(solution)/shard_map/ppermute | solution.py:20
  8.4 0.0 collective-permute-start
  8.4 0.0 copy-done.1
  8.4 0.0 copy-done.2
  8.4 2.2 %own_scores.1 = (bf16[2,1024,256]{2,1,0:T(8,128)(2,1)S(1)}, bf16[256,1024]{1,0:T(8,128)(2,1)S(1)}, bf16[256,1024]{1,0:T(8,128)(2,1)S(1)}, f32[20,256,256]{2,1,0:...) custom-call(bf16[1024,256]{1,0:T(8,128)(2,1)S(1)} %copy-done.1, bf16[1024,256]{1,0:T(8,128)(2,1)S(1)} %copy-done.2, ...), custom_call_target="tpu_custom_call" | custom-call | flops 671088640 | bytes 2097152 | tf_op jit(solution)/shard_map/own_scores/pallas_call | solution.py:126
  10.6 0.0 collective-permute-done.3.block_ref.refs_3_
  10.6 1.0 %block_scores.7 = (f32[8,256,256]{2,1,0:T(8,128)S(1)}, f32[8,256,256]{2,1,0:T(8,128)S(1)}, f32[3,8,256]{2,1,0:T(8,128)S(1)}) custom-call(bf16[256,1024]{1,0:T(8,128)(2,1)S(1)} %get-tuple-element.42.qt_ref, bf16[256,1024]{1,0:T(8,128)(2,1)S(1)} %get-tuple-element.43.gt_ref, bf16[256,256]{1,0:T(8,128)(2,1)S(1)} %collective-permute-done.3.block_ref.refs_3_), custom_call_target="tpu_custom_call" | custom-call | flops 268435456 | bytes 2097152 | tf_op jit(solution)/shard_map/block_scores/pallas_call | solution.py:160
  11.6 0.0 collective-permute-done.2.block_ref.refs_2_
  11.6 1.0 %block_scores.6 = (f32[8,256,256]{2,1,0:T(8,128)S(1)}, f32[8,256,256]{2,1,0:T(8,128)S(1)}, f32[3,8,256]{2,1,0:T(8,128)S(1)}) custom-call(bf16[256,1024]{1,0:T(8,128)(2,1)S(1)} %get-tuple-element.42.qt_ref, bf16[256,1024]{1,0:T(8,128)(2,1)S(1)} %get-tuple-element.43.gt_ref, bf16[256,256]{1,0:T(8,128)(2,1)S(1)} %collective-permute-done.2.block_ref.refs_2_), custom_call_target="tpu_custom_call" | custom-call | flops 268435456 | bytes 2097152 | tf_op jit(solution)/shard_map/block_scores/pallas_call | solution.py:160
  12.6 1.0 %collective-permute-done.1.block_ref.refs_1_ = bf16[256,256]{1,0:T(8,128)(2,1)S(1)} collective-permute-done((bf16[256,256]{1,0:T(8,128)(2,1)S(1)}, bf16[256,256]{1,0:T(8,128)(2,1)S(1)}, u32[]{:S(2)}, u32[]{:S(2)}) %collective-permute-start.1) | collective-permute-done | bytes 131104 | tf_op jit(solution)/shard_map/ppermute | solution.py:20
  13.6 0.9 %block_scores.5 = (f32[8,256,256]{2,1,0:T(8,128)S(1)}, f32[8,256,256]{2,1,0:T(8,128)S(1)}, f32[3,8,256]{2,1,0:T(8,128)S(1)}) custom-call(bf16[256,1024]{1,0:T(8,128)(2,1)S(1)} %get-tuple-element.42.qt_ref, bf16[256,1024]{1,0:T(8,128)(2,1)S(1)} %get-tuple-element.43.gt_ref, bf16[256,256]{1,0:T(8,128)(2,1)S(1)} %collective-permute-done.1.block_ref.refs_1_), custom_call_target="tpu_custom_call" | custom-call | flops 268435456 | bytes 2097152 | tf_op jit(solution)/shard_map/block_scores/pallas_call | solution.py:160
  14.5 0.0 collective-permute-done.block_ref.refs_0_
  14.5 0.9 %block_scores.4 = (f32[8,256,256]{2,1,0:T(8,128)S(1)}, f32[8,256,256]{2,1,0:T(8,128)S(1)}, f32[3,8,256]{2,1,0:T(8,128)S(1)}) custom-call(bf16[256,1024]{1,0:T(8,128)(2,1)S(1)} %get-tuple-element.42.qt_ref, bf16[256,1024]{1,0:T(8,128)(2,1)S(1)} %get-tuple-element.43.gt_ref, bf16[256,256]{1,0:T(8,128)(2,1)S(1)} %collective-permute-done.block_ref.refs_0_), custom_call_target="tpu_custom_call" | custom-call | flops 268435456 | bytes 2097152 | tf_op jit(solution)/shard_map/block_scores/pallas_call | solution.py:160
  15.4 3.2 %partner_part.1 = (bf16[1024,128]{1,0:T(8,128)(2,1)S(1)}, bf16[2,2,1024,1024]{3,2,1,0:T(8,128)(2,1)S(1)}, f32[28,256]{1,0:T(8,128)S(1)}) custom-call(bf16[2,1024,256]{2,1,0:T(8,128)(2,1)S(1)} %get-tuple-element.38.both_ref, f32[3,20,256]{2,1,0:T(8,128)S(1)} %get-tuple-element.41.own_ref, f32[8,256,256]{2,1,0:T(8,128)S(1)} %get-tuple-element.45.refs_0_, ...), custom_call_target="tpu_custom_call" | custom-call | flops 1073741824 | bytes 2097152 | tf_op jit(solution)/shard_map/partner_part/pallas_call | solution.py:229
  18.7 1.3 %collective-permute-start.5 = (bf16[1024,128]{1,0:T(8,128)(2,1)S(1)}, bf16[1024,128]{1,0:T(8,128)(2,1)S(1)}, u32[]{:S(2)}, u32[]{:S(2)}) collective-permute-start(bf16[1024,128]{1,0:T(8,128)(2,1)S(1)} %get-tuple-element.66), channel_id=1, source_target_pairs={{0,1},{1,0},{2,3},{3,2},{4,5},{5,4},{6,7},{7,6},{8,9},{9,8},{10,11... | collective-permute-start | bytes 786440 | tf_op jit(solution)/shard_map/ppermute | solution.py:24
  19.9 0.0 copy-start
  19.9 4.4 %own_part.1 = (f32[1024,128]{1,0:T(8,128)S(1)}, f32[1024,128]{1,0:T(8,128)S(1)}, bf16[1024,128]{1,0:T(8,128)(2,1)S(1)}, bf16[1024,384]{1,0:T(8,128)(2,1)S(1)}) custom-call(bf16[2,1024,256]{2,1,0:T(8,128)(2,1)S(1)} %get-tuple-element.38.both_ref, bf16[1024,256]{1,0:T(8,128)(2,1)S(1)} %get-tuple-element.37.own_ref, ...), custom_call_target="tpu_custom_call" | custom-call | flops 2080374784 | bytes 2097152 | tf_op jit(solution)/shard_map/own_part/pallas_call | solution.py:289
  24.3 1.1 %collective-permute-start.4 = (bf16[1024,128]{1,0:T(8,128)(2,1)S(1)}, bf16[1024,128]{1,0:T(8,128)(2,1)S(1)}, u32[]{:S(2)}, u32[]{:S(2)}) collective-permute-start(bf16[1024,128]{1,0:T(8,128)(2,1)S(1)} %get-tuple-element.64), channel_id=1, source_target_pairs={{0,1},{1,0},{2,3},{3,2},{4,5},{5,4},{6,7},{7,6},{8,9},{9,8},{10,11... | collective-permute-start | bytes 786440 | tf_op jit(solution)/shard_map/ppermute | solution.py:24
  25.4 1.7 %collective-permute-done.5.received_ref = bf16[1024,128]{1,0:T(8,128)(2,1)S(1)} collective-permute-done((bf16[1024,128]{1,0:T(8,128)(2,1)S(1)}, bf16[1024,128]{1,0:T(8,128)(2,1)S(1)}, u32[]{:S(2)}, u32[]{:S(2)}) %collective-permute-start.5) | collective-permute-done | bytes 262176 | tf_op jit(solution)/shard_map/ppermute | solution.py:24
  27.1 0.1 pair_parts.1
  27.1 0.1 collective-permute-start.6
  27.2 1.9 %collective-permute-start.7 = (bf16[256,128]{1,0:T(8,128)(2,1)S(1)}, bf16[256,128]{1,0:T(8,128)(2,1)S(1)}, u32[]{:S(2)}, u32[]{:S(2)}) collective-permute-start(bf16[256,128]{1,0:T(8,128)(2,1)S(1)} %get-tuple-element.68), channel_id=1, source_target_pairs={{0,224},{16,240},{32,0},{48,16},{64,32},{80,48},{96,64},{112,80},{... | collective-permute-start | bytes 196616 | tf_op jit(solution)/shard_map/ppermute | solution.py:20
  29.1 5.1 %collective-permute-start.8 = (bf16[256,128]{1,0:T(8,128)(2,1)S(1)}, bf16[256,128]{1,0:T(8,128)(2,1)S(1)}, u32[]{:S(2)}, u32[]{:S(2)}) collective-permute-start(bf16[256,128]{1,0:T(8,128)(2,1)S(1)} %get-tuple-element.69), channel_id=1, source_target_pairs={{0,192},{16,208},{32,224},{48,240},{64,0},{80,16},{96,32},{112,48}... | collective-permute-start | bytes 196616 | tf_op jit(solution)/shard_map/ppermute | solution.py:20
  34.2 0.0 collective-permute-start.9
  34.2 0.0 collective-permute-done.4.received_ref
  34.2 0.0 collective-permute-done.6.refs_0_
  34.2 1.1 %collective-permute-done.7.refs_1_ = bf16[256,128]{1,0:T(8,128)(2,1)S(1)} collective-permute-done((bf16[256,128]{1,0:T(8,128)(2,1)S(1)}, bf16[256,128]{1,0:T(8,128)(2,1)S(1)}, u32[]{:S(2)}, u32[]{:S(2)}) %collective-permute-start.7) | collective-permute-done | bytes 65568 | tf_op jit(solution)/shard_map/ppermute | solution.py:20
  35.3 2.0 %collective-permute-done.8.refs_2_ = bf16[256,128]{1,0:T(8,128)(2,1)S(1)} collective-permute-done((bf16[256,128]{1,0:T(8,128)(2,1)S(1)}, bf16[256,128]{1,0:T(8,128)(2,1)S(1)}, u32[]{:S(2)}, u32[]{:S(2)}) %collective-permute-start.8) | collective-permute-done | bytes 65568 | tf_op jit(solution)/shard_map/ppermute | solution.py:20
  37.3 2.6 %collective-permute-done.9.refs_3_ = bf16[256,128]{1,0:T(8,128)(2,1)S(1)} collective-permute-done((bf16[256,128]{1,0:T(8,128)(2,1)S(1)}, bf16[256,128]{1,0:T(8,128)(2,1)S(1)}, u32[]{:S(2)}, u32[]{:S(2)}) %collective-permute-start.9) | collective-permute-done | bytes 65568 | tf_op jit(solution)/shard_map/ppermute | solution.py:20
  39.9 0.0 copy-done
  39.9 0.7 %add_returned.1 = bf16[1024,384]{1,0:T(8,128)(2,1)S(1)} custom-call(s32[4,16]{1,0:T(4,128)S(1)} %bitcast.4, bf16[1024,384]{1,0:T(8,128)(2,1)S(1)} %get-tuple-element.62.joined_ref, f32[1024,128]{1,0:T(8,128)S(1)} %get-tuple-element.63.kept_ref, bf16[1024,128]{1,0:T(8,128)(2,1)S(1)} %collective-permute-done.4.received_ref, ...), custom_call_target="tpu_custom_call", output_to_operand_aliasing={{}: (1, {})} | custom-call | tf_op jit(solution)/shard_map/add_returned/pallas_call | solution.py:337
  40.7 28.7 %all_to_all.5.in_ref = bf16[16,64,384]{2,1,0:T(8,128)(2,1)S(1)} all-to-all(bf16[16,64,384]{2,1,0:T(8,128)(2,1)S(1)} %bitcast.2), channel_id=1, replica_groups=mesh['ctx'=16,'head'=16] {'head'}, dimensions={0} | all-to-all | bytes 1572864 | tf_op jit(solution)/shard_map/all_to_all | solution.py:389
  69.4 1.0 %lay_out.1 = (bf16[64,4096]{1,0:T(8,128)(2,1)}, bf16[64,1024]{1,0:T(8,128)(2,1)}, bf16[64,1024]{1,0:T(8,128)(2,1)}) custom-call(bf16[16,64,384]{2,1,0:T(8,128)(2,1)S(1)} %all_to_all.5.in_ref), custom_call_target="tpu_custom_call" | custom-call | tf_op jit(solution)/shard_map/lay_out/pallas_call | solution.py:360
Async XLA Ops:
  0.6 7.8 %copy-start.1 = (bf16[1024,256]{1,0:T(8,128)(2,1)S(1)}, bf16[1024,256]{1,0:T(8,128)(2,1)}, u32[]{:S(2)}) copy-start(bf16[1024,256]{1,0:T(8,128)(2,1)} %q_ref.1) | copy-start | bytes 1572868
  0.6 7.8 %copy-start.2 = (bf16[1024,256]{1,0:T(8,128)(2,1)S(1)}, bf16[1024,256]{1,0:T(8,128)(2,1)}, u32[]{:S(2)}) copy-start(bf16[1024,256]{1,0:T(8,128)(2,1)} %g_ref.1) | copy-start | bytes 1572868
  1.9 8.8 %collective-permute-start.3 = (bf16[256,256]{1,0:T(8,128)(2,1)S(1)}, bf16[256,256]{1,0:T(8,128)(2,1)S(1)}, u32[]{:S(2)}, u32[]{:S(2)}) collective-permute-start(bf16[256,256]{1,0:T(8,128)(2,1)S(1)} %get-tuple-element.56), channel_id=1, source_target_pairs={{0,128},{16,144},{32,160},{48,176},{64,192},{80,208},{96,224},{112... | collective-permute-start | bytes 393224 | tf_op jit(solution)/shard_map/ppermute | solution.py:20
  5.1 6.5 %collective-permute-start.2 = (bf16[256,256]{1,0:T(8,128)(2,1)S(1)}, bf16[256,256]{1,0:T(8,128)(2,1)S(1)}, u32[]{:S(2)}, u32[]{:S(2)}) collective-permute-start(bf16[256,256]{1,0:T(8,128)(2,1)S(1)} %get-tuple-element.52), channel_id=1, source_target_pairs={{0,64},{16,80},{32,96},{48,112},{64,128},{80,144},{96,160},{112,17... | collective-permute-start | bytes 393224 | tf_op jit(solution)/shard_map/ppermute | solution.py:20
  6.3 7.2 %collective-permute-start.1 = (bf16[256,256]{1,0:T(8,128)(2,1)S(1)}, bf16[256,256]{1,0:T(8,128)(2,1)S(1)}, u32[]{:S(2)}, u32[]{:S(2)}) collective-permute-start(bf16[256,256]{1,0:T(8,128)(2,1)S(1)} %get-tuple-element.48), channel_id=1, source_target_pairs={{0,32},{16,48},{32,64},{48,80},{64,96},{80,112},{96,128},{112,144}... | collective-permute-start | bytes 393224 | tf_op jit(solution)/shard_map/ppermute | solution.py:20
  8.4 6.1 %collective-permute-start = (bf16[256,256]{1,0:T(8,128)(2,1)S(1)}, bf16[256,256]{1,0:T(8,128)(2,1)S(1)}, u32[]{:S(2)}, u32[]{:S(2)}) collective-permute-start(bf16[256,256]{1,0:T(8,128)(2,1)S(1)} %get-tuple-element.44), channel_id=1, source_target_pairs={{0,16},{16,32},{32,48},{48,64},{64,80},{80,96},{96,112},{112,128},... | collective-permute-start | bytes 393224 | tf_op jit(solution)/shard_map/ppermute | solution.py:20
  18.7 8.4 %collective-permute-start.5 = (bf16[1024,128]{1,0:T(8,128)(2,1)S(1)}, bf16[1024,128]{1,0:T(8,128)(2,1)S(1)}, u32[]{:S(2)}, u32[]{:S(2)}) collective-permute-start(bf16[1024,128]{1,0:T(8,128)(2,1)S(1)} %get-tuple-element.66), channel_id=1, source_target_pairs={{0,1},{1,0},{2,3},{3,2},{4,5},{5,4},{6,7},{7,6},{8,9},{9,8},{10,11... | collective-permute-start | bytes 786440 | tf_op jit(solution)/shard_map/ppermute | solution.py:24
  19.9 20.0 %copy-start = (s32[16,4]{0,1:T(4,128)S(1)}, s32[16,4]{0,1:T(4,128)}, u32[]{:S(2)}) copy-start(s32[16,4]{0,1:T(4,128)} %param.9) | copy-start | bytes 772
  24.3 9.9 %collective-permute-start.4 = (bf16[1024,128]{1,0:T(8,128)(2,1)S(1)}, bf16[1024,128]{1,0:T(8,128)(2,1)S(1)}, u32[]{:S(2)}, u32[]{:S(2)}) collective-permute-start(bf16[1024,128]{1,0:T(8,128)(2,1)S(1)} %get-tuple-element.64), channel_id=1, source_target_pairs={{0,1},{1,0},{2,3},{3,2},{4,5},{5,4},{6,7},{7,6},{8,9},{9,8},{10,11... | collective-permute-start | bytes 786440 | tf_op jit(solution)/shard_map/ppermute | solution.py:24
  27.1 7.1 %collective-permute-start.6 = (bf16[256,128]{1,0:T(8,128)(2,1)S(1)}, bf16[256,128]{1,0:T(8,128)(2,1)S(1)}, u32[]{:S(2)}, u32[]{:S(2)}) collective-permute-start(bf16[256,128]{1,0:T(8,128)(2,1)S(1)} %get-tuple-element.67), channel_id=1, source_target_pairs={{0,240},{16,0},{32,16},{48,32},{64,48},{80,64},{96,80},{112,96},{1... | collective-permute-start | bytes 196616 | tf_op jit(solution)/shard_map/ppermute | solution.py:20
  27.2 8.1 %collective-permute-start.7 = (bf16[256,128]{1,0:T(8,128)(2,1)S(1)}, bf16[256,128]{1,0:T(8,128)(2,1)S(1)}, u32[]{:S(2)}, u32[]{:S(2)}) collective-permute-start(bf16[256,128]{1,0:T(8,128)(2,1)S(1)} %get-tuple-element.68), channel_id=1, source_target_pairs={{0,224},{16,240},{32,0},{48,16},{64,32},{80,48},{96,64},{112,80},{... | collective-permute-start | bytes 196616 | tf_op jit(solution)/shard_map/ppermute | solution.py:20
  29.1 8.2 %collective-permute-start.8 = (bf16[256,128]{1,0:T(8,128)(2,1)S(1)}, bf16[256,128]{1,0:T(8,128)(2,1)S(1)}, u32[]{:S(2)}, u32[]{:S(2)}) collective-permute-start(bf16[256,128]{1,0:T(8,128)(2,1)S(1)} %get-tuple-element.69), channel_id=1, source_target_pairs={{0,192},{16,208},{32,224},{48,240},{64,0},{80,16},{96,32},{112,48}... | collective-permute-start | bytes 196616 | tf_op jit(solution)/shard_map/ppermute | solution.py:20
  34.2 5.8 %collective-permute-start.9 = (bf16[256,128]{1,0:T(8,128)(2,1)S(1)}, bf16[256,128]{1,0:T(8,128)(2,1)S(1)}, u32[]{:S(2)}, u32[]{:S(2)}) collective-permute-start(bf16[256,128]{1,0:T(8,128)(2,1)S(1)} %get-tuple-element.70), channel_id=1, source_target_pairs={{0,128},{16,144},{32,160},{48,176},{64,192},{80,208},{96,224},{112... | collective-permute-start | bytes 196616 | tf_op jit(solution)/shard_map/ppermute | solution.py:20
